TPU v7x, 128 devices: a whole 4x4x4 slice. The times are simulated.
128 devices in a mesh: tm: 16 (over z, x), gauge: 8 (over y, core).
Axes of the slice: x: 4, y: 4, z: 4, core: 2. Of those that a mesh axis runs over, the one named last changes fastest.
Arguments:
- records: bfloat16 [262144, 1536], P('tm', 'gauge'), may hold values from -400 to 400
- offsets: int32 [256], P('tm'), may hold values from 0 to 960
- column_map: int32 [1536], replicated, may hold values from 0 to 1535, each once
- angles: float32 [512], replicated, may hold values from -3.140625 to 3.140625
Outputs:
- factor: float32 [1536, 1536], replicated
All inputs are finite; a program needn't handle non-finite values.
Results may differ from a plain program's by a relative error of at most 0.0014.
Values may be sent and summed in bfloat16 or wider, within the bound.
No kernel may reach another device: no remote copies, remote signals or barrier semaphores. Data moves between devices by JAX's collectives and lax.ppermute only.
A program may use at most 128 MiB of HBM per device.

v0:
```python
import jax
import jax.numpy as jnp
from jax import lax
from jax.sharding import PartitionSpec as P

BLOCK = 1024
BAND = 64


def band_mask(offsets_here, total_rows):
    positions = jnp.arange(total_rows, dtype=jnp.int32)
    block_of = positions // BLOCK
    within = positions % BLOCK
    blocks = jnp.arange(offsets_here.shape[0], dtype=jnp.int32)
    inside = (
        (block_of[None, :] == blocks[:, None])
        & (within[None, :] >= offsets_here[:, None])
        & (within[None, :] < offsets_here[:, None] + BAND)
    )
    return inside.astype(jnp.bfloat16)


def drift_filter(rows, offsets_here):
    masks = band_mask(offsets_here, rows.shape[0])
    baseline = jnp.dot(masks, rows, preferred_element_type=jnp.float32) / BAND
    nblocks = offsets_here.shape[0]
    shaped = rows.astype(jnp.float32).reshape(nblocks, BLOCK, rows.shape[1]) - baseline[:, None, :]
    return shaped.reshape(rows.shape[0], rows.shape[1]).astype(jnp.bfloat16)


def rosette_rotate(full_rows, column_map, angles):
    count = angles.shape[0]
    picked = jnp.take(full_rows, column_map, axis=1)
    first_arm = picked[:, :count].astype(jnp.float32)
    middle_arm = picked[:, count : 2 * count].astype(jnp.float32)
    last_arm = picked[:, 2 * count :].astype(jnp.float32)
    shear = 2.0 * middle_arm - first_arm - last_arm
    cosine = jnp.cos(angles)[None, :]
    sine = jnp.sin(angles)[None, :]
    cos_sq = cosine * cosine
    sin_sq = sine * sine
    mixed = sine * cosine
    along_x = first_arm * cos_sq + last_arm * sin_sq + shear * mixed
    along_y = first_arm * sin_sq + last_arm * cos_sq - shear * mixed
    shear_new = 2.0 * (last_arm - first_arm) * mixed + shear * (cos_sq - sin_sq)
    return jnp.concatenate([along_x, along_y, shear_new], axis=1).astype(jnp.bfloat16)


def gram_of(rotated):
    return lax.dot_general(
        rotated, rotated, (((0,), (0,)), ((), ())), preferred_element_type=jnp.float32
    )


def shards(records, offsets, column_map, angles):
    filtered = drift_filter(records, offsets)
    regrouped = lax.all_to_all(filtered, "gauge", split_axis=0, concat_axis=1, tiled=True)
    rotated = rosette_rotate(regrouped, column_map, angles)
    total_rows = rotated.shape[0] * lax.axis_size("tm") * lax.axis_size("gauge")
    gram_full = lax.psum(gram_of(rotated), ("tm", "gauge"))
    return jnp.linalg.cholesky(gram_full / total_rows).T


def solution(mesh):
    placed = (P("tm", "gauge"), P("tm"), P(), P())
    return jax.shard_map(shards, mesh=mesh, in_specs=placed, out_specs=P(), check_vma=False)
```

profile of v0, /device:TPU:1, one launch (start us, length us, event | category | flops | bytes accessed | tf_op | source)
XLA Modules:
  0.0 724.9 jit_solution(10787455784423801423)
XLA Ops:
  17.4 21.2 %copy.12 = f32[24,8,16,1024]{3,1,2,0:T(8,128)} copy(f32[24,8,16,1024]{3,2,1,0:T(8,128)} %bitcast.78) | data formatting | bytes 25165824
  38.6 10.5 %subtract_convert_fusion = bf16[16384,192]{0,1:T(8,128)(2,1)} fusion(f32[16384,192]{0,1:T(8,128)} %bitcast.79, bf16[16384,192]{0,1:T(8,128)(2,1)} %param.4), kind=kLoop, calls=%fused_computation.1 | loop fusion | flops 9437184 | bytes 25165824 | tf_op jit(solution)/shard_map/convert_element_type | solution.py:28
  62.0 71.3 %all-to-all-done = bf16[8,2048,192]{1,2,0:T(8,128)(2,1)} async-done(((bf16[8,2048,192]{1,2,0:T(8,128)(2,1)}), bf16[8,2048,192]{1,2,0:T(8,128)(2,1)}, u32[]{:S(2)}, u32[]{:S(2)}) %all-to-all-start) | async-done | bytes 6291488 | tf_op jit(solution)/shard_map/all_to_all | solution.py:57
  133.3 16.3 %gather_fusion = bf16[1536,2048]{1,0:T(8,128)(2,1)} fusion(bf16[2048,1536]{0,1:T(8,128)(2,1)} %bitcast.1, s32[2048]{0:T(1024)S(1)} %pad_clamp_fusion), kind=kCustom, calls=%fused_computation | custom fusion | bytes 12589056 | tf_op jit(solution)/shard_map/jit(_take)/gather | solution.py:33
  157.8 17.2 %fusion.1 = f32[1536,1536]{0,1:T(8,128)} fusion(bf16[2048,512]{0,1:T(8,128)(2,1)} %get-tuple-element.9, bf16[2048,512]{0,1:T(8,128)(2,1)} %get-tuple-element.8, bf16[2048,512]{0,1:T(8,128)(2,1)S(1)} %get-tuple-element.7), kind=kOutput, calls=%fused_computation.14 | convolution fusion | flops 9682550784 | bytes 15728640 | tf_op jit(solution)/shard_map/dot_general | solution.py:50
  175.0 164.8 %all-reduce.3.cloned.1.call-done = f32[1536,1536]{0,1:T(8,128)} async-done(((f32[1536,1536]{0,1:T(8,128)}), f32[1536,1536]{0,1:T(8,128)}) %all-reduce.3.cloned.1.call-update) | async-done | bytes 9437200 | tf_op jit(solution)/shard_map/psum | solution.py:60
  348.3 9.8 %copy.8 = f32[1536,1536]{1,0:T(8,128)} copy(f32[1536,1536]{0,1:T(8,128)} %broadcast_multiply_fusion) | data formatting | bytes 18874368 | tf_op jit(solution)/shard_map/div | solution.py:61
  358.1 12.4 %fusion = f32[1536,1536]{1,0:T(8,128)} fusion(f32[1536,1536]{1,0:T(8,128)} %copy.8, f32[1536,1536]{0,1:T(8,128)} %all-reduce.3.cloned.1.call-done), kind=kLoop, calls=%fused_computation.3 | loop fusion | flops 7077888 | bytes 28311552 | tf_op jit(solution)/shard_map/jit(cholesky)/div | solution.py:61
  371.3 11.7 %cholesky.341 = f32[128,128]{1,0:T(8,128)S(1)} custom-call(f32[128,128]{1,0:T(8,128)S(1)} %cholesky.892), custom_call_target="Cholesky" | custom-call | tf_op jit(solution)/shard_map/jit(cholesky)/cholesky | solution.py:61
  383.7 9.8 %custom-call.91 = f32[1,128,128]{1,2,0:T(8,128)S(1)} custom-call(f32[1,128,128]{2,1,0:T(8,128)S(1)} %get-tuple-element.43), custom_call_target="InvertDiagBlocksLowerTriangular" | custom-call | tf_op jit(solution)/shard_map/jit(cholesky)/cholesky | solution.py:61
  403.1 11.9 %cholesky.362 = f32[128,128]{1,0:T(8,128)S(1)} custom-call(f32[128,128]{1,0:T(8,128)S(1)} %cholesky.896), custom_call_target="Cholesky" | custom-call | tf_op jit(solution)/shard_map/jit(cholesky)/cholesky | solution.py:61
  416.3 9.8 %custom-call.92 = f32[1,128,128]{1,2,0:T(8,128)S(1)} custom-call(f32[1,128,128]{2,1,0:T(8,128)S(1)} %get-tuple-element.40), custom_call_target="InvertDiagBlocksLowerTriangular" | custom-call | tf_op jit(solution)/shard_map/jit(cholesky)/cholesky | solution.py:61
  430.5 11.7 %cholesky.385 = f32[128,128]{1,0:T(8,128)S(1)} custom-call(f32[128,128]{1,0:T(8,128)S(1)} %cholesky.901), custom_call_target="Cholesky" | custom-call | tf_op jit(solution)/shard_map/jit(cholesky)/cholesky | solution.py:61
  443.6 10.2 %custom-call.93 = f32[1,128,128]{1,2,0:T(8,128)S(1)} custom-call(f32[1,128,128]{2,1,0:T(8,128)S(1)} %get-tuple-element.37), custom_call_target="InvertDiagBlocksLowerTriangular" | custom-call | tf_op jit(solution)/shard_map/jit(cholesky)/cholesky | solution.py:61
  458.6 11.7 %cholesky.715 = f32[128,128]{1,0:T(8,128)S(1)} custom-call(f32[128,128]{1,0:T(8,128)S(1)} %cholesky.906), custom_call_target="Cholesky" | custom-call | tf_op jit(solution)/shard_map/jit(cholesky)/cholesky | solution.py:61
  471.7 9.8 %custom-call.94 = f32[1,128,128]{1,2,0:T(8,128)S(1)} custom-call(f32[1,128,128]{2,1,0:T(8,128)S(1)} %get-tuple-element.34), custom_call_target="InvertDiagBlocksLowerTriangular" | custom-call | tf_op jit(solution)/shard_map/jit(cholesky)/cholesky | solution.py:61
  486.5 11.9 %cholesky.734 = f32[128,128]{1,0:T(8,128)S(1)} custom-call(f32[128,128]{1,0:T(8,128)S(1)} %cholesky.911), custom_call_target="Cholesky" | custom-call | tf_op jit(solution)/shard_map/jit(cholesky)/cholesky | solution.py:61
  499.7 9.8 %custom-call.95 = f32[1,128,128]{1,2,0:T(8,128)S(1)} custom-call(f32[1,128,128]{2,1,0:T(8,128)S(1)} %get-tuple-element.31), custom_call_target="InvertDiagBlocksLowerTriangular" | custom-call | tf_op jit(solution)/shard_map/jit(cholesky)/cholesky | solution.py:61
  514.7 11.7 %cholesky.754 = f32[128,128]{1,0:T(8,128)S(1)} custom-call(f32[128,128]{1,0:T(8,128)S(1)} %cholesky.916), custom_call_target="Cholesky" | custom-call | tf_op jit(solution)/shard_map/jit(cholesky)/cholesky | solution.py:61
  527.8 10.0 %custom-call.96 = f32[1,128,128]{1,2,0:T(8,128)S(1)} custom-call(f32[1,128,128]{2,1,0:T(8,128)S(1)} %get-tuple-element.28), custom_call_target="InvertDiagBlocksLowerTriangular" | custom-call | tf_op jit(solution)/shard_map/jit(cholesky)/cholesky | solution.py:61
  543.0 11.7 %cholesky.774 = f32[128,128]{1,0:T(8,128)S(1)} custom-call(f32[128,128]{1,0:T(8,128)S(1)} %cholesky.921), custom_call_target="Cholesky" | custom-call | tf_op jit(solution)/shard_map/jit(cholesky)/cholesky | solution.py:61
  556.0 9.8 %custom-call.97 = f32[1,128,128]{1,2,0:T(8,128)S(1)} custom-call(f32[1,128,128]{2,1,0:T(8,128)S(1)} %get-tuple-element.25), custom_call_target="InvertDiagBlocksLowerTriangular" | custom-call | tf_op jit(solution)/shard_map/jit(cholesky)/cholesky | solution.py:61
  571.3 11.7 %cholesky.794 = f32[128,128]{1,0:T(8,128)S(1)} custom-call(f32[128,128]{1,0:T(8,128)S(1)} %cholesky.926), custom_call_target="Cholesky" | custom-call | tf_op jit(solution)/shard_map/jit(cholesky)/cholesky | solution.py:61
  584.3 9.8 %custom-call.98 = f32[1,128,128]{1,2,0:T(8,128)S(1)} custom-call(f32[1,128,128]{2,1,0:T(8,128)S(1)} %get-tuple-element.22), custom_call_target="InvertDiagBlocksLowerTriangular" | custom-call | tf_op jit(solution)/shard_map/jit(cholesky)/cholesky | solution.py:61
  598.8 11.9 %cholesky.814 = f32[128,128]{1,0:T(8,128)S(1)} custom-call(f32[128,128]{1,0:T(8,128)S(1)} %cholesky.931), custom_call_target="Cholesky" | custom-call | tf_op jit(solution)/shard_map/jit(cholesky)/cholesky | solution.py:61
  612.0 9.8 %custom-call.99 = f32[1,128,128]{1,2,0:T(8,128)S(1)} custom-call(f32[1,128,128]{2,1,0:T(8,128)S(1)} %get-tuple-element.19), custom_call_target="InvertDiagBlocksLowerTriangular" | custom-call | tf_op jit(solution)/shard_map/jit(cholesky)/cholesky | solution.py:61
  626.2 11.7 %cholesky.834 = f32[128,128]{1,0:T(8,128)S(1)} custom-call(f32[128,128]{1,0:T(8,128)S(1)} %cholesky.936), custom_call_target="Cholesky" | custom-call | tf_op jit(solution)/shard_map/jit(cholesky)/cholesky | solution.py:61
  639.2 9.8 %custom-call.100 = f32[1,128,128]{1,2,0:T(8,128)S(1)} custom-call(f32[1,128,128]{2,1,0:T(8,128)S(1)} %get-tuple-element.16), custom_call_target="InvertDiagBlocksLowerTriangular" | custom-call | tf_op jit(solution)/shard_map/jit(cholesky)/cholesky | solution.py:61
  652.9 11.7 %cholesky.854 = f32[128,128]{1,0:T(8,128)S(1)} custom-call(f32[128,128]{1,0:T(8,128)S(1)} %cholesky.941), custom_call_target="Cholesky" | custom-call | tf_op jit(solution)/shard_map/jit(cholesky)/cholesky | solution.py:61
  665.9 9.8 %custom-call.101 = f32[1,128,128]{1,2,0:T(8,128)S(1)} custom-call(f32[1,128,128]{2,1,0:T(8,128)S(1)} %get-tuple-element.13), custom_call_target="InvertDiagBlocksLowerTriangular" | custom-call | tf_op jit(solution)/shard_map/jit(cholesky)/cholesky | solution.py:61
  678.9 11.7 %cholesky.872 = f32[128,128]{1,0:T(8,128)S(1)} custom-call(f32[128,128]{1,0:T(8,128)S(1)} %convolution_subtract_fusion.3), custom_call_target="Cholesky" | custom-call | tf_op jit(solution)/shard_map/jit(cholesky)/cholesky | solution.py:61
  708.1 9.6 %copy.9 = f32[1536,1536]{1,0:T(8,128)} copy(f32[1536,1536]{0,1:T(8,128)} %select_bitcast_fusion) | data formatting | bytes 18874368 | tf_op jit(solution)/shard_map/transpose | solution.py:61
  (80 shorter events, 120.6 us)
Async XLA Ops:
  55.7 6.2 copy-start
  55.7 6.2 copy-start.1
  55.7 77.6 %all-to-all-start = ((bf16[8,2048,192]{1,2,0:T(8,128)(2,1)}), bf16[8,2048,192]{1,2,0:T(8,128)(2,1)}, u32[]{:S(2)}, u32[]{:S(2)}) async-start(bf16[8,2048,192]{1,2,0:T(8,128)(2,1)} %bitcast.80), calls=%async_computation | async-start | bytes 12582912 | tf_op jit(solution)/shard_map/all_to_all | solution.py:57
  61.9 278.0 %all-reduce.3.cloned.1.call-start = ((), (), s32[]{:S(2)}) async-start(), calls=%async_computation.1 | async-start | bytes 18874368 | tf_op jit(solution)/shard_map/psum | solution.py:60
Sparse Core Ops, SparseCore 0:
  175.1 164.6 all-reduce.2
where the time goes:
time: 735 us; the launch traced here: 725 us
  other arithmetic  314 us (43%)
  waiting for transfers between devices  236 us (32%)
  local copies, waits for them, and re-layouts  74.8 us (10%)
  matrix products  72.5 us (10%)
  between operations  21.8 us (3%)
    another operation x47, other arithmetic, shards(): return jnp.linalg.cholesky(gram_full / total_rows).T  265 us
    psum x1, waiting for transfers between devices, shards(): gram_full = lax.psum(gram_of(rotated), ('tm', 'gauge'))  165 us
    all_to_all x1, waiting for transfers between devices, shards(): lax.all_to_all(filtered, 'gauge', split_axis=0, concat_axis=1, tiled=True)  71.3 us
    another operation x22, matrix products, shards(): return jnp.linalg.cholesky(gram_full / total_rows).T  50.7 us
    unnamed x5, local copies, waits for them, and re-layouts  21.3 us
    div x2, other arithmetic, shards(): return jnp.linalg.cholesky(gram_full / total_rows).T  20.9 us
    dot_general x1, matrix products, gram_of(): lax.dot_general(rotated, rotated, (((0,), (0,)), ((), ())), preferred_ele...  17.2 us
    gather x1, local copies, waits for them, and re-layouts, rosette_rotate(): picked = jnp.take(full_rows, column_map, axis=1)  16.3 us
  transfers between devices with their start and end apart: 2, of which 2 were waited for; matrix products, arithmetic and copies ran while one was open for 0% of the time, Pallas kernels for 0%

commit v1 on v0

v1 whole, which is shorter than its diff:
```python
import functools

import jax
import jax.numpy as jnp
from jax import lax
from jax.experimental import pallas as pl
from jax.experimental.pallas import tpu as pltpu
from jax.sharding import Mesh
from jax.sharding import PartitionSpec as P

BLOCK = 1024
BAND = 64
TILE = 128
CORES = 2
SAMPLE_AXES = ("z", "x")
GAUGE_AXES = ("y", "core")
PLANE_AXES = ("z", "x", "y")
HIGHEST = lax.Precision.HIGHEST
VMEM_BYTES = 56 * 1024 * 1024


def block_index(nb, i, j):
    return sum(nb - k for k in range(i)) + (j - i)


def half_blocks(nb):
    return -(-(nb * (nb + 1) // 2) // (4 * CORES)) * 4


def filter_kernel(chunk, nchunk, offsets, x_ref, out_ref):
    start = offsets[pl.program_id(0) * nchunk + chunk]
    x = x_ref[...].astype(jnp.float32)
    lane = lax.broadcasted_iota(jnp.int32, x.shape, 1)
    inside = (lane >= start) & (lane < start + BAND)
    baseline = jnp.sum(jnp.where(inside, x, 0.0), axis=1, keepdims=True) * (1.0 / BAND)
    out_ref[0] = (x - baseline).astype(out_ref.dtype)


def filter_chunk(records_t, offsets, chunk, nchunk, parts):
    rows = records_t.shape[0]
    return pl.pallas_call(
        functools.partial(filter_kernel, chunk, nchunk),
        out_shape=jax.ShapeDtypeStruct((parts, rows, BLOCK), jnp.bfloat16),
        grid_spec=pltpu.PrefetchScalarGridSpec(
            num_scalar_prefetch=1,
            grid=(parts,),
            in_specs=[pl.BlockSpec((rows, BLOCK), lambda d, off: (0, d * nchunk + chunk))],
            out_specs=pl.BlockSpec((1, rows, BLOCK), lambda d, off: (d, 0, 0)),
        ),
        compiler_params=pltpu.CompilerParams(vmem_limit_bytes=VMEM_BYTES),
        name="drift_filter",
    )(offsets, records_t)


def gram_kernel(first, core, *refs):
    if first:
        pick_ref, ft_ref, coef_ref, mine_out, other_out, rt_ref, acc_ref, sem = refs
        mine_in = other_in = None
    else:
        pick_ref, ft_ref, coef_ref, mine_in, other_in, mine_out, other_out, rt_ref, acc_ref, sem = refs
    step = pl.program_id(0)
    me = core[0]

    def loads():
        return (
            pltpu.make_async_copy(mine_in, acc_ref.at[me], sem.at[0]),
            pltpu.make_async_copy(other_in, acc_ref.at[1 - me], sem.at[1]),
        )

    if not first:

        @pl.when(step == 0)
        def _():
            for copy in loads():
                copy.start()

    ft = ft_ref[...]
    gauges = pick_ref.shape[1]
    samples = ft.shape[1]
    first_arm, middle_arm, last_arm = (
        jnp.dot(pick_ref[k], ft, preferred_element_type=jnp.float32) for k in range(3)
    )
    shear = 2.0 * middle_arm - first_arm - last_arm
    cos_sq, sin_sq, mixed = (
        jnp.broadcast_to(coef_ref[k][:, 0:1], (gauges, samples)) for k in range(3)
    )
    twist = shear * mixed
    along_x = first_arm * cos_sq + last_arm * sin_sq + twist
    along_y = first_arm * sin_sq + last_arm * cos_sq - twist
    shear_new = 2.0 * (last_arm - first_arm) * mixed + shear * (cos_sq - sin_sq)
    per_arm = rt_ref.shape[0] // 3
    here = pl.multiple_of(step * gauges, gauges)
    for k, value in enumerate((along_x, along_y, shear_new)):
        rt_ref[pl.ds(k * per_arm + here, gauges), :] = value.astype(jnp.bfloat16)

    @pl.when(step == pl.num_programs(0) - 1)
    def _():
        if not first:
            for copy in loads():
                copy.wait()
        nb = rt_ref.shape[0] // TILE
        used = nb * (nb + 1) // 2
        if first:
            for idx in range(used, CORES * acc_ref.shape[1]):
                acc_ref[idx % CORES, idx // CORES] = jnp.zeros((TILE, TILE), jnp.float32)
        for j in range(0, nb, 2):
            cols = rt_ref[TILE * j : TILE * (j + 2), :]
            rows = rt_ref[0 : TILE * (j + 2), :]
            part = lax.dot_general(
                rows, cols, (((1,), (1,)), ((), ())), preferred_element_type=jnp.float32
            )
            for i in range(j + 2):
                for jj in range(max(i, j), j + 2):
                    idx = block_index(nb, i, jj)
                    block = part[TILE * i : TILE * (i + 1), TILE * (jj - j) : TILE * (jj - j + 1)]
                    if first:
                        acc_ref[idx % CORES, idx // CORES] = block
                    else:
                        acc_ref[idx % CORES, idx // CORES] += block
        stores = (
            pltpu.make_async_copy(acc_ref.at[me], mine_out, sem.at[0]),
            pltpu.make_async_copy(acc_ref.at[1 - me], other_out, sem.at[1]),
        )
        for copy in stores:
            copy.start()
        for copy in stores:
            copy.wait()


def gram_chunk(core, pick, ft, coef, so_far):
    per_arm, cols = pick.shape[1], pick.shape[2]
    samples = ft.shape[1]
    half = half_blocks(cols // TILE)
    shape = jax.ShapeDtypeStruct((half, TILE, TILE), jnp.float32)
    anywhere = pl.BlockSpec(memory_space=pl.ANY)
    return pl.pallas_call(
        functools.partial(gram_kernel, so_far is None),
        out_shape=(shape, shape),
        grid_spec=pltpu.PrefetchScalarGridSpec(
            num_scalar_prefetch=1,
            grid=(per_arm // TILE,),
            in_specs=[
                pl.BlockSpec((3, TILE, cols), lambda g, core: (0, g, 0)),
                pl.BlockSpec((cols, samples), lambda g, core: (0, 0)),
                pl.BlockSpec((3, TILE, TILE), lambda g, core: (0, g, 0)),
            ]
            + ([] if so_far is None else [anywhere, anywhere]),
            out_specs=(anywhere, anywhere),
            scratch_shapes=[
                pltpu.VMEM((cols, samples), jnp.bfloat16),
                pltpu.VMEM((CORES, half, TILE, TILE), jnp.float32),
                pltpu.SemaphoreType.DMA((2,)),
            ],
        ),
        compiler_params=pltpu.CompilerParams(vmem_limit_bytes=VMEM_BYTES),
        name="rotate_gram",
    )(core, pick, ft, coef, *(() if so_far is None else so_far))


def dot_tn(a, b):
    return lax.dot_general(
        a, b, (((0,), (0,)), ((), ())), precision=HIGHEST, preferred_element_type=jnp.float32
    )


def dot_nn(a, b):
    return lax.dot_general(
        a, b, (((1,), (0,)), ((), ())), precision=HIGHEST, preferred_element_type=jnp.float32
    )


def factor_block(a_ref, e_ref):
    lane = lax.broadcasted_iota(jnp.int32, (8, TILE), 1)
    sub = lax.broadcasted_iota(jnp.int32, (8, TILE), 0)
    rows = lax.broadcasted_iota(jnp.int32, (TILE, TILE), 0)
    cols = lax.broadcasted_iota(jnp.int32, (TILE, TILE), 1)
    e_ref[...] = (rows == cols).astype(jnp.float32)

    def strip(s, carry):
        r0 = pl.multiple_of(8 * s, 8)
        cur = a_ref[pl.ds(r0, 8), :]
        ecur = e_ref[pl.ds(r0, 8), :]
        d = [
            jnp.take_along_axis(cur, jnp.full((8, TILE), r0 + j, jnp.int32), axis=1)
            for j in range(8)
        ]
        for j in range(7):
            m = jnp.where(sub > j, d[j] * (1.0 / d[j][j : j + 1, :]), 0.0)
            cur = cur - m * cur[j : j + 1, :]
            ecur = ecur - m * ecur[j : j + 1, :]
            for k in range(j + 1, 8):
                d[k] = d[k] - m * d[k][j : j + 1, :]
        pivot = d[0]
        for j in range(1, 8):
            pivot = jnp.where(sub == j, d[j], pivot)
        scale = lax.rsqrt(pivot)
        cur = jnp.where(lane >= r0 + sub, cur * scale, 0.0)
        ecur = ecur * scale
        later = jnp.where(lane >= r0 + 8, cur, 0.0)
        a_ref[...] -= dot_tn(later, cur)
        e_ref[...] -= dot_tn(later, ecur)
        a_ref[pl.ds(r0, 8), :] = cur
        e_ref[pl.ds(r0, 8), :] = ecur
        return carry

    lax.fori_loop(0, TILE // 8, strip, 0)


def cholesky_kernel(scale, core, mine_ref, other_ref, u_ref, g_ref, a_ref, e_ref, s_ref, sem):
    me = core[0]
    loads = (
        pltpu.make_async_copy(mine_ref, g_ref.at[me], sem.at[0]),
        pltpu.make_async_copy(other_ref, g_ref.at[1 - me], sem.at[1]),
    )
    for copy in loads:
        copy.start()
    for copy in loads:
        copy.wait()
    size = u_ref.shape[0]
    nb = size // TILE
    for r0 in range(0, size, 2 * TILE):
        u_ref[r0 : r0 + 2 * TILE, :] = jnp.zeros((2 * TILE, size), jnp.float32)
        for h in range(2):
            i = r0 // TILE + h
            for j in range(i, nb):
                idx = block_index(nb, i, j)
                s_ref[TILE * h : TILE * (h + 1), TILE * j : TILE * (j + 1)] = (
                    g_ref[idx % CORES, idx // CORES] * scale
                )
        for h in range(2):
            c0 = r0 + TILE * h
            here = slice(TILE * h, TILE * (h + 1))
            if r0:
                s_ref[here, c0:] -= dot_tn(u_ref[0:r0, c0 : c0 + TILE], u_ref[0:r0, c0:])
        for h in range(2):
            c0 = r0 + TILE * h
            here = slice(TILE * h, TILE * (h + 1))
            if h:
                s_ref[here, c0:] -= dot_tn(u_ref[r0:c0, c0 : c0 + TILE], u_ref[r0:c0, c0:])
            a_ref[...] = s_ref[here, c0 : c0 + TILE]
            factor_block(a_ref, e_ref)
            u_ref[c0 : c0 + TILE, c0 : c0 + TILE] = a_ref[...]
            if c0 + TILE < size:
                u_ref[c0 : c0 + TILE, c0 + TILE :] = dot_nn(e_ref[...], s_ref[here, c0 + TILE :])


def cholesky_blocks(core, mine, other, size, scale):
    half = mine.shape[0]
    anywhere = pl.BlockSpec(memory_space=pl.ANY)
    return pl.pallas_call(
        functools.partial(cholesky_kernel, scale),
        out_shape=jax.ShapeDtypeStruct((size, size), jnp.float32),
        grid_spec=pltpu.PrefetchScalarGridSpec(
            num_scalar_prefetch=1,
            grid=(1,),
            in_specs=[anywhere, anywhere],
            out_specs=pl.BlockSpec((size, size), lambda g, core: (0, 0), pipeline_mode=pl.Buffered(1)),
            scratch_shapes=[
                pltpu.VMEM((CORES, half, TILE, TILE), jnp.float32),
                pltpu.VMEM((TILE, TILE), jnp.float32),
                pltpu.VMEM((TILE, TILE), jnp.float32),
                pltpu.VMEM((2 * TILE, size), jnp.float32),
                pltpu.SemaphoreType.DMA((2,)),
            ],
        ),
        compiler_params=pltpu.CompilerParams(vmem_limit_bytes=VMEM_BYTES),
        name="cholesky",
    )(core, mine, other)


def swap_cores(x):
    return lax.ppermute(x, "core", [(0, 1), (1, 0)])


def gather_plane(x):
    plane = lax.axis_size(PLANE_AXES)
    copies = jnp.broadcast_to(x[None], (plane, *x.shape))
    return lax.all_to_all(copies, PLANE_AXES, split_axis=0, concat_axis=0, tiled=True)


def shards(records, offsets, column_map, angles):
    parts = lax.axis_size(GAUGE_AXES)
    rows, cols_here = records.shape
    cols = column_map.shape[0]
    per_arm = cols // 3
    nchunk = rows // BLOCK // parts
    core = lax.axis_index("core").astype(jnp.int32).reshape(1)
    records_t = records.T
    arms = column_map.reshape(3, per_arm, 1)
    pick = (arms == jnp.arange(cols, dtype=jnp.int32)[None, None, :]).astype(jnp.bfloat16)
    cosine, sine = jnp.cos(angles), jnp.sin(angles)
    coef = jnp.stack([cosine * cosine, sine * sine, sine * cosine])
    coef = jnp.broadcast_to(coef[:, :, None], (3, per_arm, TILE))
    chunks = [filter_chunk(records_t, offsets, c, nchunk, parts) for c in range(nchunk)]
    acc = None
    for filtered in chunks:
        regrouped = lax.all_to_all(filtered, GAUGE_AXES, split_axis=0, concat_axis=0, tiled=True)
        acc = gram_chunk(core, pick, regrouped.reshape(cols, BLOCK), coef, acc)
    mine, other = acc
    half = mine.shape[0]
    mine = mine + swap_cores(other)
    plane = lax.axis_size(PLANE_AXES)
    share = half * TILE // plane
    spread = lax.all_to_all(
        mine.reshape(plane, share, TILE), PLANE_AXES, split_axis=0, concat_axis=0, tiled=True
    )
    mine = gather_plane(spread.sum(0)).reshape(half, TILE, TILE)
    other = swap_cores(mine)
    total = rows * lax.axis_size(SAMPLE_AXES)
    return cholesky_blocks(core, mine, other, cols, 1.0 / total)


def solution(mesh):
    devices = mesh.devices
    tm, gauge = devices.shape
    side = int(round(tm**0.5))
    fine = Mesh(
        devices.reshape(side, tm // side, gauge // CORES, CORES), SAMPLE_AXES + GAUGE_AXES
    )
    placed = (P(SAMPLE_AXES, GAUGE_AXES), P(SAMPLE_AXES), P(), P())
    return jax.shard_map(shards, mesh=fine, in_specs=placed, out_specs=P(), check_vma=False)
```

time: 735 us -> 324 us (0.44); the launches traced: 725 us -> 323 us
  other arithmetic: 314 us -> 5.42 us
  waiting for transfers between devices: 236 us -> 58.8 us
  Pallas kernels: 0 us -> 156 us
  blocking collectives: 0 us -> 82.6 us
  matrix products: 72.5 us -> 0 us
  local copies, waits for them, and re-layouts: 74.8 us -> 4.62 us
  between operations: 21.8 us -> 0.24 us
  starting transfers between devices: 6.17 us -> 15.2 us
    another operation x48 -> x1, other arithmetic: 270 us -> 0.01 us  [shards(): coef = jnp.stack([cosine * cosine, sine * sine, sine * cosine])]
    psum x1 -> x0, waiting for transfers between devices: 165 us -> none  [shards(): gram_full = lax.psum(gram_of(rotated), ('tm', 'gauge'))]
    pallas_call x0 -> x5, Pallas kernels: none -> 156 us  [the longest x1 113 us: cholesky_blocks(): pl.pallas_call(functools.partial(cholesky_kernel, scale), out_shape=jax.S...]
    all_to_all x0 -> x2, blocking collectives: none -> 82.6 us  [the longest x1 43.6 us: shards(): lax.all_to_all(mine.reshape(plane, share, TILE), PLANE_AXES, split_axis=0...]
    another operation x22 -> x0, matrix products: 50.7 us -> none  [shards(): return jnp.linalg.cholesky(gram_full / total_rows).T]
    dot_general x2 -> x0, matrix products: 21.8 us -> none  [the longest x1 17.2 us: gram_of(): lax.dot_general(rotated, rotated, (((0,), (0,)), ((), ())), preferred_ele...]
    all_to_all x1 -> x2, waiting for transfers between devices: 71.3 us -> 49.5 us  [shards(): lax.all_to_all(filtered, GAUGE_AXES, split_axis=0, concat_axis=0, tiled=T...]
    div x2 -> x0, other arithmetic: 20.9 us -> none  [shards(): return jnp.linalg.cholesky(gram_full / total_rows).T]
  transfers between devices with their start and end apart: 2 -> 4, of which waited for: 2 -> 4; matrix products, arithmetic and copies ran while one was open for 0% -> 1% of each run, Pallas kernels for 0% -> 7%
where the time goes in v1:
time: 324 us; the launch traced here: 323 us
  Pallas kernels  156 us (48%)
  blocking collectives  82.6 us (25%)
  waiting for transfers between devices  58.8 us (18%)
  starting transfers between devices  15.2 us (5%)
  other arithmetic  5.42 us (2%)
  local copies, waits for them, and re-layouts  4.62 us (1%)
    pallas_call x1, Pallas kernels, cholesky_blocks(): pl.pallas_call(functools.partial(cholesky_kernel, scale), out_shape=jax.S...  113 us
    all_to_all x2, waiting for transfers between devices, shards(): lax.all_to_all(filtered, GAUGE_AXES, split_axis=0, concat_axis=0, tiled=T...  49.5 us
    all_to_all x1, blocking collectives, shards(): lax.all_to_all(mine.reshape(plane, share, TILE), PLANE_AXES, split_axis=0...  43.6 us
    all_to_all x1, blocking collectives, gather_plane(): lax.all_to_all(copies, PLANE_AXES, split_axis=0, concat_axis=0, tiled=True)  39 us
    pallas_call x2, Pallas kernels, gram_chunk(): pl.pallas_call(functools.partial(gram_kernel, so_far is None), out_shape=...  28.2 us
    pallas_call x2, Pallas kernels, filter_chunk(): pl.pallas_call(functools.partial(filter_kernel, chunk, nchunk), out_shape...  14.6 us
    all_to_all x2, starting transfers between devices, shards(): lax.all_to_all(filtered, GAUGE_AXES, split_axis=0, concat_axis=0, tiled=T...  11.2 us
    ppermute x2, waiting for transfers between devices, swap_cores(): return lax.ppermute(x, 'core', [(0, 1), (1, 0)])  9.28 us
  transfers between devices with their start and end apart: 4, of which 4 were waited for; matrix products, arithmetic and copies ran while one was open for 1% of the time, Pallas kernels for 7%

profile of v1, /device:TPU:1, one launch (start us, length us, event | category | flops | bytes accessed | tf_op | source)
XLA Modules:
  0.0 323.2 jit_solution(15454869682160511735)
XLA Ops:
  0.0 7.3 %drift_filter.3 = bf16[8,192,1024]{2,1,0:T(8,128)(2,1)} custom-call(s32[16]{0:T(128)} %offsets.3, bf16[192,16384]{1,0:T(8,128)(2,1)} %bitcast.9), custom_call_target="tpu_custom_call" | custom-call | tf_op jit(solution)/shard_map/drift_filter/pallas_call | solution.py:41
  7.3 6.0 %all-to-all-start.1 = ((bf16[8,192,1024]{2,1,0:T(8,128)(2,1)}), bf16[8,192,1024]{2,1,0:T(8,128)(2,1)S(1)}, u32[]{:S(2)}, u32[]{:S(2)}) async-start(bf16[8,192,1024]{2,1,0:T(8,128)(2,1)} %drift_filter.3), calls=%async_computation.1 | async-start | bytes 6291456 | tf_op jit(solution)/shard_map/all_to_all | solution.py:297
  13.3 7.3 %drift_filter.2 = bf16[8,192,1024]{2,1,0:T(8,128)(2,1)} custom-call(s32[16]{0:T(128)} %offsets.3, bf16[192,16384]{1,0:T(8,128)(2,1)} %bitcast.10), custom_call_target="tpu_custom_call" | custom-call | tf_op jit(solution)/shard_map/drift_filter/pallas_call | solution.py:41
  20.6 0.0 copy-start.3
  20.6 0.0 copy-start.4
  20.6 30.2 %all-to-all-done.1 = bf16[8,192,1024]{2,1,0:T(8,128)(2,1)S(1)} async-done(((bf16[8,192,1024]{2,1,0:T(8,128)(2,1)}), bf16[8,192,1024]{2,1,0:T(8,128)(2,1)S(1)}, u32[]{:S(2)}, u32[]{:S(2)}) %all-to-all-start.1) | async-done | bytes 3145760 | tf_op jit(solution)/shard_map/all_to_all | solution.py:297
  50.8 0.0 copy-start
  50.8 1.7 copy-done
  52.5 5.2 %all-to-all-start = ((bf16[8,192,1024]{2,1,0:T(8,128)(2,1)}), bf16[8,192,1024]{2,1,0:T(8,128)(2,1)}, u32[]{:S(2)}, u32[]{:S(2)}) async-start(bf16[8,192,1024]{2,1,0:T(8,128)(2,1)} %drift_filter.2), calls=%async_computation | async-start | bytes 6291456 | tf_op jit(solution)/shard_map/all_to_all | solution.py:297
  57.7 0.0 copy-done.3
  57.7 0.0 copy-done.4
  57.8 3.0 fusion.refs_0_
  60.8 1.2 broadcast_in_dim.4.refs_2_
  62.0 14.1 %rotate_gram.2 = (f32[40,128,128]{2,1,0:T(8,128)}, f32[40,128,128]{2,1,0:T(8,128)}) custom-call(s32[1]{0:T(128)} %bitcast.core, bf16[3,512,1536]{2,1,0:T(8,128)(2,1)} %fusion.refs_0_, bf16[1536,1024]{1,0:T(8,128)(2,1)} %bitcast.11, f32[3,512,128]{2,1,0:T(8,128)} %broadcast_in_dim.4.refs_2_), custom_call_target="tpu_custom_call" | custom-call | tf_op jit(solution)/shard_map/rotate_gram/pallas_call | solution.py:136
  76.2 19.3 %all-to-all-done = bf16[8,192,1024]{2,1,0:T(8,128)(2,1)} async-done(((bf16[8,192,1024]{2,1,0:T(8,128)(2,1)}), bf16[8,192,1024]{2,1,0:T(8,128)(2,1)}, u32[]{:S(2)}, u32[]{:S(2)}) %all-to-all-start) | async-done | bytes 3145760 | tf_op jit(solution)/shard_map/all_to_all | solution.py:297
  95.4 14.0 %rotate_gram.3 = (f32[40,128,128]{2,1,0:T(8,128)}, f32[40,128,128]{2,1,0:T(8,128)}) custom-call(s32[1]{0:T(128)} %bitcast.core, bf16[3,512,1536]{2,1,0:T(8,128)(2,1)} %fusion.refs_0_, bf16[1536,1024]{1,0:T(8,128)(2,1)} %bitcast.2.refs_1_, f32[3,512,128]{2,1,0:T(8,128)} %broadcast_in_dim.4.refs_2_, f32[40,128,128]{2,1,0:T(8,128)} %get-tuple-element.9.refs_3_, ...), custom_call_target="tpu_custom_call" | custom-call | tf_op jit(solution)/shard_map/rotate_gram/pallas_call | solution.py:136
  109.5 1.0 collective-permute-start
  110.4 4.7 %collective-permute-done = f32[40,128,128]{2,1,0:T(8,128)S(1)} collective-permute-done((f32[40,128,128]{2,1,0:T(8,128)}, f32[40,128,128]{2,1,0:T(8,128)S(1)}, u32[]{:S(2)}, u32[]{:S(2)}) %collective-permute-start) | collective-permute-done | bytes 2621472 | tf_op jit(solution)/shard_map/ppermute | solution.py:272
  115.2 2.2 add.3
  117.4 43.6 %all_to_all.20 = f32[64,80,128]{2,1,0:T(8,128)S(1)} all-to-all(f32[64,80,128]{2,1,0:T(8,128)S(1)} %bitcast.14), channel_id=1, replica_groups=mesh['z'=4,'x'=4,'y'=4,'core'=2] {'z','x','y'}, dimensions={0} | all-to-all | bytes 5242880 | tf_op jit(solution)/shard_map/all_to_all | solution.py:304
  161.0 0.2 reduce_sum.9
  161.2 0.2 broadcast_in_dim.5
  161.4 39.0 %all_to_all.21 = f32[64,80,128]{2,1,0:T(8,128)S(1)} all-to-all(f32[64,80,128]{2,1,0:T(8,128)S(1)} %broadcast_in_dim.5), channel_id=1, replica_groups=mesh['z'=4,'x'=4,'y'=4,'core'=2] {'z','x','y'}, dimensions={0} | all-to-all | bytes 5242880 | tf_op jit(solution)/shard_map/all_to_all | solution.py:278
  200.4 0.0 copy-start.1
  200.4 3.1 collective-permute-start.1
  203.5 4.5 %collective-permute-done.1.other_ref = f32[40,128,128]{2,1,0:T(8,128)S(1)} collective-permute-done((f32[40,128,128]{2,1,0:T(8,128)S(1)}, f32[40,128,128]{2,1,0:T(8,128)S(1)}, u32[]{:S(2)}, u32[]{:S(2)}) %collective-permute-start.1) | collective-permute-done | bytes 2621472 | tf_op jit(solution)/shard_map/ppermute | solution.py:272
  208.0 0.0 copy-done.1
  208.1 0.0 copy-start.2
  208.1 1.5 copy-done.2
  209.6 113.4 %cholesky.1 = f32[1536,1536]{1,0:T(8,128)} custom-call(s32[1]{0:T(128)} %bitcast.core, f32[40,128,128]{2,1,0:T(8,128)} %bitcast.13, f32[40,128,128]{2,1,0:T(8,128)} %copy-done.2), custom_call_target="tpu_custom_call" | custom-call | tf_op jit(solution)/shard_map/cholesky/pallas_call | solution.py:250
  (4 shorter events, 0.1 us)
Async XLA Ops:
  7.3 43.5 %all-to-all-start.1 = ((bf16[8,192,1024]{2,1,0:T(8,128)(2,1)}), bf16[8,192,1024]{2,1,0:T(8,128)(2,1)S(1)}, u32[]{:S(2)}, u32[]{:S(2)}) async-start(bf16[8,192,1024]{2,1,0:T(8,128)(2,1)} %drift_filter.3), calls=%async_computation.1 | async-start | bytes 6291456 | tf_op jit(solution)/shard_map/all_to_all | solution.py:297
  20.6 37.1 %copy-start.3 = (s32[1536]{0:T(1024)S(1)}, s32[1536]{0:T(1024)}, u32[]{:S(2)}) copy-start(s32[1536]{0:T(1024)} %param.6) | copy-start | bytes 18436
  20.6 37.2 %copy-start.4 = (f32[512]{0:T(512)S(1)}, f32[512]{0:T(512)}, u32[]{:S(2)}) copy-start(f32[512]{0:T(512)} %param.7) | copy-start | bytes 6148
  50.8 1.7 copy-start
  52.5 42.9 %all-to-all-start = ((bf16[8,192,1024]{2,1,0:T(8,128)(2,1)}), bf16[8,192,1024]{2,1,0:T(8,128)(2,1)}, u32[]{:S(2)}, u32[]{:S(2)}) async-start(bf16[8,192,1024]{2,1,0:T(8,128)(2,1)} %drift_filter.2), calls=%async_computation | async-start | bytes 6291456 | tf_op jit(solution)/shard_map/all_to_all | solution.py:297
  109.5 5.7 %collective-permute-start = (f32[40,128,128]{2,1,0:T(8,128)}, f32[40,128,128]{2,1,0:T(8,128)S(1)}, u32[]{:S(2)}, u32[]{:S(2)}) collective-permute-start(f32[40,128,128]{2,1,0:T(8,128)} %get-tuple-element.12), channel_id=1, source_target_pairs={{0,1},{1,0},{2,3},{3,2},{4,5},{5,4},{6,7},{7,6},{8,9},{9,8},{10,11... | collective-permute-start | bytes 7864328 | tf_op jit(solution)/shard_map/ppermute | solution.py:272
  200.4 7.7 %copy-start.1 = (f32[64,80,128]{2,1,0:T(8,128)}, f32[64,80,128]{2,1,0:T(8,128)S(1)}, u32[]{:S(2)}) copy-start(f32[64,80,128]{2,1,0:T(8,128)S(1)} %all_to_all.21) | copy-start | bytes 7864324
  200.4 7.6 %collective-permute-start.1 = (f32[40,128,128]{2,1,0:T(8,128)S(1)}, f32[40,128,128]{2,1,0:T(8,128)S(1)}, u32[]{:S(2)}, u32[]{:S(2)}) collective-permute-start(f32[40,128,128]{2,1,0:T(8,128)S(1)} %bitcast.12), channel_id=1, source_target_pairs={{0,1},{1,0},{2,3},{3,2},{4,5},{5,4},{6,7},{7,6},{8,9},{9,8},{10,11... | collective-permute-start | bytes 7864328 | tf_op jit(solution)/shard_map/ppermute | solution.py:272
  208.1 1.5 copy-start.2

commit v2 on v1

--- a/solution.py
+++ b/solution.py
@@ -27,25 +27,37 @@
     return -(-(nb * (nb + 1) // 2) // (4 * CORES)) * 4
 
 
-def filter_kernel(chunk, nchunk, offsets, x_ref, out_ref):
-    start = offsets[pl.program_id(0) * nchunk + chunk]
-    x = x_ref[...].astype(jnp.float32)
-    lane = lax.broadcasted_iota(jnp.int32, x.shape, 1)
-    inside = (lane >= start) & (lane < start + BAND)
-    baseline = jnp.sum(jnp.where(inside, x, 0.0), axis=1, keepdims=True) * (1.0 / BAND)
-    out_ref[0] = (x - baseline).astype(out_ref.dtype)
-
-
-def filter_chunk(records_t, offsets, chunk, nchunk, parts):
-    rows = records_t.shape[0]
+def filter_kernel(blocks, offsets, x_ref, head_ref, tail_ref):
+    split = head_ref.shape[2]
+    for b in range(blocks):
+        start = offsets[pl.program_id(0) * blocks + b]
+        x = x_ref[:, b * BLOCK : (b + 1) * BLOCK]
+        sample = lax.broadcasted_iota(jnp.int32, (BLOCK, TILE), 0)
+        inside = jnp.where((sample >= start) & (sample < start + BAND), 1.0, 0.0)
+        total = jnp.dot(x, inside.astype(jnp.bfloat16), preferred_element_type=jnp.float32)
+        baseline = total * (1.0 / BAND)
+        for t in range(0, BLOCK, TILE):
+            value = (x[:, t : t + TILE].astype(jnp.float32) - baseline).astype(jnp.bfloat16)
+            here = b * BLOCK + t
+            if here < split:
+                head_ref[0, :, here : here + TILE] = value
+            else:
+                tail_ref[0, :, here - split : here - split + TILE] = value
+
+
+def filter_records(records_t, offsets, parts):
+    rows, samples = records_t.shape
+    each = samples // parts
+    tail = BLOCK // 2
+    widths = (each - tail, tail)
     return pl.pallas_call(
-        functools.partial(filter_kernel, chunk, nchunk),
-        out_shape=jax.ShapeDtypeStruct((parts, rows, BLOCK), jnp.bfloat16),
+        functools.partial(filter_kernel, each // BLOCK),
+        out_shape=tuple(jax.ShapeDtypeStruct((parts, rows, w), jnp.bfloat16) for w in widths),
         grid_spec=pltpu.PrefetchScalarGridSpec(
             num_scalar_prefetch=1,
             grid=(parts,),
-            in_specs=[pl.BlockSpec((rows, BLOCK), lambda d, off: (0, d * nchunk + chunk))],
-            out_specs=pl.BlockSpec((1, rows, BLOCK), lambda d, off: (d, 0, 0)),
+            in_specs=[pl.BlockSpec((rows, each), lambda d, off: (0, d))],
+            out_specs=tuple(pl.BlockSpec((1, rows, w), lambda d, off: (d, 0, 0)) for w in widths),
         ),
         compiler_params=pltpu.CompilerParams(vmem_limit_bytes=VMEM_BYTES),
         name="drift_filter",
@@ -169,79 +181,154 @@
     )
 
 
+def split3(x):
+    high = x.astype(jnp.bfloat16).astype(jnp.float32)
+    rest = x - high
+    middle = rest.astype(jnp.bfloat16).astype(jnp.float32)
+    return high, middle, rest - middle
+
+
+def outer_product(a, b):
+    a1, a2, a3 = split3(a)
+    b1, b2, b3 = split3(b)
+    left = jnp.concatenate([a1, a1, a2, a2, a1, a3], axis=0).astype(jnp.bfloat16)
+    right = jnp.concatenate([b1, b2, b1, b2, b3, b1], axis=0).astype(jnp.bfloat16)
+    return lax.dot_general(
+        left, right, (((0,), (0,)), ((), ())), preferred_element_type=jnp.float32
+    )
+
+
 def factor_block(a_ref, e_ref):
     lane = lax.broadcasted_iota(jnp.int32, (8, TILE), 1)
     sub = lax.broadcasted_iota(jnp.int32, (8, TILE), 0)
-    rows = lax.broadcasted_iota(jnp.int32, (TILE, TILE), 0)
-    cols = lax.broadcasted_iota(jnp.int32, (TILE, TILE), 1)
-    e_ref[...] = (rows == cols).astype(jnp.float32)
-
-    def strip(s, carry):
-        r0 = pl.multiple_of(8 * s, 8)
-        cur = a_ref[pl.ds(r0, 8), :]
-        ecur = e_ref[pl.ds(r0, 8), :]
-        d = [
-            jnp.take_along_axis(cur, jnp.full((8, TILE), r0 + j, jnp.int32), axis=1)
-            for j in range(8)
-        ]
-        for j in range(7):
-            m = jnp.where(sub > j, d[j] * (1.0 / d[j][j : j + 1, :]), 0.0)
-            cur = cur - m * cur[j : j + 1, :]
-            ecur = ecur - m * ecur[j : j + 1, :]
+    strips = TILE // 8
+    work = [a_ref[8 * t : 8 * t + 8, :] for t in range(strips)]
+
+    def columns(x, r0):
+        return [jnp.broadcast_to(x[:, r0 + j : r0 + j + 1], (8, TILE)) for j in range(8)]
+
+    def row_of(x, j):
+        return jnp.broadcast_to(x[j : j + 1, :], (8, TILE))
+
+    for s in range(strips):
+        r0 = 8 * s
+        last = s == strips - 1
+        here = (lane >= r0) & (lane < r0 + 8)
+        top = columns(work[s], r0)
+        cur = jnp.where(here, jnp.where(lane == r0 + sub, 1.0, 0.0), work[s])
+        if not last:
+            low = columns(work[s + 1], r0)
+            nxt = jnp.where(here, 0.0, work[s + 1])
+        for j in range(8):
+            inv = 1.0 / row_of(top[j], j)
+            m_top = jnp.where(sub > j, top[j] * inv, 0.0)
+            m_low = None if last else low[j] * inv
             for k in range(j + 1, 8):
-                d[k] = d[k] - m * d[k][j : j + 1, :]
-        pivot = d[0]
+                c = row_of(top[k], j)
+                if k == j + 1:
+                    top[k] = top[k] - jnp.where(sub > j, top[j] * c, 0.0) * inv
+                else:
+                    top[k] = top[k] - m_top * c
+                if not last:
+                    low[k] = low[k] - m_low * c
+            row = row_of(cur, j)
+            cur = cur - m_top * row
+            if not last:
+                nxt = nxt - m_low * row
+        pivot = top[0]
         for j in range(1, 8):
-            pivot = jnp.where(sub == j, d[j], pivot)
+            pivot = jnp.where(sub == j, top[j], pivot)
         scale = lax.rsqrt(pivot)
-        cur = jnp.where(lane >= r0 + sub, cur * scale, 0.0)
-        ecur = ecur * scale
+        cur = cur * scale
         later = jnp.where(lane >= r0 + 8, cur, 0.0)
-        a_ref[...] -= dot_tn(later, cur)
-        e_ref[...] -= dot_tn(later, ecur)
-        a_ref[pl.ds(r0, 8), :] = cur
-        e_ref[pl.ds(r0, 8), :] = ecur
-        return carry
-
-    lax.fori_loop(0, TILE // 8, strip, 0)
-
-
-def cholesky_kernel(scale, core, mine_ref, other_ref, u_ref, g_ref, a_ref, e_ref, s_ref, sem):
+        out = later
+        for k in range(8):
+            out = jnp.where((lane == r0 + k) & (sub <= k), top[k] * scale, out)
+        a_ref[r0 : r0 + 8, :] = out
+        e_ref[r0 : r0 + 8, :] = jnp.where(lane < r0 + 8, cur, 0.0)
+        if not last:
+            work[s + 1] = nxt
+        if s + 2 < strips:
+            update = outer_product(later, cur)
+            for t in range(s + 2, strips):
+                work[t] = jnp.where(here, 0.0, work[t]) - update[8 * t : 8 * t + 8, :]
+
+
+def cholesky_kernel(
+    scale, core, mine_ref, other_ref, out_ref, u_ref, g_ref, a_ref, e_ref, s_ref, in_sem, out_sem
+):
     me = core[0]
-    loads = (
-        pltpu.make_async_copy(mine_ref, g_ref.at[me], sem.at[0]),
-        pltpu.make_async_copy(other_ref, g_ref.at[1 - me], sem.at[1]),
-    )
-    for copy in loads:
-        copy.start()
-    for copy in loads:
-        copy.wait()
     size = u_ref.shape[0]
     nb = size // TILE
-    for r0 in range(0, size, 2 * TILE):
-        u_ref[r0 : r0 + 2 * TILE, :] = jnp.zeros((2 * TILE, size), jnp.float32)
-        for h in range(2):
-            i = r0 // TILE + h
-            for j in range(i, nb):
-                idx = block_index(nb, i, j)
-                s_ref[TILE * h : TILE * (h + 1), TILE * j : TILE * (j + 1)] = (
-                    g_ref[idx % CORES, idx // CORES] * scale
-                )
-        for h in range(2):
-            c0 = r0 + TILE * h
-            here = slice(TILE * h, TILE * (h + 1))
-            if r0:
-                s_ref[here, c0:] -= dot_tn(u_ref[0:r0, c0 : c0 + TILE], u_ref[0:r0, c0:])
-        for h in range(2):
-            c0 = r0 + TILE * h
-            here = slice(TILE * h, TILE * (h + 1))
-            if h:
-                s_ref[here, c0:] -= dot_tn(u_ref[r0:c0, c0 : c0 + TILE], u_ref[r0:c0, c0:])
-            a_ref[...] = s_ref[here, c0 : c0 + TILE]
-            factor_block(a_ref, e_ref)
-            u_ref[c0 : c0 + TILE, c0 : c0 + TILE] = a_ref[...]
-            if c0 + TILE < size:
-                u_ref[c0 : c0 + TILE, c0 + TILE :] = dot_nn(e_ref[...], s_ref[here, c0 + TILE :])
+    early = nb
+    pieces = ((0, early), (early, g_ref.shape[1]))
+
+    def loads(k):
+        lo, hi = pieces[k]
+        return (
+            pltpu.make_async_copy(mine_ref.at[lo:hi], g_ref.at[me, lo:hi], in_sem.at[2 * k]),
+            pltpu.make_async_copy(
+                other_ref.at[lo:hi], g_ref.at[1 - me, lo:hi], in_sem.at[2 * k + 1]
+            ),
+        )
+
+    def store(k):
+        rows = slice(TILE * k, TILE * (k + 1))
+        return pltpu.make_async_copy(u_ref.at[rows], out_ref.at[rows], out_sem.at[k])
+
+    for k in range(2):
+        for copy in loads(k):
+            copy.start()
+
+    def body(i, carry):
+        for k in range(nb):
+            h = k % 2
+            r0 = TILE * (k - h)
+            c0 = TILE * k
+
+            @pl.when(i == k)
+            def _(k=k, h=h, r0=r0, c0=c0):
+                if k == 0 or k == 2:
+                    for copy in loads(k // 2):
+                        copy.wait()
+                if h == 0:
+                    for hh in range(2):
+                        for j in range(k + hh, nb):
+                            idx = block_index(nb, k + hh, j)
+                            s_ref[TILE * hh : TILE * (hh + 1), TILE * j : TILE * (j + 1)] = (
+                                g_ref[idx % CORES, idx // CORES] * scale
+                            )
+                        if r0:
+                            first = c0 + TILE * hh
+                            s_ref[TILE * hh : TILE * (hh + 1), first:] -= dot_tn(
+                                u_ref[0:r0, first : first + TILE], u_ref[0:r0, first:]
+                            )
+                else:
+                    s_ref[TILE:, c0:] -= dot_tn(u_ref[r0:c0, c0 : c0 + TILE], u_ref[r0:c0, c0:])
+                a_ref[...] = s_ref[TILE * h : TILE * (h + 1), c0 : c0 + TILE]
+
+        factor_block(a_ref, e_ref)
+        for k in range(nb):
+            h = k % 2
+            c0 = TILE * k
+
+            @pl.when(i == k)
+            def _(k=k, h=h, c0=c0):
+                rows = slice(c0, c0 + TILE)
+                if c0:
+                    u_ref[rows, 0:c0] = jnp.zeros((TILE, c0), jnp.float32)
+                u_ref[rows, c0 : c0 + TILE] = a_ref[...]
+                if c0 + TILE < size:
+                    u_ref[rows, c0 + TILE :] = dot_nn(
+                        e_ref[...], s_ref[TILE * h : TILE * (h + 1), c0 + TILE :]
+                    )
+                store(k).start()
+
+        return carry
+
+    lax.fori_loop(0, nb, body, 0)
+    for k in range(nb):
+        store(k).wait()
 
 
 def cholesky_blocks(core, mine, other, size, scale):
@@ -254,13 +341,15 @@
             num_scalar_prefetch=1,
             grid=(1,),
             in_specs=[anywhere, anywhere],
-            out_specs=pl.BlockSpec((size, size), lambda g, core: (0, 0), pipeline_mode=pl.Buffered(1)),
+            out_specs=anywhere,
             scratch_shapes=[
+                pltpu.VMEM((size, size), jnp.float32),
                 pltpu.VMEM((CORES, half, TILE, TILE), jnp.float32),
                 pltpu.VMEM((TILE, TILE), jnp.float32),
                 pltpu.VMEM((TILE, TILE), jnp.float32),
                 pltpu.VMEM((2 * TILE, size), jnp.float32),
-                pltpu.SemaphoreType.DMA((2,)),
+                pltpu.SemaphoreType.DMA((4,)),
+                pltpu.SemaphoreType.DMA((size // TILE,)),
             ],
         ),
         compiler_params=pltpu.CompilerParams(vmem_limit_bytes=VMEM_BYTES),
@@ -283,7 +372,6 @@
     rows, cols_here = records.shape
     cols = column_map.shape[0]
     per_arm = cols // 3
-    nchunk = rows // BLOCK // parts
     core = lax.axis_index("core").astype(jnp.int32).reshape(1)
     records_t = records.T
     arms = column_map.reshape(3, per_arm, 1)
@@ -291,11 +379,10 @@
     cosine, sine = jnp.cos(angles), jnp.sin(angles)
     coef = jnp.stack([cosine * cosine, sine * sine, sine * cosine])
     coef = jnp.broadcast_to(coef[:, :, None], (3, per_arm, TILE))
-    chunks = [filter_chunk(records_t, offsets, c, nchunk, parts) for c in range(nchunk)]
     acc = None
-    for filtered in chunks:
+    for filtered in filter_records(records_t, offsets, parts):
         regrouped = lax.all_to_all(filtered, GAUGE_AXES, split_axis=0, concat_axis=0, tiled=True)
-        acc = gram_chunk(core, pick, regrouped.reshape(cols, BLOCK), coef, acc)
+        acc = gram_chunk(core, pick, regrouped.reshape(cols, -1), coef, acc)
     mine, other = acc
     half = mine.shape[0]
     mine = mine + swap_cores(other)

time: 324 us -> 277 us (0.85)
  blocking collectives: 82.6 us -> 146 us
  Pallas kernels: 156 us -> 104 us
  waiting for transfers between devices: 58.8 us -> 9.53 us
  starting transfers between devices: 15.2 us -> 7.97 us
    all_to_all x0 -> x1, blocking collectives: none -> 61 us  [shards(): lax.all_to_all(filtered, GAUGE_AXES, split_axis=0, concat_axis=0, tiled=T...]
    all_to_all x2 -> x1, waiting for transfers between devices: 49.5 us -> 0.01 us  [shards(): lax.all_to_all(filtered, GAUGE_AXES, split_axis=0, concat_axis=0, tiled=T...]
    pallas_call x1, Pallas kernels: 113 us -> 64.8 us  [cholesky_blocks(): pl.pallas_call(functools.partial(cholesky_kernel, scale), out_shape=jax.S...]
    all_to_all x2 -> x1, starting transfers between devices: 11.2 us -> 4.65 us  [shards(): lax.all_to_all(filtered, GAUGE_AXES, split_axis=0, concat_axis=0, tiled=T...]
    pallas_call x2 -> x1, Pallas kernels: 14.6 us -> 9.58 us  [filter_records(): pl.pallas_call(functools.partial(filter_kernel, each // BLOCK), out_shape...]
  transfers between devices with their start and end apart: 4 -> 3, of which waited for: 4 -> 2; matrix products, arithmetic and copies ran while one was open for 1% -> 2% of each run, Pallas kernels for 7% -> 7%
where the time goes in v2:
time: 277 us
  blocking collectives  146 us (53%)
  Pallas kernels  104 us (38%)
  waiting for transfers between devices  9.53 us (3%)
  starting transfers between devices  7.97 us (3%)
  other arithmetic  5.42 us (2%)
  local copies, waits for them, and re-layouts  4.13 us (1%)
    pallas_call x1, Pallas kernels, cholesky_blocks(): pl.pallas_call(functools.partial(cholesky_kernel, scale), out_shape=jax.S...  64.8 us
    all_to_all x1, blocking collectives, shards(): lax.all_to_all(filtered, GAUGE_AXES, split_axis=0, concat_axis=0, tiled=T...  61 us
    all_to_all x1, blocking collectives, shards(): lax.all_to_all(mine.reshape(plane, share, TILE), PLANE_AXES, split_axis=0...  45.7 us
    all_to_all x1, blocking collectives, gather_plane(): lax.all_to_all(copies, PLANE_AXES, split_axis=0, concat_axis=0, tiled=True)  39 us
    pallas_call x2, Pallas kernels, gram_chunk(): pl.pallas_call(functools.partial(gram_kernel, so_far is None), out_shape=...  29.3 us
    pallas_call x1, Pallas kernels, filter_records(): pl.pallas_call(functools.partial(filter_kernel, each // BLOCK), out_shape...  9.58 us
    ppermute x2, waiting for transfers between devices, swap_cores(): return lax.ppermute(x, 'core', [(0, 1), (1, 0)])  9.53 us
  transfers between devices with their start and end apart: 3, of which 2 were waited for; matrix products, arithmetic and copies ran while one was open for 2% of the time, Pallas kernels for 7%

profile of v2, /device:TPU:1, one launch (start us, length us, event | category | flops | bytes accessed | tf_op | source)
XLA Modules:
  0.0 276.8 jit_solution(14763575514703022379)
XLA Ops:
  0.0 9.6 %drift_filter.1 = (bf16[8,192,1536]{2,1,0:T(8,128)(2,1)}, bf16[8,192,512]{2,1,0:T(8,128)(2,1)}) custom-call(s32[16]{0:T(128)} %offsets.1, bf16[192,16384]{1,0:T(8,128)(2,1)} %bitcast.13), custom_call_target="tpu_custom_call" | custom-call | tf_op jit(solution)/shard_map/drift_filter/pallas_call | solution.py:53
  9.6 61.0 %all_to_all.20 = bf16[8,192,1536]{2,1,0:T(8,128)(2,1)} all-to-all(bf16[8,192,1536]{2,1,0:T(8,128)(2,1)} %get-tuple-element.12), channel_id=1, replica_groups=mesh['z'=4,'x'=4,'y'=4,'core'=2] {'y','core'}, dimensions={0} | all-to-all | bytes 9437184 | tf_op jit(solution)/shard_map/all_to_all | solution.py:384
  70.6 0.0 copy-start.3
  70.6 0.0 copy-start.4
  70.6 4.7 %all-to-all-start = ((bf16[8,192,512]{2,1,0:T(8,128)(2,1)}), bf16[8,192,512]{2,1,0:T(8,128)(2,1)S(1)}, u32[]{:S(2)}, u32[]{:S(2)}) async-start(bf16[8,192,512]{2,1,0:T(8,128)(2,1)} %get-tuple-element.11), calls=%async_computation | async-start | bytes 3145728 | tf_op jit(solution)/shard_map/all_to_all | solution.py:384
  75.3 0.0 copy-done.3
  75.3 0.0 copy-done.4
  75.4 3.0 %fusion.refs_0_ = bf16[3,512,1536]{2,1,0:T(8,128)(2,1)} fusion(s32[3,512]{1,0:T(4,128)S(1)} %eq.15), kind=kLoop, calls=%fused_computation.1 | loop fusion | flops 4718592 | bytes 4724736 | tf_op jit(solution)/shard_map/convert_element_type | solution.py:378
  78.4 1.2 broadcast_in_dim.4.refs_2_
  79.6 18.6 %rotate_gram.2 = (f32[40,128,128]{2,1,0:T(8,128)}, f32[40,128,128]{2,1,0:T(8,128)}) custom-call(s32[1]{0:T(128)} %bitcast.core, bf16[3,512,1536]{2,1,0:T(8,128)(2,1)} %fusion.refs_0_, bf16[1536,1536]{1,0:T(8,128)(2,1)} %bitcast.9, f32[3,512,128]{2,1,0:T(8,128)} %broadcast_in_dim.4.refs_2_), custom_call_target="tpu_custom_call" | custom-call | tf_op jit(solution)/shard_map/rotate_gram/pallas_call | solution.py:148
  98.2 0.0 all-to-all-done
  98.2 0.0 copy-start.1
  98.2 1.2 copy-done.1
  99.4 10.7 %rotate_gram.3 = (f32[40,128,128]{2,1,0:T(8,128)}, f32[40,128,128]{2,1,0:T(8,128)}) custom-call(s32[1]{0:T(128)} %bitcast.core, bf16[3,512,1536]{2,1,0:T(8,128)(2,1)} %fusion.refs_0_, bf16[1536,512]{1,0:T(8,128)(2,1)} %bitcast.14, f32[3,512,128]{2,1,0:T(8,128)} %broadcast_in_dim.4.refs_2_, f32[40,128,128]{2,1,0:T(8,128)} %get-tuple-element.13.refs_3_, ...), custom_call_target="tpu_custom_call" | custom-call | tf_op jit(solution)/shard_map/rotate_gram/pallas_call | solution.py:148
  110.1 0.2 collective-permute-start
  110.3 5.0 %collective-permute-done = f32[40,128,128]{2,1,0:T(8,128)S(1)} collective-permute-done((f32[40,128,128]{2,1,0:T(8,128)}, f32[40,128,128]{2,1,0:T(8,128)S(1)}, u32[]{:S(2)}, u32[]{:S(2)}) %collective-permute-start) | collective-permute-done | bytes 2621472 | tf_op jit(solution)/shard_map/ppermute | solution.py:361
  115.3 2.2 add.3
  117.6 45.7 %all_to_all.21 = f32[64,80,128]{2,1,0:T(8,128)S(1)} all-to-all(f32[64,80,128]{2,1,0:T(8,128)S(1)} %bitcast.12), channel_id=1, replica_groups=mesh['z'=4,'x'=4,'y'=4,'core'=2] {'z','x','y'}, dimensions={0} | all-to-all | bytes 5242880 | tf_op jit(solution)/shard_map/all_to_all | solution.py:391
  163.3 0.2 reduce_sum.9
  163.5 0.2 broadcast_in_dim.5
  163.6 39.0 %all_to_all.22 = f32[64,80,128]{2,1,0:T(8,128)S(1)} all-to-all(f32[64,80,128]{2,1,0:T(8,128)S(1)} %broadcast_in_dim.5), channel_id=1, replica_groups=mesh['z'=4,'x'=4,'y'=4,'core'=2] {'z','x','y'}, dimensions={0} | all-to-all | bytes 5242880 | tf_op jit(solution)/shard_map/all_to_all | solution.py:367
  202.6 0.0 copy-start
  202.6 3.1 %collective-permute-start.1 = (f32[40,128,128]{2,1,0:T(8,128)S(1)}, f32[40,128,128]{2,1,0:T(8,128)S(1)}, u32[]{:S(2)}, u32[]{:S(2)}) collective-permute-start(f32[40,128,128]{2,1,0:T(8,128)S(1)} %bitcast.10), channel_id=1, source_target_pairs={{0,1},{1,0},{2,3},{3,2},{4,5},{5,4},{6,7},{7,6},{8,9},{9,8},{10,11... | collective-permute-start | bytes 7864328 | tf_op jit(solution)/shard_map/ppermute | solution.py:361
  205.8 4.5 %collective-permute-done.1.other_ref = f32[40,128,128]{2,1,0:T(8,128)S(1)} collective-permute-done((f32[40,128,128]{2,1,0:T(8,128)S(1)}, f32[40,128,128]{2,1,0:T(8,128)S(1)}, u32[]{:S(2)}, u32[]{:S(2)}) %collective-permute-start.1) | collective-permute-done | bytes 2621472 | tf_op jit(solution)/shard_map/ppermute | solution.py:361
  210.3 0.0 copy-done
  210.3 0.0 copy-start.2
  210.3 1.5 copy-done.2
  211.8 64.8 %cholesky.1 = f32[1536,1536]{1,0:T(8,128)} custom-call(s32[1]{0:T(128)} %bitcast.core, f32[40,128,128]{2,1,0:T(8,128)} %bitcast.11, f32[40,128,128]{2,1,0:T(8,128)} %copy-done.2), custom_call_target="tpu_custom_call" | custom-call | tf_op jit(solution)/shard_map/cholesky/pallas_call | solution.py:337
  (4 shorter events, 0.1 us)
Async XLA Ops:
  70.6 4.7 %copy-start.3 = (s32[1536]{0:T(1024)S(1)}, s32[1536]{0:T(1024)}, u32[]{:S(2)}) copy-start(s32[1536]{0:T(1024)} %param.6) | copy-start | bytes 18436
  70.6 4.7 %copy-start.4 = (f32[512]{0:T(512)S(1)}, f32[512]{0:T(512)}, u32[]{:S(2)}) copy-start(f32[512]{0:T(512)} %param.7) | copy-start | bytes 6148
  70.6 27.6 %all-to-all-start = ((bf16[8,192,512]{2,1,0:T(8,128)(2,1)}), bf16[8,192,512]{2,1,0:T(8,128)(2,1)S(1)}, u32[]{:S(2)}, u32[]{:S(2)}) async-start(bf16[8,192,512]{2,1,0:T(8,128)(2,1)} %get-tuple-element.11), calls=%async_computation | async-start | bytes 3145728 | tf_op jit(solution)/shard_map/all_to_all | solution.py:384
  98.2 1.2 copy-start.1
  110.1 5.2 %collective-permute-start = (f32[40,128,128]{2,1,0:T(8,128)}, f32[40,128,128]{2,1,0:T(8,128)S(1)}, u32[]{:S(2)}, u32[]{:S(2)}) collective-permute-start(f32[40,128,128]{2,1,0:T(8,128)} %get-tuple-element.16), channel_id=1, source_target_pairs={{0,1},{1,0},{2,3},{3,2},{4,5},{5,4},{6,7},{7,6},{8,9},{9,8},{10,11... | collective-permute-start | bytes 7864328 | tf_op jit(solution)/shard_map/ppermute | solution.py:361
  202.6 7.7 %copy-start = (f32[64,80,128]{2,1,0:T(8,128)}, f32[64,80,128]{2,1,0:T(8,128)S(1)}, u32[]{:S(2)}) copy-start(f32[64,80,128]{2,1,0:T(8,128)S(1)} %all_to_all.22) | copy-start | bytes 7864324
  202.6 7.6 %collective-permute-start.1 = (f32[40,128,128]{2,1,0:T(8,128)S(1)}, f32[40,128,128]{2,1,0:T(8,128)S(1)}, u32[]{:S(2)}, u32[]{:S(2)}) collective-permute-start(f32[40,128,128]{2,1,0:T(8,128)S(1)} %bitcast.10), channel_id=1, source_target_pairs={{0,1},{1,0},{2,3},{3,2},{4,5},{5,4},{6,7},{7,6},{8,9},{9,8},{10,11... | collective-permute-start | bytes 7864328 | tf_op jit(solution)/shard_map/ppermute | solution.py:361
  210.3 1.5 copy-start.2

commit v3 on v2

--- a/solution.py
+++ b/solution.py
@@ -27,14 +27,19 @@
     return -(-(nb * (nb + 1) // 2) // (4 * CORES)) * 4
 
 
+def dot_nt(a, b):
+    return lax.dot_general(a, b, (((1,), (1,)), ((), ())), preferred_element_type=jnp.float32)
+
+
 def filter_kernel(blocks, offsets, x_ref, head_ref, tail_ref):
     split = head_ref.shape[2]
     for b in range(blocks):
         start = offsets[pl.program_id(0) * blocks + b]
         x = x_ref[:, b * BLOCK : (b + 1) * BLOCK]
-        sample = lax.broadcasted_iota(jnp.int32, (BLOCK, TILE), 0)
+        sample = lax.broadcasted_iota(jnp.int32, (1, BLOCK), 1)
         inside = jnp.where((sample >= start) & (sample < start + BAND), 1.0, 0.0)
-        total = jnp.dot(x, inside.astype(jnp.bfloat16), preferred_element_type=jnp.float32)
+        mask = jnp.broadcast_to(inside.astype(jnp.bfloat16), (TILE, BLOCK))
+        total = dot_nt(x, mask)
         baseline = total * (1.0 / BAND)
         for t in range(0, BLOCK, TILE):
             value = (x[:, t : t + TILE].astype(jnp.float32) - baseline).astype(jnp.bfloat16)
@@ -66,10 +71,10 @@
 
 def gram_kernel(first, core, *refs):
     if first:
-        pick_ref, ft_ref, coef_ref, mine_out, other_out, rt_ref, acc_ref, sem = refs
+        map_ref, ft_ref, angle_ref, mine_out, other_out, rt_ref, acc_ref, sem = refs
         mine_in = other_in = None
     else:
-        pick_ref, ft_ref, coef_ref, mine_in, other_in, mine_out, other_out, rt_ref, acc_ref, sem = refs
+        map_ref, ft_ref, angle_ref, mine_in, other_in, mine_out, other_out, rt_ref, acc_ref, sem = refs
     step = pl.program_id(0)
     me = core[0]
 
@@ -87,23 +92,36 @@
                 copy.start()
 
     ft = ft_ref[...]
-    gauges = pick_ref.shape[1]
-    samples = ft.shape[1]
-    first_arm, middle_arm, last_arm = (
-        jnp.dot(pick_ref[k], ft, preferred_element_type=jnp.float32) for k in range(3)
-    )
+    cols, samples = ft.shape
+    lanes = map_ref.shape[1]
+    steps = pl.num_programs(0)
+
+    def down(row):
+        return jnp.broadcast_to(row, (lanes, lanes)).T
+
+    def arm(k):
+        source = down(map_ref[pl.ds(k * steps + step, 1), :].astype(jnp.float32))
+        index = lax.broadcasted_iota(jnp.int32, (lanes, lanes), 1).astype(jnp.float32)
+        pick = [jnp.where(source - c == index, 1.0, 0.0) for c in range(0, cols, lanes)]
+        pick = jnp.concatenate(pick, axis=1).astype(jnp.bfloat16)
+        return jnp.dot(pick, ft, preferred_element_type=jnp.float32)
+
+    first_arm, middle_arm, last_arm = (arm(k) for k in range(3))
     shear = 2.0 * middle_arm - first_arm - last_arm
+    angle = angle_ref[pl.ds(step, 1), :]
+    cosine, sine = jnp.cos(angle), jnp.sin(angle)
     cos_sq, sin_sq, mixed = (
-        jnp.broadcast_to(coef_ref[k][:, 0:1], (gauges, samples)) for k in range(3)
+        jnp.tile(down(c), (1, samples // lanes))
+        for c in (cosine * cosine, sine * sine, sine * cosine)
     )
     twist = shear * mixed
     along_x = first_arm * cos_sq + last_arm * sin_sq + twist
     along_y = first_arm * sin_sq + last_arm * cos_sq - twist
     shear_new = 2.0 * (last_arm - first_arm) * mixed + shear * (cos_sq - sin_sq)
     per_arm = rt_ref.shape[0] // 3
-    here = pl.multiple_of(step * gauges, gauges)
+    here = pl.multiple_of(step * lanes, lanes)
     for k, value in enumerate((along_x, along_y, shear_new)):
-        rt_ref[pl.ds(k * per_arm + here, gauges), :] = value.astype(jnp.bfloat16)
+        rt_ref[pl.ds(k * per_arm + here, lanes), :] = value.astype(jnp.bfloat16)
 
     @pl.when(step == pl.num_programs(0) - 1)
     def _():
@@ -118,9 +136,7 @@
         for j in range(0, nb, 2):
             cols = rt_ref[TILE * j : TILE * (j + 2), :]
             rows = rt_ref[0 : TILE * (j + 2), :]
-            part = lax.dot_general(
-                rows, cols, (((1,), (1,)), ((), ())), preferred_element_type=jnp.float32
-            )
+            part = dot_nt(rows, cols)
             for i in range(j + 2):
                 for jj in range(max(i, j), j + 2):
                     idx = block_index(nb, i, jj)
@@ -139,9 +155,8 @@
             copy.wait()
 
 
-def gram_chunk(core, pick, ft, coef, so_far):
-    per_arm, cols = pick.shape[1], pick.shape[2]
-    samples = ft.shape[1]
+def gram_chunk(core, arms, ft, angles, so_far):
+    cols, samples = ft.shape
     half = half_blocks(cols // TILE)
     shape = jax.ShapeDtypeStruct((half, TILE, TILE), jnp.float32)
     anywhere = pl.BlockSpec(memory_space=pl.ANY)
@@ -150,11 +165,11 @@
         out_shape=(shape, shape),
         grid_spec=pltpu.PrefetchScalarGridSpec(
             num_scalar_prefetch=1,
-            grid=(per_arm // TILE,),
+            grid=(angles.shape[0],),
             in_specs=[
-                pl.BlockSpec((3, TILE, cols), lambda g, core: (0, g, 0)),
+                pl.BlockSpec(arms.shape, lambda g, core: (0, 0)),
                 pl.BlockSpec((cols, samples), lambda g, core: (0, 0)),
-                pl.BlockSpec((3, TILE, TILE), lambda g, core: (0, g, 0)),
+                pl.BlockSpec(angles.shape, lambda g, core: (0, 0)),
             ]
             + ([] if so_far is None else [anywhere, anywhere]),
             out_specs=(anywhere, anywhere),
@@ -166,7 +181,7 @@
         ),
         compiler_params=pltpu.CompilerParams(vmem_limit_bytes=VMEM_BYTES),
         name="rotate_gram",
-    )(core, pick, ft, coef, *(() if so_far is None else so_far))
+    )(core, arms, ft, angles, *(() if so_far is None else so_far))
 
 
 def dot_tn(a, b):
@@ -210,14 +225,16 @@
     def row_of(x, j):
         return jnp.broadcast_to(x[j : j + 1, :], (8, TILE))
 
+    top = columns(work[0], 0)
     for s in range(strips):
         r0 = 8 * s
         last = s == strips - 1
         here = (lane >= r0) & (lane < r0 + 8)
-        top = columns(work[s], r0)
         cur = jnp.where(here, jnp.where(lane == r0 + sub, 1.0, 0.0), work[s])
         if not last:
             low = columns(work[s + 1], r0)
+            top2 = columns(work[s], r0 + 8)
+            low2 = columns(work[s + 1], r0 + 8)
             nxt = jnp.where(here, 0.0, work[s + 1])
         for j in range(8):
             inv = 1.0 / row_of(top[j], j)
@@ -231,6 +248,12 @@
                     top[k] = top[k] - m_top * c
                 if not last:
                     low[k] = low[k] - m_low * c
+            if not last:
+                for k in range(8):
+                    c = row_of(top2[k], j)
+                    if j < 7:
+                        top2[k] = top2[k] - m_top * c
+                    low2[k] = low2[k] - m_low * c
             row = row_of(cur, j)
             cur = cur - m_top * row
             if not last:
@@ -248,6 +271,7 @@
         e_ref[r0 : r0 + 8, :] = jnp.where(lane < r0 + 8, cur, 0.0)
         if not last:
             work[s + 1] = nxt
+            top = low2
         if s + 2 < strips:
             update = outer_product(later, cur)
             for t in range(s + 2, strips):
@@ -371,18 +395,14 @@
     parts = lax.axis_size(GAUGE_AXES)
     rows, cols_here = records.shape
     cols = column_map.shape[0]
-    per_arm = cols // 3
     core = lax.axis_index("core").astype(jnp.int32).reshape(1)
     records_t = records.T
-    arms = column_map.reshape(3, per_arm, 1)
-    pick = (arms == jnp.arange(cols, dtype=jnp.int32)[None, None, :]).astype(jnp.bfloat16)
-    cosine, sine = jnp.cos(angles), jnp.sin(angles)
-    coef = jnp.stack([cosine * cosine, sine * sine, sine * cosine])
-    coef = jnp.broadcast_to(coef[:, :, None], (3, per_arm, TILE))
+    arms = column_map.reshape(-1, TILE)
+    angles = angles.reshape(-1, TILE)
     acc = None
     for filtered in filter_records(records_t, offsets, parts):
         regrouped = lax.all_to_all(filtered, GAUGE_AXES, split_axis=0, concat_axis=0, tiled=True)
-        acc = gram_chunk(core, pick, regrouped.reshape(cols, -1), coef, acc)
+        acc = gram_chunk(core, arms, regrouped.reshape(cols, -1), angles, acc)
     mine, other = acc
     half = mine.shape[0]
     mine = mine + swap_cores(other)

time: 277 us -> 265 us (0.957)
  Pallas kernels: 104 us -> 95.4 us
  other arithmetic: 5.42 us -> 2.39 us
    pallas_call x1, Pallas kernels: 64.8 us -> 58.2 us  [cholesky_blocks(): pl.pallas_call(functools.partial(cholesky_kernel, scale), out_shape=jax.S...]
    convert_element_type x1 -> x0, other arithmetic: 3.01 us -> none  [shards(): (arms == jnp.arange(cols, dtype=jnp.int32)[None, None, :]).astype(jnp.bfl...]
  transfers between devices with their start and end apart: 3 -> 3, of which waited for: 2 -> 3; matrix products, arithmetic and copies ran while one was open for 2% -> 0% of each run, Pallas kernels for 7% -> 7%
where the time goes in v3:
time: 265 us
  blocking collectives  144 us (54%)
  Pallas kernels  95.4 us (36%)
  waiting for transfers between devices  11.6 us (4%)
  starting transfers between devices  8.59 us (3%)
  local copies, waits for them, and re-layouts  2.92 us (1%)
    all_to_all x1, blocking collectives, shards(): lax.all_to_all(filtered, GAUGE_AXES, split_axis=0, concat_axis=0, tiled=T...  61.1 us
    pallas_call x1, Pallas kernels, cholesky_blocks(): pl.pallas_call(functools.partial(cholesky_kernel, scale), out_shape=jax.S...  58.2 us
    all_to_all x1, blocking collectives, shards(): lax.all_to_all(mine.reshape(plane, share, TILE), PLANE_AXES, split_axis=0...  43.6 us
    all_to_all x1, blocking collectives, gather_plane(): lax.all_to_all(copies, PLANE_AXES, split_axis=0, concat_axis=0, tiled=True)  39 us
    pallas_call x2, Pallas kernels, gram_chunk(): pl.pallas_call(functools.partial(gram_kernel, so_far is None), out_shape=...  27.6 us
    pallas_call x1, Pallas kernels, filter_records(): pl.pallas_call(functools.partial(filter_kernel, each // BLOCK), out_shape...  9.63 us
    ppermute x2, waiting for transfers between devices, swap_cores(): return lax.ppermute(x, 'core', [(0, 1), (1, 0)])  9.28 us
  transfers between devices with their start and end apart: 3, of which 3 were waited for; matrix products, arithmetic and copies ran while one was open for 0% of the time, Pallas kernels for 7%

profile of v3, /device:TPU:1, one launch (start us, length us, event | category | flops | bytes accessed | tf_op | source)
XLA Modules:
  0.0 264.8 jit_solution(14549782306646550276)
XLA Ops:
  0.0 9.6 %drift_filter.1 = (bf16[8,192,1536]{2,1,0:T(8,128)(2,1)}, bf16[8,192,512]{2,1,0:T(8,128)(2,1)}) custom-call(s32[16]{0:T(128)} %offsets.1, bf16[192,16384]{1,0:T(8,128)(2,1)} %bitcast.12), custom_call_target="tpu_custom_call" | custom-call | tf_op jit(solution)/shard_map/drift_filter/pallas_call | solution.py:58
  9.6 61.1 %all_to_all.20 = bf16[8,192,1536]{2,1,0:T(8,128)(2,1)} all-to-all(bf16[8,192,1536]{2,1,0:T(8,128)(2,1)} %get-tuple-element.12), channel_id=1, replica_groups=mesh['z'=4,'x'=4,'y'=4,'core'=2] {'y','core'}, dimensions={0} | all-to-all | bytes 9437184 | tf_op jit(solution)/shard_map/all_to_all | solution.py:404
  70.7 4.5 %all-to-all-start = ((bf16[8,192,512]{2,1,0:T(8,128)(2,1)}), bf16[8,192,512]{2,1,0:T(8,128)(2,1)S(1)}, u32[]{:S(2)}, u32[]{:S(2)}) async-start(bf16[8,192,512]{2,1,0:T(8,128)(2,1)} %get-tuple-element.11), calls=%async_computation | async-start | bytes 3145728 | tf_op jit(solution)/shard_map/all_to_all | solution.py:404
  75.2 18.4 %rotate_gram.2 = (f32[40,128,128]{2,1,0:T(8,128)}, f32[40,128,128]{2,1,0:T(8,128)}) custom-call(s32[1]{0:T(128)} %bitcast.core, s32[12,128]{1,0:T(8,128)} %bitcast.14, bf16[1536,1536]{1,0:T(8,128)(2,1)} %bitcast.8, f32[4,128]{1,0:T(4,128)} %bitcast.16), custom_call_target="tpu_custom_call" | custom-call | tf_op jit(solution)/shard_map/rotate_gram/pallas_call | solution.py:163
  93.7 2.3 all-to-all-done
  96.0 0.0 copy-start.1
  96.0 1.2 copy-done.1
  97.2 9.1 %rotate_gram.3 = (f32[40,128,128]{2,1,0:T(8,128)}, f32[40,128,128]{2,1,0:T(8,128)}) custom-call(s32[1]{0:T(128)} %bitcast.core, s32[12,128]{1,0:T(8,128)} %bitcast.15, bf16[1536,512]{1,0:T(8,128)(2,1)} %bitcast.13, f32[4,128]{1,0:T(4,128)} %bitcast.17, f32[40,128,128]{2,1,0:T(8,128)} %get-tuple-element.13.refs_3_, f32[40,128,128]{2,1,0:T(8,128)} %get-tuple-element.14.refs_4_), custom_call_target="tpu_custom_call" | custom-call | tf_op jit(solution)/shard_map/rotate_gram/pallas_call | solution.py:163
  106.3 1.0 collective-permute-start
  107.3 4.7 %collective-permute-done = f32[40,128,128]{2,1,0:T(8,128)S(1)} collective-permute-done((f32[40,128,128]{2,1,0:T(8,128)}, f32[40,128,128]{2,1,0:T(8,128)S(1)}, u32[]{:S(2)}, u32[]{:S(2)}) %collective-permute-start) | collective-permute-done | bytes 2621472 | tf_op jit(solution)/shard_map/ppermute | solution.py:385
  112.0 2.2 add.3
  114.3 43.6 %all_to_all.21 = f32[64,80,128]{2,1,0:T(8,128)S(1)} all-to-all(f32[64,80,128]{2,1,0:T(8,128)S(1)} %bitcast.11), channel_id=1, replica_groups=mesh['z'=4,'x'=4,'y'=4,'core'=2] {'z','x','y'}, dimensions={0} | all-to-all | bytes 5242880 | tf_op jit(solution)/shard_map/all_to_all | solution.py:411
  157.9 0.2 reduce_sum.9
  158.0 0.2 broadcast_in_dim.2
  158.2 39.0 %all_to_all.22 = f32[64,80,128]{2,1,0:T(8,128)S(1)} all-to-all(f32[64,80,128]{2,1,0:T(8,128)S(1)} %broadcast_in_dim.2), channel_id=1, replica_groups=mesh['z'=4,'x'=4,'y'=4,'core'=2] {'z','x','y'}, dimensions={0} | all-to-all | bytes 5242880 | tf_op jit(solution)/shard_map/all_to_all | solution.py:391
  197.2 0.0 copy-start
  197.2 3.1 %collective-permute-start.1 = (f32[40,128,128]{2,1,0:T(8,128)S(1)}, f32[40,128,128]{2,1,0:T(8,128)S(1)}, u32[]{:S(2)}, u32[]{:S(2)}) collective-permute-start(f32[40,128,128]{2,1,0:T(8,128)S(1)} %bitcast.9), channel_id=1, source_target_pairs={{0,1},{1,0},{2,3},{3,2},{4,5},{5,4},{6,7},{7,6},{8,9},{9,8},{10,11... | collective-permute-start | bytes 7864328 | tf_op jit(solution)/shard_map/ppermute | solution.py:385
  200.4 4.5 %collective-permute-done.1.other_ref = f32[40,128,128]{2,1,0:T(8,128)S(1)} collective-permute-done((f32[40,128,128]{2,1,0:T(8,128)S(1)}, f32[40,128,128]{2,1,0:T(8,128)S(1)}, u32[]{:S(2)}, u32[]{:S(2)}) %collective-permute-start.1) | collective-permute-done | bytes 2621472 | tf_op jit(solution)/shard_map/ppermute | solution.py:385
  204.9 0.0 copy-done
  204.9 0.0 copy-start.2
  204.9 1.5 copy-done.2
  206.4 58.2 %cholesky.1 = f32[1536,1536]{1,0:T(8,128)} custom-call(s32[1]{0:T(128)} %bitcast.core, f32[40,128,128]{2,1,0:T(8,128)} %bitcast.10, f32[40,128,128]{2,1,0:T(8,128)} %copy-done.2), custom_call_target="tpu_custom_call" | custom-call | tf_op jit(solution)/shard_map/cholesky/pallas_call | solution.py:361
Async XLA Ops:
  70.7 25.3 %all-to-all-start = ((bf16[8,192,512]{2,1,0:T(8,128)(2,1)}), bf16[8,192,512]{2,1,0:T(8,128)(2,1)S(1)}, u32[]{:S(2)}, u32[]{:S(2)}) async-start(bf16[8,192,512]{2,1,0:T(8,128)(2,1)} %get-tuple-element.11), calls=%async_computation | async-start | bytes 3145728 | tf_op jit(solution)/shard_map/all_to_all | solution.py:404
  96.0 1.2 copy-start.1
  106.3 5.7 %collective-permute-start = (f32[40,128,128]{2,1,0:T(8,128)}, f32[40,128,128]{2,1,0:T(8,128)S(1)}, u32[]{:S(2)}, u32[]{:S(2)}) collective-permute-start(f32[40,128,128]{2,1,0:T(8,128)} %get-tuple-element.16), channel_id=1, source_target_pairs={{0,1},{1,0},{2,3},{3,2},{4,5},{5,4},{6,7},{7,6},{8,9},{9,8},{10,11... | collective-permute-start | bytes 7864328 | tf_op jit(solution)/shard_map/ppermute | solution.py:385
  197.2 7.7 %copy-start = (f32[64,80,128]{2,1,0:T(8,128)}, f32[64,80,128]{2,1,0:T(8,128)S(1)}, u32[]{:S(2)}) copy-start(f32[64,80,128]{2,1,0:T(8,128)S(1)} %all_to_all.22) | copy-start | bytes 7864324
  197.2 7.6 %collective-permute-start.1 = (f32[40,128,128]{2,1,0:T(8,128)S(1)}, f32[40,128,128]{2,1,0:T(8,128)S(1)}, u32[]{:S(2)}, u32[]{:S(2)}) collective-permute-start(f32[40,128,128]{2,1,0:T(8,128)S(1)} %bitcast.9), channel_id=1, source_target_pairs={{0,1},{1,0},{2,3},{3,2},{4,5},{5,4},{6,7},{7,6},{8,9},{9,8},{10,11... | collective-permute-start | bytes 7864328 | tf_op jit(solution)/shard_map/ppermute | solution.py:385
  204.9 1.5 copy-start.2

commit v4 on v3

v4 whole, which is shorter than its diff:
```python
import functools

import jax
import jax.numpy as jnp
from jax import lax
from jax.experimental import pallas as pl
from jax.experimental.pallas import tpu as pltpu
from jax.sharding import Mesh
from jax.sharding import PartitionSpec as P

BLOCK = 1024
BAND = 64
TILE = 128
CORES = 2
SAMPLE_AXES = ("z", "x")
GAUGE_AXES = ("y", "core")
PLANE_AXES = ("z", "x", "y")
HIGHEST = lax.Precision.HIGHEST
VMEM_BYTES = 56 * 1024 * 1024


def block_index(nb, i, j):
    return sum(nb - k for k in range(i)) + (j - i)


class Layout:
    def __init__(self, nb, plane):
        self.nb, self.plane = nb, plane
        self.used = nb * (nb + 1) // 2
        self.rows_early = nb // 3
        need = block_index(nb, self.rows_early, self.rows_early)
        step = max(1, 8 * plane // TILE)
        self.early = -(-(-(-need // CORES)) // step) * step
        self.half = -(-(-(-self.used // CORES)) // step) * step
        self.share = (self.early * TILE // plane, (self.half - self.early) * TILE // plane)

    def pieces(self, position):
        late = position >= self.early
        share = self.share[late]
        base = self.share[0] if late else 0
        row = (position - (self.early if late else 0)) * TILE
        at, out = 0, []
        while at < TILE:
            chip, inside = divmod(row + at, share)
            n = min(share - inside, TILE - at)
            out.append((at, chip, base + inside, n))
            at += n
        return out


def dot_nt(a, b):
    return lax.dot_general(a, b, (((1,), (1,)), ((), ())), preferred_element_type=jnp.float32)


def filter_kernel(offsets, x_ref, head_ref, tail_ref):
    parts, _, split = head_ref.shape
    blocks = x_ref.shape[1] // BLOCK // parts
    for b in range(parts * blocks):
        start = offsets[pl.program_id(0) * parts * blocks + b]
        x = x_ref[:, b * BLOCK : (b + 1) * BLOCK]
        sample = lax.broadcasted_iota(jnp.int32, (1, BLOCK), 1)
        inside = jnp.where((sample >= start) & (sample < start + BAND), 1.0, 0.0)
        mask = jnp.broadcast_to(inside.astype(jnp.bfloat16), (TILE, BLOCK))
        baseline = dot_nt(x, mask) * (1.0 / BAND)
        for t in range(0, BLOCK, TILE):
            value = (x[:, t : t + TILE].astype(jnp.float32) - baseline).astype(jnp.bfloat16)
            here = b % blocks * BLOCK + t
            if here < split:
                head_ref[b // blocks, :, here : here + TILE] = value
            else:
                tail_ref[b // blocks, :, here - split : here - split + TILE] = value


def filter_records(records_t, offsets, parts):
    rows, samples = records_t.shape
    each = samples // parts
    tail = BLOCK // 2
    widths = (each - tail, tail)
    per = 2
    return pl.pallas_call(
        filter_kernel,
        out_shape=tuple(jax.ShapeDtypeStruct((parts, rows, w), jnp.bfloat16) for w in widths),
        grid_spec=pltpu.PrefetchScalarGridSpec(
            num_scalar_prefetch=1,
            grid=(parts // per,),
            in_specs=[pl.BlockSpec((rows, per * each), lambda d, off: (0, d))],
            out_specs=tuple(
                pl.BlockSpec((per, rows, w), lambda d, off: (d, 0, 0)) for w in widths
            ),
        ),
        compiler_params=pltpu.CompilerParams(vmem_limit_bytes=VMEM_BYTES),
        name="drift_filter",
    )(offsets, records_t)


def gram_kernel(layout, first, core, *refs):
    if first:
        map_ref, ft_ref, angle_ref, mine_out, other_out, rt_ref, acc_ref, sem = refs
        mine_in = other_in = None
    else:
        map_ref, ft_ref, angle_ref, mine_in, other_in, mine_out, other_out, rt_ref, acc_ref, sem = refs
    step = pl.program_id(0)
    me = core[0]

    def loads():
        return (
            pltpu.make_async_copy(mine_in, acc_ref.at[me], sem.at[0]),
            pltpu.make_async_copy(other_in, acc_ref.at[1 - me], sem.at[1]),
        )

    if not first:

        @pl.when(step == 0)
        def _():
            for copy in loads():
                copy.start()

    ft = ft_ref[...]
    cols, samples = ft.shape
    lanes = map_ref.shape[1]
    steps = pl.num_programs(0)

    def down(row):
        return jnp.broadcast_to(row, (lanes, lanes)).T

    def arm(k):
        source = down(map_ref[pl.ds(k * steps + step, 1), :].astype(jnp.float32))
        index = lax.broadcasted_iota(jnp.int32, (lanes, lanes), 1).astype(jnp.float32)
        pick = [jnp.where(source - c == index, 1.0, 0.0) for c in range(0, cols, lanes)]
        pick = jnp.concatenate(pick, axis=1).astype(jnp.bfloat16)
        return jnp.dot(pick, ft, preferred_element_type=jnp.float32)

    first_arm, middle_arm, last_arm = (arm(k) for k in range(3))
    shear = 2.0 * middle_arm - first_arm - last_arm
    angle = angle_ref[pl.ds(step, 1), :]
    cosine, sine = jnp.cos(angle), jnp.sin(angle)
    cos_sq, sin_sq, mixed = (
        jnp.tile(down(c), (1, samples // lanes))
        for c in (cosine * cosine, sine * sine, sine * cosine)
    )
    twist = shear * mixed
    along_x = first_arm * cos_sq + last_arm * sin_sq + twist
    along_y = first_arm * sin_sq + last_arm * cos_sq - twist
    shear_new = 2.0 * (last_arm - first_arm) * mixed + shear * (cos_sq - sin_sq)
    per_arm = rt_ref.shape[0] // 3
    here = pl.multiple_of(step * lanes, lanes)
    for k, value in enumerate((along_x, along_y, shear_new)):
        rt_ref[pl.ds(k * per_arm + here, lanes), :] = value.astype(jnp.bfloat16)

    @pl.when(step == pl.num_programs(0) - 1)
    def _():
        if not first:
            for copy in loads():
                copy.wait()
        nb = layout.nb

        def add(idx, block):
            for at, chip, row, n in layout.pieces(idx // CORES):
                here = (idx % CORES, chip, slice(row, row + n))
                if first:
                    acc_ref[here] = block[at : at + n]
                else:
                    acc_ref[here] += block[at : at + n]

        if first:
            for idx in range(layout.used, CORES * layout.half):
                add(idx, jnp.zeros((TILE, TILE), jnp.float32))
        for j in range(0, nb, 2):
            part = dot_nt(rt_ref[0 : TILE * (j + 2), :], rt_ref[TILE * j : TILE * (j + 2), :])
            for i in range(j + 2):
                for jj in range(max(i, j), j + 2):
                    cut = slice(TILE * (jj - j), TILE * (jj - j + 1))
                    add(block_index(nb, i, jj), part[TILE * i : TILE * (i + 1), cut])
        stores = (
            pltpu.make_async_copy(acc_ref.at[me], mine_out, sem.at[0]),
            pltpu.make_async_copy(acc_ref.at[1 - me], other_out, sem.at[1]),
        )
        for copy in stores:
            copy.start()
        for copy in stores:
            copy.wait()


def gram_chunk(layout, core, arms, ft, angles, so_far):
    cols, samples = ft.shape
    run = (layout.plane, sum(layout.share), TILE)
    shape = jax.ShapeDtypeStruct(run, jnp.float32)
    anywhere = pl.BlockSpec(memory_space=pl.ANY)
    return pl.pallas_call(
        functools.partial(gram_kernel, layout, so_far is None),
        out_shape=(shape, shape),
        grid_spec=pltpu.PrefetchScalarGridSpec(
            num_scalar_prefetch=1,
            grid=(angles.shape[0],),
            in_specs=[
                pl.BlockSpec(arms.shape, lambda g, core: (0, 0)),
                pl.BlockSpec((cols, samples), lambda g, core: (0, 0)),
                pl.BlockSpec(angles.shape, lambda g, core: (0, 0)),
            ]
            + ([] if so_far is None else [anywhere, anywhere]),
            out_specs=(anywhere, anywhere),
            scratch_shapes=[
                pltpu.VMEM((cols, samples), jnp.bfloat16),
                pltpu.VMEM((CORES, *run), jnp.float32),
                pltpu.SemaphoreType.DMA((2,)),
            ],
        ),
        compiler_params=pltpu.CompilerParams(vmem_limit_bytes=VMEM_BYTES),
        name="rotate_gram",
    )(core, arms, ft, angles, *(() if so_far is None else so_far))


def split3(x):
    high = x.astype(jnp.bfloat16).astype(jnp.float32)
    rest = x - high
    middle = rest.astype(jnp.bfloat16).astype(jnp.float32)
    return high, middle, rest - middle


def outer_product(a, b):
    a1, a2, a3 = split3(a)
    b1, b2, b3 = split3(b)
    left = jnp.concatenate([a1, a1, a2, a2, a1, a3], axis=0).astype(jnp.bfloat16)
    right = jnp.concatenate([b1, b2, b1, b2, b3, b1], axis=0).astype(jnp.bfloat16)
    return lax.dot_general(
        left, right, (((0,), (0,)), ((), ())), preferred_element_type=jnp.float32
    )


def factor_block(a_ref, e_ref):
    lane = lax.broadcasted_iota(jnp.int32, (8, TILE), 1)
    sub = lax.broadcasted_iota(jnp.int32, (8, TILE), 0)
    strips = TILE // 8
    work = [a_ref[8 * t : 8 * t + 8, :] for t in range(strips)]

    def columns(x, r0):
        return [jnp.broadcast_to(x[:, r0 + j : r0 + j + 1], (8, TILE)) for j in range(8)]

    def row_of(x, j):
        return jnp.broadcast_to(x[j : j + 1, :], (8, TILE))

    top = columns(work[0], 0)
    for s in range(strips):
        r0 = 8 * s
        below = strips - 1 - s
        here = (lane >= r0) & (lane < r0 + 8)
        cur = jnp.where(here, jnp.where(lane == r0 + sub, 1.0, 0.0), work[s])
        if below:
            low = columns(work[s + 1], r0)
            top2 = columns(work[s], r0 + 8)
            low2 = columns(work[s + 1], r0 + 8)
            nxt = jnp.where(here, 0.0, work[s + 1])
        if below > 1:
            third = columns(work[s + 2], r0)
            nxt2 = jnp.where(here, 0.0, work[s + 2])
        for j in range(8):
            inv = 1.0 / row_of(top[j], j)
            m_top = jnp.where(sub > j, top[j] * inv, 0.0)
            m_low = low[j] * inv if below else None
            m_third = third[j] * inv if below > 1 else None
            for k in range(j + 1, 8):
                c = row_of(top[k], j)
                if k == j + 1:
                    top[k] = top[k] - jnp.where(sub > j, top[j] * c, 0.0) * inv
                else:
                    top[k] = top[k] - m_top * c
                if below:
                    low[k] = low[k] - m_low * c
                if below > 1:
                    third[k] = third[k] - m_third * c
            if below:
                for k in range(8):
                    c = row_of(top2[k], j)
                    if j < 7:
                        top2[k] = top2[k] - m_top * c
                    low2[k] = low2[k] - m_low * c
            row = row_of(cur, j)
            cur = cur - m_top * row
            if below:
                nxt = nxt - m_low * row
            if below > 1:
                nxt2 = nxt2 - m_third * row
        pivot = top[0]
        for j in range(1, 8):
            pivot = jnp.where(sub == j, top[j], pivot)
        scale = lax.rsqrt(pivot)
        cur = cur * scale
        later = jnp.where(lane >= r0 + 8, cur, 0.0)
        out = later
        for k in range(8):
            out = jnp.where((lane == r0 + k) & (sub <= k), top[k] * scale, out)
        a_ref[r0 : r0 + 8, :] = out
        e_ref[r0 : r0 + 8, :] = jnp.where(lane < r0 + 8, cur, 0.0)
        if below:
            work[s + 1] = nxt
            top = low2
        if below > 1:
            work[s + 2] = nxt2
        if below > 2:
            update = outer_product(later, cur)
            for t in range(s + 3, strips):
                work[t] = jnp.where(here, 0.0, work[t]) - update[8 * t : 8 * t + 8, :]


def dot_parts(a, b, contract):
    return lax.dot_general(
        a, b, (((contract,), (0,)), ((), ())), preferred_element_type=jnp.float32
    )


def product(left, right, contract):
    m = left[0].shape[1 - contract]
    p = dot_parts(jnp.concatenate(left, axis=1 - contract), right[0], contract)
    q = dot_parts(jnp.concatenate(left[:2], axis=1 - contract), right[1], contract)
    r = dot_parts(left[0], right[2], contract)
    return p[:m] + ((p[m : 2 * m] + q[:m]) + ((p[2 * m :] + q[m:]) + r))


def parts3(x):
    return [v.astype(jnp.bfloat16) for v in split3(x)]


def cholesky_kernel(layout, scale, begin, end, core, *refs):
    sources = refs[: 2 if begin == 0 else 5]
    out_ref, u_ref, g_ref, a_ref, e_ref, s_ref, p_ref, in_sem, out_sem = refs[len(sources) :]
    me = core[0]
    size = u_ref.shape[0]
    nb, early = layout.nb, layout.early
    below = slice(0, TILE * begin)

    def part_loads(pair, lo, hi, to, sems):
        mine, other = pair
        n = hi - lo
        return [
            pltpu.make_async_copy(mine.at[lo:hi], g_ref.at[me, to : to + n], in_sem.at[sems]),
            pltpu.make_async_copy(
                other.at[lo:hi], g_ref.at[1 - me, to : to + n], in_sem.at[sems + 1]
            ),
        ]

    if begin == 0:
        first = block_index(nb, 2, 2) // CORES + 1
        now = part_loads(sources[:2], 0, first, 0, 0)
        later = part_loads(sources[:2], first, early, first, 2)
    else:
        first = block_index(nb, begin, begin) // CORES
        now = part_loads(sources[:2], first, early, first, 0)
        now += part_loads(sources[2:4], 0, layout.half - early, early, 2)
        now.append(pltpu.make_async_copy(sources[4].at[below], u_ref.at[below], in_sem.at[4]))
        later = []

    def store(k):
        rows = slice(TILE * k, TILE * (k + 1))
        return pltpu.make_async_copy(u_ref.at[rows], out_ref.at[rows], out_sem.at[k])

    for copy in now + later:
        copy.start()
    for copy in now:
        copy.wait()
    if begin:
        rest = slice(TILE * begin, size)
        for q, v in enumerate(parts3(u_ref[below, rest])):
            p_ref[q, below, rest] = v

    def up(rows, cols):
        return [p_ref[q, rows, cols] for q in range(3)]

    def body(i, carry):
        for k in range(begin, end):
            h = k % 2
            r0 = TILE * (k - h)
            c0 = TILE * k

            @pl.when(i == k)
            def _(k=k, h=h, r0=r0, c0=c0):
                if k == 2:
                    for copy in later:
                        copy.wait()
                if h == 0:
                    for hh in range(2):
                        for j in range(k, nb):
                            if j < k + hh:
                                block = jnp.zeros((TILE, TILE), jnp.float32)
                            else:
                                idx = block_index(nb, k + hh, j)
                                block = g_ref[idx % CORES, idx // CORES] * scale
                            s_ref[TILE * hh : TILE * (hh + 1), TILE * j : TILE * (j + 1)] = block
                    if r0:
                        panel = slice(r0, r0 + 2 * TILE)
                        s_ref[:, r0:] -= product(
                            up(slice(0, r0), panel), up(slice(0, r0), slice(r0, size)), 0
                        )
                else:
                    above = slice(r0, c0)
                    s_ref[TILE:, c0:] -= product(
                        up(above, slice(c0, c0 + TILE)), up(above, slice(c0, size)), 0
                    )
                a_ref[...] = s_ref[TILE * h : TILE * (h + 1), c0 : c0 + TILE]

        factor_block(a_ref, e_ref)
        for k in range(begin, end):
            h = k % 2
            c0 = TILE * k

            @pl.when(i == k)
            def _(k=k, h=h, c0=c0):
                rows = slice(c0, c0 + TILE)
                if c0:
                    u_ref[rows, 0:c0] = jnp.zeros((TILE, c0), jnp.float32)
                u_ref[rows, c0 : c0 + TILE] = a_ref[...]
                if c0 + TILE < size:
                    rest = slice(c0 + TILE, size)
                    solved = product(
                        parts3(e_ref[...]), parts3(s_ref[TILE * h : TILE * (h + 1), rest]), 1
                    )
                    u_ref[rows, rest] = solved
                    for q, v in enumerate(parts3(solved)):
                        p_ref[q, rows, rest] = v
                store(k).start()

        return carry

    lax.fori_loop(begin, end, body, 0)
    for k in range(begin, end):
        store(k).wait()


def cholesky_rows(layout, core, groups, so_far, scale):
    size = layout.nb * TILE
    begin, end = (0, layout.rows_early) if so_far is None else (layout.rows_early, layout.nb)
    anywhere = pl.BlockSpec(memory_space=pl.ANY)
    sources = [x for pair in groups for x in pair] + ([] if so_far is None else [so_far])
    return pl.pallas_call(
        functools.partial(cholesky_kernel, layout, scale, begin, end),
        out_shape=jax.ShapeDtypeStruct((size, size), jnp.float32),
        grid_spec=pltpu.PrefetchScalarGridSpec(
            num_scalar_prefetch=1,
            grid=(1,),
            in_specs=[anywhere] * len(sources),
            out_specs=anywhere,
            scratch_shapes=[
                pltpu.VMEM((size, size), jnp.float32),
                pltpu.VMEM((CORES, layout.half, TILE, TILE), jnp.float32),
                pltpu.VMEM((TILE, TILE), jnp.float32),
                pltpu.VMEM((TILE, TILE), jnp.float32),
                pltpu.VMEM((2 * TILE, size), jnp.float32),
                pltpu.VMEM((3, size, size), jnp.bfloat16),
                pltpu.SemaphoreType.DMA((5,)),
                pltpu.SemaphoreType.DMA((layout.nb,)),
            ],
        ),
        input_output_aliases={} if so_far is None else {len(sources): 0},
        cost_estimate=pl.CostEstimate(
            flops=40 * (end - begin) * size**2 * TILE, transcendentals=0, bytes_accessed=12 * size**2
        ),
        compiler_params=pltpu.CompilerParams(vmem_limit_bytes=VMEM_BYTES),
        name="cholesky",
    )(core, *sources)


def swap_cores(x):
    return lax.ppermute(x, "core", [(0, 1), (1, 0)])


def gather_plane(x):
    plane = lax.axis_size(PLANE_AXES)
    copies = jnp.broadcast_to(x[None], (plane, *x.shape))
    return lax.all_to_all(copies, PLANE_AXES, split_axis=0, concat_axis=0, tiled=True)


def shards(records, offsets, column_map, angles):
    parts = lax.axis_size(GAUGE_AXES)
    rows, cols_here = records.shape
    cols = column_map.shape[0]
    core = lax.axis_index("core").astype(jnp.int32).reshape(1)
    records_t = records.T
    arms = column_map.reshape(-1, TILE)
    angles = angles.reshape(-1, TILE)
    layout = Layout(cols // TILE, lax.axis_size(PLANE_AXES))
    acc = None
    for filtered in filter_records(records_t, offsets, parts):
        regrouped = lax.all_to_all(filtered, GAUGE_AXES, split_axis=0, concat_axis=0, tiled=True)
        acc = gram_chunk(layout, core, arms, regrouped.reshape(cols, -1), angles, acc)
    mine, other = acc
    mine = mine + swap_cores(other)
    spread = lax.all_to_all(mine, PLANE_AXES, split_axis=0, concat_axis=0, tiled=True).sum(0)
    scale = 1.0 / (rows * lax.axis_size(SAMPLE_AXES))
    early, late = jnp.split(spread, [layout.share[0]])
    early = gather_plane(early)
    late, early = lax.optimization_barrier((late, early))
    late = gather_plane(late)
    early, late = (g.reshape(-1, TILE, TILE) for g in (early, late))
    groups = [(early, swap_cores(early))]
    upper = cholesky_rows(layout, core, groups, None, scale)
    late, upper = lax.optimization_barrier((late, upper))
    groups.append((late, swap_cores(late)))
    return cholesky_rows(layout, core, groups, upper, scale)


def solution(mesh):
    devices = mesh.devices
    tm, gauge = devices.shape
    side = int(round(tm**0.5))
    fine = Mesh(
        devices.reshape(side, tm // side, gauge // CORES, CORES), SAMPLE_AXES + GAUGE_AXES
    )
    placed = (P(SAMPLE_AXES, GAUGE_AXES), P(SAMPLE_AXES), P(), P())
    return jax.shard_map(shards, mesh=fine, in_specs=placed, out_specs=P(), check_vma=False)
```

time: 265 us -> 259 us (0.977)
  blocking collectives: 144 us -> 105 us
  waiting for transfers between devices: 11.6 us -> 31.1 us
  starting transfers between devices: 8.59 us -> 20.1 us
    all_to_all x2 -> x1, blocking collectives: 82.6 us -> 43.6 us  [shards(): lax.all_to_all(mine, PLANE_AXES, split_axis=0, concat_axis=0, tiled=True)]
    all_to_all x0 -> x2, waiting for transfers between devices: none -> 21.7 us  [gather_plane(): lax.all_to_all(copies, PLANE_AXES, split_axis=0, concat_axis=0, tiled=True)]
    all_to_all x0 -> x2, starting transfers between devices: none -> 10.6 us  [gather_plane(): lax.all_to_all(copies, PLANE_AXES, split_axis=0, concat_axis=0, tiled=True)]
    ppermute x2 -> x3, waiting for transfers between devices: 9.28 us -> 7.05 us  [swap_cores(): return lax.ppermute(x, 'core', [(0, 1), (1, 0)])]
    pallas_call x4 -> x5, Pallas kernels: 95.4 us -> 95.5 us  [the longest x2 59.8 us: cholesky_rows(): pl.pallas_call(functools.partial(cholesky_kernel, layout, scale, begin, e...]
  transfers between devices with their start and end apart: 3 -> 6, of which waited for: 3 -> 4; matrix products, arithmetic and copies ran while one was open for 0% -> 0% of each run, Pallas kernels for 7% -> 15%
where the time goes in v4:
time: 259 us
  blocking collectives  105 us (41%)
  Pallas kernels  95.5 us (37%)
  waiting for transfers between devices  31.1 us (12%)
  starting transfers between devices  20.1 us (8%)
  local copies, waits for them, and re-layouts  4.59 us (2%)
    all_to_all x1, blocking collectives, shards(): lax.all_to_all(filtered, GAUGE_AXES, split_axis=0, concat_axis=0, tiled=T...  61.1 us
    pallas_call x2, Pallas kernels, cholesky_rows(): pl.pallas_call(functools.partial(cholesky_kernel, layout, scale, begin, e...  59.8 us
    all_to_all x1, blocking collectives, shards(): lax.all_to_all(mine, PLANE_AXES, split_axis=0, concat_axis=0, tiled=True)  43.6 us
    pallas_call x2, Pallas kernels, gram_chunk(): pl.pallas_call(functools.partial(gram_kernel, layout, so_far is None), ou...  27.6 us
    all_to_all x2, waiting for transfers between devices, gather_plane(): lax.all_to_all(copies, PLANE_AXES, split_axis=0, concat_axis=0, tiled=True)  21.7 us
    all_to_all x2, starting transfers between devices, gather_plane(): lax.all_to_all(copies, PLANE_AXES, split_axis=0, concat_axis=0, tiled=True)  10.6 us
    pallas_call x1, Pallas kernels, filter_records(): pl.pallas_call(filter_kernel, out_shape=tuple((jax.ShapeDtypeStruct((part...  8.18 us
    ppermute x3, waiting for transfers between devices, swap_cores(): return lax.ppermute(x, 'core', [(0, 1), (1, 0)])  7.05 us
  transfers between devices with their start and end apart: 6, of which 4 were waited for; matrix products, arithmetic and copies ran while one was open for 0% of the time, Pallas kernels for 15%

profile of v4, /device:TPU:1, one launch (start us, length us, event | category | flops | bytes accessed | tf_op | source)
XLA Modules:
  0.0 258.5 jit_solution(7490367779748070027)
XLA Ops:
  0.0 8.2 %drift_filter.1 = (bf16[8,192,1536]{2,1,0:T(8,128)(2,1)}, bf16[8,192,512]{2,1,0:T(8,128)(2,1)}) custom-call(s32[16]{0:T(128)} %offsets.1, bf16[192,16384]{1,0:T(8,128)(2,1)} %bitcast.9), custom_call_target="tpu_custom_call" | custom-call | tf_op jit(solution)/shard_map/drift_filter/pallas_call | solution.py:80
  8.2 61.1 %all_to_all.25 = bf16[8,192,1536]{2,1,0:T(8,128)(2,1)} all-to-all(bf16[8,192,1536]{2,1,0:T(8,128)(2,1)} %get-tuple-element.16), channel_id=1, replica_groups=mesh['z'=4,'x'=4,'y'=4,'core'=2] {'y','core'}, dimensions={0} | all-to-all | bytes 9437184 | tf_op jit(solution)/shard_map/all_to_all | solution.py:482
  69.3 4.5 %all-to-all-start = ((bf16[8,192,512]{2,1,0:T(8,128)(2,1)}), bf16[8,192,512]{2,1,0:T(8,128)(2,1)S(1)}, u32[]{:S(2)}, u32[]{:S(2)}) async-start(bf16[8,192,512]{2,1,0:T(8,128)(2,1)} %get-tuple-element.15), calls=%async_computation | async-start | bytes 3145728 | tf_op jit(solution)/shard_map/all_to_all | solution.py:482
  73.8 18.4 %rotate_gram.2 = (f32[64,80,128]{2,1,0:T(8,128)}, f32[64,80,128]{2,1,0:T(8,128)}) custom-call(s32[1]{0:T(128)} %bitcast.core, s32[12,128]{1,0:T(8,128)} %bitcast.16, bf16[1536,1536]{1,0:T(8,128)(2,1)} %bitcast.8, f32[4,128]{1,0:T(4,128)} %bitcast.18), custom_call_target="tpu_custom_call" | custom-call | tf_op jit(solution)/shard_map/rotate_gram/pallas_call | solution.py:189
  92.2 2.3 all-to-all-done
  94.5 0.0 copy-start
  94.5 1.2 copy-done
  95.8 9.1 %rotate_gram.3 = (f32[64,80,128]{2,1,0:T(8,128)}, f32[64,80,128]{2,1,0:T(8,128)}) custom-call(s32[1]{0:T(128)} %bitcast.core, s32[12,128]{1,0:T(8,128)} %bitcast.17, bf16[1536,512]{1,0:T(8,128)(2,1)} %bitcast.10, f32[4,128]{1,0:T(4,128)} %bitcast.19, f32[64,80,128]{2,1,0:T(8,128)} %get-tuple-element.17.refs_3_, f32[64,80,128]{2,1,0:T(8,128)} %get-tuple-element.18.refs_4_), custom_call_target="tpu_custom_call" | custom-call | tf_op jit(solution)/shard_map/rotate_gram/pallas_call | solution.py:189
  104.9 0.9 collective-permute-start
  105.9 4.7 %collective-permute-done = f32[64,80,128]{2,1,0:T(8,128)S(1)} collective-permute-done((f32[64,80,128]{2,1,0:T(8,128)}, f32[64,80,128]{2,1,0:T(8,128)S(1)}, u32[]{:S(2)}, u32[]{:S(2)}) %collective-permute-start) | collective-permute-done | bytes 2621472 | tf_op jit(solution)/shard_map/ppermute | solution.py:462
  110.6 2.1 add.3
  112.7 43.6 %all_to_all.26 = f32[64,80,128]{2,1,0:T(8,128)S(1)} all-to-all(f32[64,80,128]{2,1,0:T(8,128)S(1)} %add.3), channel_id=1, replica_groups=mesh['z'=4,'x'=4,'y'=4,'core'=2] {'z','x','y'}, dimensions={0} | all-to-all | bytes 5242880 | tf_op jit(solution)/shard_map/all_to_all | solution.py:486
  156.3 0.2 reduce_sum.9
  156.5 1.2 broadcast_in_dim.4
  157.7 5.6 %all-to-all-start.3 = ((f32[64,48,128]{2,1,0:T(8,128)}), f32[64,48,128]{2,1,0:T(8,128)S(1)}, u32[]{:S(2)}, u32[]{:S(2)}) async-start(f32[64,48,128]{2,1,0:T(8,128)} %broadcast_in_dim.4), calls=%async_computation.3 | async-start | bytes 3145728 | tf_op jit(solution)/shard_map/all_to_all | solution.py:468
  163.4 21.7 %all-to-all-done.3 = f32[64,48,128]{2,1,0:T(8,128)S(1)} async-done(((f32[64,48,128]{2,1,0:T(8,128)}), f32[64,48,128]{2,1,0:T(8,128)S(1)}, u32[]{:S(2)}, u32[]{:S(2)}) %all-to-all-start.3) | async-done | bytes 1572896 | tf_op jit(solution)/shard_map/all_to_all | solution.py:468
  185.1 0.0 copy-start.1
  185.1 3.4 %collective-permute-start.1 = (f32[24,128,128]{2,1,0:T(8,128)S(1)}, f32[24,128,128]{2,1,0:T(8,128)}, u32[]{:S(2)}, u32[]{:S(2)}) collective-permute-start(f32[24,128,128]{2,1,0:T(8,128)S(1)} %bitcast.11), channel_id=1, source_target_pairs={{0,1},{1,0},{2,3},{3,2},{4,5},{5,4},{6,7},{7,6},{8,9},{9,8},{10,11... | collective-permute-start | bytes 4718600 | tf_op jit(solution)/shard_map/ppermute | solution.py:462
  188.5 1.1 broadcast_in_dim.5
  189.6 4.9 %all-to-all-start.4 = ((f32[64,32,128]{2,1,0:T(8,128)}), f32[64,32,128]{2,1,0:T(8,128)S(1)}, u32[]{:S(2)}, u32[]{:S(2)}) async-start(f32[64,32,128]{2,1,0:T(8,128)} %broadcast_in_dim.5), calls=%async_computation.4 | async-start | bytes 2097152 | tf_op jit(solution)/shard_map/all_to_all | solution.py:468
  194.5 0.0 collective-permute-done.1.refs_1_
  194.6 0.0 copy-done.1
  194.6 20.0 %cholesky.2.refs_4_ = f32[1536,1536]{1,0:T(8,128)} custom-call(s32[1]{0:T(128)} %bitcast.core, f32[24,128,128]{2,1,0:T(8,128)} %bitcast.12, f32[24,128,128]{2,1,0:T(8,128)} %collective-permute-done.1.refs_1_), custom_call_target="tpu_custom_call" | custom-call | flops 48318382080 | bytes 28311552 | tf_op jit(solution)/shard_map/cholesky/pallas_call | solution.py:433
  214.5 0.0 all-to-all-done.4
  214.5 0.0 copy-start.2
  214.6 0.7 collective-permute-start.2
  215.2 2.3 collective-permute-done.2.refs_3_
  217.5 0.0 copy-done.2
  217.5 0.0 copy-start.3
  217.5 1.0 copy-done.3
  218.5 39.8 %cholesky.3 = f32[1536,1536]{1,0:T(8,128)} custom-call(s32[1]{0:T(128)} %bitcast.core, f32[24,128,128]{2,1,0:T(8,128)} %bitcast.13, f32[24,128,128]{2,1,0:T(8,128)} %collective-permute-done.1.refs_1_, f32[16,128,128]{2,1,0:T(8,128)} %bitcast.15, f32[16,128,128]{2,1,0:T(8,128)} %copy-done.3, f32[1536,1536]{1,0:T(8,128)} %cholesky.2.refs_4_), custom_call_target="tpu_custom_call", output_to_operand_aliasing={{}: (5, {})} | custom-call | flops 96636764160 | bytes 28311552 | tf_op jit(solution)/shard_map/cholesky/pallas_call | solution.py:433
  (2 shorter events, 0.0 us)
Async XLA Ops:
  69.3 25.3 %all-to-all-start = ((bf16[8,192,512]{2,1,0:T(8,128)(2,1)}), bf16[8,192,512]{2,1,0:T(8,128)(2,1)S(1)}, u32[]{:S(2)}, u32[]{:S(2)}) async-start(bf16[8,192,512]{2,1,0:T(8,128)(2,1)} %get-tuple-element.15), calls=%async_computation | async-start | bytes 3145728 | tf_op jit(solution)/shard_map/all_to_all | solution.py:482
  94.5 1.2 copy-start
  104.9 5.7 %collective-permute-start = (f32[64,80,128]{2,1,0:T(8,128)}, f32[64,80,128]{2,1,0:T(8,128)S(1)}, u32[]{:S(2)}, u32[]{:S(2)}) collective-permute-start(f32[64,80,128]{2,1,0:T(8,128)} %get-tuple-element.20), channel_id=1, source_target_pairs={{0,1},{1,0},{2,3},{3,2},{4,5},{5,4},{6,7},{7,6},{8,9},{9,8},{10,11... | collective-permute-start | bytes 7864328 | tf_op jit(solution)/shard_map/ppermute | solution.py:462
  157.7 27.4 %all-to-all-start.3 = ((f32[64,48,128]{2,1,0:T(8,128)}), f32[64,48,128]{2,1,0:T(8,128)S(1)}, u32[]{:S(2)}, u32[]{:S(2)}) async-start(f32[64,48,128]{2,1,0:T(8,128)} %broadcast_in_dim.4), calls=%async_computation.3 | async-start | bytes 3145728 | tf_op jit(solution)/shard_map/all_to_all | solution.py:468
  185.1 9.5 %copy-start.1 = (f32[64,48,128]{2,1,0:T(8,128)}, f32[64,48,128]{2,1,0:T(8,128)S(1)}, u32[]{:S(2)}) copy-start(f32[64,48,128]{2,1,0:T(8,128)S(1)} %all-to-all-done.3) | copy-start | bytes 4718596
  185.1 9.5 %collective-permute-start.1 = (f32[24,128,128]{2,1,0:T(8,128)S(1)}, f32[24,128,128]{2,1,0:T(8,128)}, u32[]{:S(2)}, u32[]{:S(2)}) collective-permute-start(f32[24,128,128]{2,1,0:T(8,128)S(1)} %bitcast.11), channel_id=1, source_target_pairs={{0,1},{1,0},{2,3},{3,2},{4,5},{5,4},{6,7},{7,6},{8,9},{9,8},{10,11... | collective-permute-start | bytes 4718600 | tf_op jit(solution)/shard_map/ppermute | solution.py:462
  189.6 24.9 %all-to-all-start.4 = ((f32[64,32,128]{2,1,0:T(8,128)}), f32[64,32,128]{2,1,0:T(8,128)S(1)}, u32[]{:S(2)}, u32[]{:S(2)}) async-start(f32[64,32,128]{2,1,0:T(8,128)} %broadcast_in_dim.5), calls=%async_computation.4 | async-start | bytes 2097152 | tf_op jit(solution)/shard_map/all_to_all | solution.py:468
  214.5 3.0 %copy-start.2 = (f32[64,32,128]{2,1,0:T(8,128)}, f32[64,32,128]{2,1,0:T(8,128)S(1)}, u32[]{:S(2)}) copy-start(f32[64,32,128]{2,1,0:T(8,128)S(1)} %all-to-all-done.4) | copy-start | bytes 3145732
  214.6 3.0 %collective-permute-start.2 = (f32[16,128,128]{2,1,0:T(8,128)S(1)}, f32[16,128,128]{2,1,0:T(8,128)S(1)}, u32[]{:S(2)}, u32[]{:S(2)}) collective-permute-start(f32[16,128,128]{2,1,0:T(8,128)S(1)} %bitcast.14), channel_id=1, source_target_pairs={{0,1},{1,0},{2,3},{3,2},{4,5},{5,4},{6,7},{7,6},{8,9},{9,8},{10,11... | collective-permute-start | bytes 3145736 | tf_op jit(solution)/shard_map/ppermute | solution.py:462
  217.5 1.0 copy-start.3

commit v5 on v4

--- a/solution.py
+++ b/solution.py
@@ -19,18 +19,17 @@
 VMEM_BYTES = 56 * 1024 * 1024
 
 
-def block_index(nb, i, j):
-    return sum(nb - k for k in range(i)) + (j - i)
-
-
 class Layout:
     def __init__(self, nb, plane):
         self.nb, self.plane = nb, plane
-        self.used = nb * (nb + 1) // 2
-        self.rows_early = nb // 3
-        need = block_index(nb, self.rows_early, self.rows_early)
+        self.lead = lead = nb * 2 // 3
+        order = [(i, j) for i in range(lead) for j in range(i, lead)]
+        self.leading = len(order)
+        order += [(i, j) for i in range(nb) for j in range(max(i, lead), nb)]
+        self.number = {ij: n for n, ij in enumerate(order)}
+        self.used = len(order)
         step = max(1, 8 * plane // TILE)
-        self.early = -(-(-(-need // CORES)) // step) * step
+        self.early = -(-(-(-self.leading // CORES)) // step) * step
         self.half = -(-(-(-self.used // CORES)) // step) * step
         self.share = (self.early * TILE // plane, (self.half - self.early) * TILE // plane)
 
@@ -170,7 +169,7 @@
             for i in range(j + 2):
                 for jj in range(max(i, j), j + 2):
                     cut = slice(TILE * (jj - j), TILE * (jj - j + 1))
-                    add(block_index(nb, i, jj), part[TILE * i : TILE * (i + 1), cut])
+                    add(layout.number[i, jj], part[TILE * i : TILE * (i + 1), cut])
         stores = (
             pltpu.make_async_copy(acc_ref.at[me], mine_out, sem.at[0]),
             pltpu.make_async_copy(acc_ref.at[1 - me], other_out, sem.at[1]),
@@ -309,6 +308,13 @@
 
 
 def product(left, right, contract):
+    if left[0].shape[contract] <= TILE:
+        pairs = ((0, 0), (0, 1), (1, 0), (1, 1), (0, 2), (2, 0))
+        return dot_parts(
+            jnp.concatenate([left[p] for p, _ in pairs], axis=contract),
+            jnp.concatenate([right[q] for _, q in pairs], axis=0),
+            contract,
+        )
     m = left[0].shape[1 - contract]
     p = dot_parts(jnp.concatenate(left, axis=1 - contract), right[0], contract)
     q = dot_parts(jnp.concatenate(left[:2], axis=1 - contract), right[1], contract)
@@ -320,13 +326,20 @@
     return [v.astype(jnp.bfloat16) for v in split3(x)]
 
 
-def cholesky_kernel(layout, scale, begin, end, core, *refs):
-    sources = refs[: 2 if begin == 0 else 5]
-    out_ref, u_ref, g_ref, a_ref, e_ref, s_ref, p_ref, in_sem, out_sem = refs[len(sources) :]
+def cholesky_kernel(layout, scale, leading, core, *refs):
+    n_in = 2 if leading else 6
+    sources, refs = refs[:n_in], refs[n_in:]
+    out_ref, refs = refs[0], refs[1:]
+    if leading:
+        inverse_ref, refs = refs[0], refs[1:]
+    u_ref, g_ref, a_ref, e_ref, s_ref, p_ref, i_ref, in_sem, out_sem = refs
     me = core[0]
-    size = u_ref.shape[0]
-    nb, early = layout.nb, layout.early
-    below = slice(0, TILE * begin)
+    nb, lead, early = layout.nb, layout.lead, layout.early
+    begin, end = (0, lead) if leading else (lead, nb)
+    edge = TILE * lead
+    size = edge if leading else TILE * nb
+    square = (slice(0, edge), slice(0, edge))
+    corner = (slice(0, edge), slice(edge, TILE * nb))
 
     def part_loads(pair, lo, hi, to, sems):
         mine, other = pair
@@ -338,32 +351,55 @@
             ),
         ]
 
-    if begin == 0:
-        first = block_index(nb, 2, 2) // CORES + 1
-        now = part_loads(sources[:2], 0, first, 0, 0)
-        later = part_loads(sources[:2], first, early, first, 2)
+    if leading:
+        loads = part_loads(sources[:2], 0, early, 0, 0)
     else:
-        first = block_index(nb, begin, begin) // CORES
-        now = part_loads(sources[:2], first, early, first, 0)
-        now += part_loads(sources[2:4], 0, layout.half - early, early, 2)
-        now.append(pltpu.make_async_copy(sources[4].at[below], u_ref.at[below], in_sem.at[4]))
-        later = []
+        first = layout.leading // CORES
+        loads = part_loads(sources[2:4], 0, layout.half - early, early, 2)
+        if first < early:
+            loads += part_loads(sources[:2], first, early, first, 0)
+        loads.append(pltpu.make_async_copy(sources[4].at[square], u_ref.at[square], in_sem.at[4]))
+        loads.append(pltpu.make_async_copy(sources[5], i_ref, in_sem.at[5]))
 
     def store(k):
-        rows = slice(TILE * k, TILE * (k + 1))
-        return pltpu.make_async_copy(u_ref.at[rows], out_ref.at[rows], out_sem.at[k])
-
-    for copy in now + later:
-        copy.start()
-    for copy in now:
-        copy.wait()
-    if begin:
-        rest = slice(TILE * begin, size)
-        for q, v in enumerate(parts3(u_ref[below, rest])):
-            p_ref[q, below, rest] = v
+        here = (slice(TILE * k, TILE * (k + 1)), slice(0, size))
+        return pltpu.make_async_copy(u_ref.at[here], out_ref.at[here], out_sem.at[k])
+
+    def gram(i, j):
+        n = layout.number[i, j]
+        return g_ref[n % CORES, n // CORES] * scale
 
     def up(rows, cols):
         return [p_ref[q, rows, cols] for q in range(3)]
+
+    def keep(rows, cols, value):
+        for q, v in enumerate(parts3(value)):
+            p_ref[q, rows, cols] = v
+
+    for copy in loads:
+        copy.start()
+    for copy in loads:
+        copy.wait()
+
+    stores = []
+    if not leading:
+        right = slice(edge, size)
+        for k in range(lead):
+            rows, cols = slice(TILE * k, TILE * (k + 1)), slice(TILE * k, edge)
+            keep(rows, cols, u_ref[rows, cols])
+        for k in range(lead):
+            rows = slice(TILE * k, TILE * (k + 1))
+            above = slice(0, TILE * k)
+            value = jnp.concatenate([gram(k, j) for j in range(lead, nb)], axis=1)
+            if k:
+                value = value - product(up(above, rows), up(above, right), 0)
+            value = product(parts3(i_ref[k]), parts3(value), 1)
+            u_ref[rows, right] = value
+            keep(rows, right, value)
+        stores.append(
+            pltpu.make_async_copy(u_ref.at[corner], out_ref.at[corner], out_sem.at[0])
+        )
+        stores[0].start()
 
     def body(i, carry):
         for k in range(begin, end):
@@ -373,26 +409,22 @@
 
             @pl.when(i == k)
             def _(k=k, h=h, r0=r0, c0=c0):
-                if k == 2:
-                    for copy in later:
-                        copy.wait()
                 if h == 0:
                     for hh in range(2):
-                        for j in range(k, nb):
+                        for j in range(k, size // TILE):
                             if j < k + hh:
                                 block = jnp.zeros((TILE, TILE), jnp.float32)
                             else:
-                                idx = block_index(nb, k + hh, j)
-                                block = g_ref[idx % CORES, idx // CORES] * scale
+                                block = gram(k + hh, j)
                             s_ref[TILE * hh : TILE * (hh + 1), TILE * j : TILE * (j + 1)] = block
                     if r0:
                         panel = slice(r0, r0 + 2 * TILE)
-                        s_ref[:, r0:] -= product(
+                        s_ref[:, r0:size] -= product(
                             up(slice(0, r0), panel), up(slice(0, r0), slice(r0, size)), 0
                         )
                 else:
                     above = slice(r0, c0)
-                    s_ref[TILE:, c0:] -= product(
+                    s_ref[TILE:, c0:size] -= product(
                         up(above, slice(c0, c0 + TILE)), up(above, slice(c0, size)), 0
                     )
                 a_ref[...] = s_ref[TILE * h : TILE * (h + 1), c0 : c0 + TILE]
@@ -408,36 +440,44 @@
                 if c0:
                     u_ref[rows, 0:c0] = jnp.zeros((TILE, c0), jnp.float32)
                 u_ref[rows, c0 : c0 + TILE] = a_ref[...]
+                if leading:
+                    i_ref[k] = e_ref[...]
                 if c0 + TILE < size:
                     rest = slice(c0 + TILE, size)
                     solved = product(
                         parts3(e_ref[...]), parts3(s_ref[TILE * h : TILE * (h + 1), rest]), 1
                     )
                     u_ref[rows, rest] = solved
-                    for q, v in enumerate(parts3(solved)):
-                        p_ref[q, rows, rest] = v
+                    keep(rows, rest, solved)
                 store(k).start()
 
         return carry
 
     lax.fori_loop(begin, end, body, 0)
-    for k in range(begin, end):
-        store(k).wait()
-
-
-def cholesky_rows(layout, core, groups, so_far, scale):
+    if leading:
+        stores.append(pltpu.make_async_copy(i_ref, inverse_ref, in_sem.at[4]))
+        stores[0].start()
+    stores += [store(k) for k in range(begin, end)]
+    for copy in stores:
+        copy.wait()
+
+
+def cholesky_part(layout, core, groups, so_far, scale):
     size = layout.nb * TILE
-    begin, end = (0, layout.rows_early) if so_far is None else (layout.rows_early, layout.nb)
+    leading = so_far is None
     anywhere = pl.BlockSpec(memory_space=pl.ANY)
-    sources = [x for pair in groups for x in pair] + ([] if so_far is None else [so_far])
+    sources = [x for pair in groups for x in pair] + ([] if leading else list(so_far))
+    factor = jax.ShapeDtypeStruct((size, size), jnp.float32)
+    inverses = jax.ShapeDtypeStruct((layout.lead, TILE, TILE), jnp.float32)
+    blocks = layout.lead if leading else layout.nb - layout.lead
     return pl.pallas_call(
-        functools.partial(cholesky_kernel, layout, scale, begin, end),
-        out_shape=jax.ShapeDtypeStruct((size, size), jnp.float32),
+        functools.partial(cholesky_kernel, layout, scale, leading),
+        out_shape=(factor, inverses) if leading else factor,
         grid_spec=pltpu.PrefetchScalarGridSpec(
             num_scalar_prefetch=1,
             grid=(1,),
             in_specs=[anywhere] * len(sources),
-            out_specs=anywhere,
+            out_specs=(anywhere, anywhere) if leading else anywhere,
             scratch_shapes=[
                 pltpu.VMEM((size, size), jnp.float32),
                 pltpu.VMEM((CORES, layout.half, TILE, TILE), jnp.float32),
@@ -445,13 +485,14 @@
                 pltpu.VMEM((TILE, TILE), jnp.float32),
                 pltpu.VMEM((2 * TILE, size), jnp.float32),
                 pltpu.VMEM((3, size, size), jnp.bfloat16),
-                pltpu.SemaphoreType.DMA((5,)),
+                pltpu.VMEM((layout.lead, TILE, TILE), jnp.float32),
+                pltpu.SemaphoreType.DMA((6,)),
                 pltpu.SemaphoreType.DMA((layout.nb,)),
             ],
         ),
-        input_output_aliases={} if so_far is None else {len(sources): 0},
+        input_output_aliases={} if leading else {len(sources) - 1: 0},
         cost_estimate=pl.CostEstimate(
-            flops=40 * (end - begin) * size**2 * TILE, transcendentals=0, bytes_accessed=12 * size**2
+            flops=40 * blocks * size**2 * TILE, transcendentals=0, bytes_accessed=12 * size**2
         ),
         compiler_params=pltpu.CompilerParams(vmem_limit_bytes=VMEM_BYTES),
         name="cholesky",
@@ -491,10 +532,10 @@
     late = gather_plane(late)
     early, late = (g.reshape(-1, TILE, TILE) for g in (early, late))
     groups = [(early, swap_cores(early))]
-    upper = cholesky_rows(layout, core, groups, None, scale)
+    upper, inverses = cholesky_part(layout, core, groups, None, scale)
     late, upper = lax.optimization_barrier((late, upper))
     groups.append((late, swap_cores(late)))
-    return cholesky_rows(layout, core, groups, upper, scale)
+    return cholesky_part(layout, core, groups, (upper, inverses), scale)
 
 
 def solution(mesh):

time: 259 us -> 256 us (0.988)
  blocking collectives: 105 us -> 129 us
  waiting for transfers between devices: 31.1 us -> 9.74 us
  starting transfers between devices: 20.1 us -> 14.4 us
    all_to_all x0 -> x1, blocking collectives: none -> 24.4 us  [gather_plane(): lax.all_to_all(copies, PLANE_AXES, split_axis=0, concat_axis=0, tiled=True)]
    all_to_all x2 -> x1, waiting for transfers between devices: 21.7 us -> 0.01 us  [gather_plane(): lax.all_to_all(copies, PLANE_AXES, split_axis=0, concat_axis=0, tiled=True)]
    all_to_all x2 -> x1, starting transfers between devices: 10.6 us -> 4.84 us  [gather_plane(): lax.all_to_all(copies, PLANE_AXES, split_axis=0, concat_axis=0, tiled=True)]
  transfers between devices with their start and end apart: 6 -> 5, of which waited for: 4 -> 3; matrix products, arithmetic and copies ran while one was open for 0% -> 0% of each run, Pallas kernels for 15% -> 20%
where the time goes in v5:
time: 256 us; the launch traced here: 255 us
  blocking collectives  129 us (50%)
  Pallas kernels  95.7 us (37%)
  starting transfers between devices  14.4 us (6%)
  waiting for transfers between devices  9.74 us (4%)
  local copies, waits for them, and re-layouts  3.6 us (1%)
    all_to_all x1, blocking collectives, shards(): lax.all_to_all(filtered, GAUGE_AXES, split_axis=0, concat_axis=0, tiled=T...  61.1 us
    pallas_call x2, Pallas kernels, cholesky_part(): pl.pallas_call(functools.partial(cholesky_kernel, layout, scale, leading)...  60 us
    all_to_all x1, blocking collectives, shards(): lax.all_to_all(mine, PLANE_AXES, split_axis=0, concat_axis=0, tiled=True)  43.6 us
    pallas_call x2, Pallas kernels, gram_chunk(): pl.pallas_call(functools.partial(gram_kernel, layout, so_far is None), ou...  27.6 us
    all_to_all x1, blocking collectives, gather_plane(): lax.all_to_all(copies, PLANE_AXES, split_axis=0, concat_axis=0, tiled=True)  24.4 us
    pallas_call x1, Pallas kernels, filter_records(): pl.pallas_call(filter_kernel, out_shape=tuple((jax.ShapeDtypeStruct((part...  8.18 us
    ppermute x3, waiting for transfers between devices, swap_cores(): return lax.ppermute(x, 'core', [(0, 1), (1, 0)])  7.43 us
  transfers between devices with their start and end apart: 5, of which 3 were waited for; matrix products, arithmetic and copies ran while one was open for 0% of the time, Pallas kernels for 20%

profile of v5, /device:TPU:1, one launch (start us, length us, event | category | flops | bytes accessed | tf_op | source)
XLA Modules:
  0.0 255.1 jit_solution(12261124772489203981)
XLA Ops:
  0.0 8.2 %drift_filter.1 = (bf16[8,192,1536]{2,1,0:T(8,128)(2,1)}, bf16[8,192,512]{2,1,0:T(8,128)(2,1)}) custom-call(s32[16]{0:T(128)} %offsets.1, bf16[192,16384]{1,0:T(8,128)(2,1)} %bitcast.9), custom_call_target="tpu_custom_call" | custom-call | tf_op jit(solution)/shard_map/drift_filter/pallas_call | solution.py:79
  8.2 61.1 %all_to_all.25 = bf16[8,192,1536]{2,1,0:T(8,128)(2,1)} all-to-all(bf16[8,192,1536]{2,1,0:T(8,128)(2,1)} %get-tuple-element.18), channel_id=1, replica_groups=mesh['z'=4,'x'=4,'y'=4,'core'=2] {'y','core'}, dimensions={0} | all-to-all | bytes 9437184 | tf_op jit(solution)/shard_map/all_to_all | solution.py:523
  69.3 4.5 %all-to-all-start = ((bf16[8,192,512]{2,1,0:T(8,128)(2,1)}), bf16[8,192,512]{2,1,0:T(8,128)(2,1)S(1)}, u32[]{:S(2)}, u32[]{:S(2)}) async-start(bf16[8,192,512]{2,1,0:T(8,128)(2,1)} %get-tuple-element.17), calls=%async_computation | async-start | bytes 3145728 | tf_op jit(solution)/shard_map/all_to_all | solution.py:523
  73.8 18.4 %rotate_gram.2 = (f32[64,80,128]{2,1,0:T(8,128)}, f32[64,80,128]{2,1,0:T(8,128)}) custom-call(s32[1]{0:T(128)} %bitcast.core, s32[12,128]{1,0:T(8,128)} %bitcast.16, bf16[1536,1536]{1,0:T(8,128)(2,1)} %bitcast.8, f32[4,128]{1,0:T(4,128)} %bitcast.18), custom_call_target="tpu_custom_call" | custom-call | tf_op jit(solution)/shard_map/rotate_gram/pallas_call | solution.py:188
  92.2 2.3 all-to-all-done
  94.5 0.0 copy-start
  94.5 1.2 copy-done
  95.8 9.1 %rotate_gram.3 = (f32[64,80,128]{2,1,0:T(8,128)}, f32[64,80,128]{2,1,0:T(8,128)}) custom-call(s32[1]{0:T(128)} %bitcast.core, s32[12,128]{1,0:T(8,128)} %bitcast.17, bf16[1536,512]{1,0:T(8,128)(2,1)} %bitcast.10, f32[4,128]{1,0:T(4,128)} %bitcast.19, f32[64,80,128]{2,1,0:T(8,128)} %get-tuple-element.19.refs_3_, f32[64,80,128]{2,1,0:T(8,128)} %get-tuple-element.20.refs_4_), custom_call_target="tpu_custom_call" | custom-call | tf_op jit(solution)/shard_map/rotate_gram/pallas_call | solution.py:188
  104.9 0.9 collective-permute-start
  105.9 4.7 %collective-permute-done = f32[64,80,128]{2,1,0:T(8,128)S(1)} collective-permute-done((f32[64,80,128]{2,1,0:T(8,128)}, f32[64,80,128]{2,1,0:T(8,128)S(1)}, u32[]{:S(2)}, u32[]{:S(2)}) %collective-permute-start) | collective-permute-done | bytes 2621472 | tf_op jit(solution)/shard_map/ppermute | solution.py:503
  110.6 2.1 add.3
  112.7 43.6 %all_to_all.26 = f32[64,80,128]{2,1,0:T(8,128)S(1)} all-to-all(f32[64,80,128]{2,1,0:T(8,128)S(1)} %add.3), channel_id=1, replica_groups=mesh['z'=4,'x'=4,'y'=4,'core'=2] {'z','x','y'}, dimensions={0} | all-to-all | bytes 5242880 | tf_op jit(solution)/shard_map/all_to_all | solution.py:527
  156.3 0.2 reduce_sum.9
  156.5 0.1 broadcast_in_dim.4
  156.6 24.4 %all_to_all.27 = f32[64,40,128]{2,1,0:T(8,128)S(1)} all-to-all(f32[64,40,128]{2,1,0:T(8,128)S(1)} %broadcast_in_dim.4), channel_id=1, replica_groups=mesh['z'=4,'x'=4,'y'=4,'core'=2] {'z','x','y'}, dimensions={0} | all-to-all | bytes 2621440 | tf_op jit(solution)/shard_map/all_to_all | solution.py:509
  180.9 0.0 copy-start.1
  180.9 3.5 %collective-permute-start.1 = (f32[20,128,128]{2,1,0:T(8,128)S(1)}, f32[20,128,128]{2,1,0:T(8,128)}, u32[]{:S(2)}, u32[]{:S(2)}) collective-permute-start(f32[20,128,128]{2,1,0:T(8,128)S(1)} %bitcast.11), channel_id=1, source_target_pairs={{0,1},{1,0},{2,3},{3,2},{4,5},{5,4},{6,7},{7,6},{8,9},{9,8},{10,11... | collective-permute-start | bytes 3932168 | tf_op jit(solution)/shard_map/ppermute | solution.py:503
  184.4 1.1 broadcast_in_dim.5
  185.5 4.8 %all-to-all-start.4 = ((f32[64,40,128]{2,1,0:T(8,128)}), f32[64,40,128]{2,1,0:T(8,128)S(1)}, u32[]{:S(2)}, u32[]{:S(2)}) async-start(f32[64,40,128]{2,1,0:T(8,128)} %broadcast_in_dim.5), calls=%async_computation.4 | async-start | bytes 2621440 | tf_op jit(solution)/shard_map/all_to_all | solution.py:509
  190.4 0.0 collective-permute-done.1.refs_1_
  190.4 0.0 copy-done.1
  190.4 33.4 %cholesky.2 = (f32[1536,1536]{1,0:T(8,128)}, f32[8,128,128]{2,1,0:T(8,128)}) custom-call(s32[1]{0:T(128)} %bitcast.core, f32[20,128,128]{2,1,0:T(8,128)} %bitcast.12, f32[20,128,128]{2,1,0:T(8,128)} %collective-permute-done.1.refs_1_), custom_call_target="tpu_custom_call" | custom-call | flops 96636764160 | bytes 28311552 | tf_op jit(solution)/shard_map/cholesky/pallas_call | solution.py:473
  223.8 0.0 all-to-all-done.4
  223.8 0.0 copy-start.2
  223.8 0.7 collective-permute-start.2
  224.5 2.7 %collective-permute-done.2.refs_3_ = f32[20,128,128]{2,1,0:T(8,128)S(1)} collective-permute-done((f32[20,128,128]{2,1,0:T(8,128)S(1)}, f32[20,128,128]{2,1,0:T(8,128)S(1)}, u32[]{:S(2)}, u32[]{:S(2)}) %collective-permute-start.2) | collective-permute-done | bytes 1310752 | tf_op jit(solution)/shard_map/ppermute | solution.py:503
  227.2 0.0 copy-start.3
  227.2 0.0 copy-done.2
  227.2 1.1 copy-done.3
  228.3 26.6 %cholesky.3 = f32[1536,1536]{1,0:T(8,128)} custom-call(s32[1]{0:T(128)} %bitcast.core, f32[20,128,128]{2,1,0:T(8,128)} %bitcast.13, f32[20,128,128]{2,1,0:T(8,128)} %collective-permute-done.1.refs_1_, f32[20,128,128]{2,1,0:T(8,128)} %bitcast.15, f32[20,128,128]{2,1,0:T(8,128)} %copy-done.3, ...), custom_call_target="tpu_custom_call", output_to_operand_aliasing={{}: (5, {})} | custom-call | flops 48318382080 | bytes 28311552 | tf_op jit(solution)/shard_map/cholesky/pallas_call | solution.py:473
  (1 shorter events, 0.0 us)
Async XLA Ops:
  69.3 25.3 %all-to-all-start = ((bf16[8,192,512]{2,1,0:T(8,128)(2,1)}), bf16[8,192,512]{2,1,0:T(8,128)(2,1)S(1)}, u32[]{:S(2)}, u32[]{:S(2)}) async-start(bf16[8,192,512]{2,1,0:T(8,128)(2,1)} %get-tuple-element.17), calls=%async_computation | async-start | bytes 3145728 | tf_op jit(solution)/shard_map/all_to_all | solution.py:523
  94.5 1.2 copy-start
  104.9 5.7 %collective-permute-start = (f32[64,80,128]{2,1,0:T(8,128)}, f32[64,80,128]{2,1,0:T(8,128)S(1)}, u32[]{:S(2)}, u32[]{:S(2)}) collective-permute-start(f32[64,80,128]{2,1,0:T(8,128)} %get-tuple-element.22), channel_id=1, source_target_pairs={{0,1},{1,0},{2,3},{3,2},{4,5},{5,4},{6,7},{7,6},{8,9},{9,8},{10,11... | collective-permute-start | bytes 7864328 | tf_op jit(solution)/shard_map/ppermute | solution.py:503
  180.9 9.5 %copy-start.1 = (f32[64,40,128]{2,1,0:T(8,128)}, f32[64,40,128]{2,1,0:T(8,128)S(1)}, u32[]{:S(2)}) copy-start(f32[64,40,128]{2,1,0:T(8,128)S(1)} %all_to_all.27) | copy-start | bytes 3932164
  180.9 9.5 %collective-permute-start.1 = (f32[20,128,128]{2,1,0:T(8,128)S(1)}, f32[20,128,128]{2,1,0:T(8,128)}, u32[]{:S(2)}, u32[]{:S(2)}) collective-permute-start(f32[20,128,128]{2,1,0:T(8,128)S(1)} %bitcast.11), channel_id=1, source_target_pairs={{0,1},{1,0},{2,3},{3,2},{4,5},{5,4},{6,7},{7,6},{8,9},{9,8},{10,11... | collective-permute-start | bytes 3932168 | tf_op jit(solution)/shard_map/ppermute | solution.py:503
  185.5 38.3 %all-to-all-start.4 = ((f32[64,40,128]{2,1,0:T(8,128)}), f32[64,40,128]{2,1,0:T(8,128)S(1)}, u32[]{:S(2)}, u32[]{:S(2)}) async-start(f32[64,40,128]{2,1,0:T(8,128)} %broadcast_in_dim.5), calls=%async_computation.4 | async-start | bytes 2621440 | tf_op jit(solution)/shard_map/all_to_all | solution.py:509
  223.8 3.4 %copy-start.2 = (f32[64,40,128]{2,1,0:T(8,128)}, f32[64,40,128]{2,1,0:T(8,128)S(1)}, u32[]{:S(2)}) copy-start(f32[64,40,128]{2,1,0:T(8,128)S(1)} %all-to-all-done.4) | copy-start | bytes 3932164
  223.8 3.3 %collective-permute-start.2 = (f32[20,128,128]{2,1,0:T(8,128)S(1)}, f32[20,128,128]{2,1,0:T(8,128)S(1)}, u32[]{:S(2)}, u32[]{:S(2)}) collective-permute-start(f32[20,128,128]{2,1,0:T(8,128)S(1)} %bitcast.14), channel_id=1, source_target_pairs={{0,1},{1,0},{2,3},{3,2},{4,5},{5,4},{6,7},{7,6},{8,9},{9,8},{10,11... | collective-permute-start | bytes 3932168 | tf_op jit(solution)/shard_map/ppermute | solution.py:503
  227.2 1.1 copy-start.3

commit v6 on v5

--- a/solution.py
+++ b/solution.py
@@ -22,7 +22,7 @@
 class Layout:
     def __init__(self, nb, plane):
         self.nb, self.plane = nb, plane
-        self.lead = lead = nb * 2 // 3
+        self.lead = lead = nb // 4 * 2
         order = [(i, j) for i in range(lead) for j in range(i, lead)]
         self.leading = len(order)
         order += [(i, j) for i in range(nb) for j in range(max(i, lead), nb)]
@@ -503,9 +503,7 @@
     return lax.ppermute(x, "core", [(0, 1), (1, 0)])
 
 
-def gather_plane(x):
-    plane = lax.axis_size(PLANE_AXES)
-    copies = jnp.broadcast_to(x[None], (plane, *x.shape))
+def gather_plane(copies):
     return lax.all_to_all(copies, PLANE_AXES, split_axis=0, concat_axis=0, tiled=True)
 
 
@@ -526,7 +524,10 @@
     mine = mine + swap_cores(other)
     spread = lax.all_to_all(mine, PLANE_AXES, split_axis=0, concat_axis=0, tiled=True).sum(0)
     scale = 1.0 / (rows * lax.axis_size(SAMPLE_AXES))
-    early, late = jnp.split(spread, [layout.share[0]])
+    early, late = (
+        jnp.broadcast_to(x[None], (layout.plane, *x.shape))
+        for x in jnp.split(spread, [layout.share[0]])
+    )
     early = gather_plane(early)
     late, early = lax.optimization_barrier((late, early))
     late = gather_plane(late)

time: 256 us -> 255 us (level)
  blocking collectives: 129 us -> 105 us
  waiting for transfers between devices: 9.74 us -> 25.6 us
  starting transfers between devices: 14.4 us -> 20.2 us
    all_to_all x1 -> x0, blocking collectives: 24.4 us -> none  [gather_plane(): lax.all_to_all(copies, PLANE_AXES, split_axis=0, concat_axis=0, tiled=True)]
    all_to_all x1 -> x2, waiting for transfers between devices: 0.01 us -> 15.2 us  [gather_plane(): lax.all_to_all(copies, PLANE_AXES, split_axis=0, concat_axis=0, tiled=True)]
    all_to_all x1 -> x2, starting transfers between devices: 4.84 us -> 10.3 us  [gather_plane(): lax.all_to_all(copies, PLANE_AXES, split_axis=0, concat_axis=0, tiled=True)]
  transfers between devices with their start and end apart: 5 -> 6, of which waited for: 3 -> 5; matrix products, arithmetic and copies ran while one was open for 0% -> 0% of each run, Pallas kernels for 20% -> 17%
where the time goes in v6:
time: 255 us; the launch traced here: 254 us
  blocking collectives  105 us (41%)
  Pallas kernels  95.2 us (37%)
  waiting for transfers between devices  25.6 us (10%)
  starting transfers between devices  20.2 us (8%)
  local copies, waits for them, and re-layouts  5.78 us (2%)
    all_to_all x1, blocking collectives, shards(): lax.all_to_all(filtered, GAUGE_AXES, split_axis=0, concat_axis=0, tiled=T...  61.1 us
    pallas_call x2, Pallas kernels, cholesky_part(): pl.pallas_call(functools.partial(cholesky_kernel, layout, scale, leading)...  59.5 us
    all_to_all x1, blocking collectives, shards(): lax.all_to_all(mine, PLANE_AXES, split_axis=0, concat_axis=0, tiled=True)  43.6 us
    pallas_call x2, Pallas kernels, gram_chunk(): pl.pallas_call(functools.partial(gram_kernel, layout, so_far is None), ou...  27.6 us
    all_to_all x2, waiting for transfers between devices, gather_plane(): lax.all_to_all(copies, PLANE_AXES, split_axis=0, concat_axis=0, tiled=True)  15.2 us
    all_to_all x2, starting transfers between devices, gather_plane(): lax.all_to_all(copies, PLANE_AXES, split_axis=0, concat_axis=0, tiled=True)  10.3 us
    pallas_call x1, Pallas kernels, filter_records(): pl.pallas_call(filter_kernel, out_shape=tuple((jax.ShapeDtypeStruct((part...  8.18 us
    ppermute x3, waiting for transfers between devices, swap_cores(): return lax.ppermute(x, 'core', [(0, 1), (1, 0)])  8.16 us
  transfers between devices with their start and end apart: 6, of which 5 were waited for; matrix products, arithmetic and copies ran while one was open for 0% of the time, Pallas kernels for 17%

profile of v6, /device:TPU:1, one launch (start us, length us, event | category | flops | bytes accessed | tf_op | source)
XLA Modules:
  0.0 254.0 jit_solution(15965249644756634431)
XLA Ops:
  0.0 8.2 %drift_filter.1 = (bf16[8,192,1536]{2,1,0:T(8,128)(2,1)}, bf16[8,192,512]{2,1,0:T(8,128)(2,1)}) custom-call(s32[16]{0:T(128)} %offsets.1, bf16[192,16384]{1,0:T(8,128)(2,1)} %bitcast.9), custom_call_target="tpu_custom_call" | custom-call | tf_op jit(solution)/shard_map/drift_filter/pallas_call | solution.py:79
  8.2 61.1 %all_to_all.25 = bf16[8,192,1536]{2,1,0:T(8,128)(2,1)} all-to-all(bf16[8,192,1536]{2,1,0:T(8,128)(2,1)} %get-tuple-element.18), channel_id=1, replica_groups=mesh['z'=4,'x'=4,'y'=4,'core'=2] {'y','core'}, dimensions={0} | all-to-all | bytes 9437184 | tf_op jit(solution)/shard_map/all_to_all | solution.py:521
  69.3 4.5 %all-to-all-start = ((bf16[8,192,512]{2,1,0:T(8,128)(2,1)}), bf16[8,192,512]{2,1,0:T(8,128)(2,1)S(1)}, u32[]{:S(2)}, u32[]{:S(2)}) async-start(bf16[8,192,512]{2,1,0:T(8,128)(2,1)} %get-tuple-element.17), calls=%async_computation | async-start | bytes 3145728 | tf_op jit(solution)/shard_map/all_to_all | solution.py:521
  73.8 18.4 %rotate_gram.2 = (f32[64,80,128]{2,1,0:T(8,128)}, f32[64,80,128]{2,1,0:T(8,128)}) custom-call(s32[1]{0:T(128)} %bitcast.core, s32[12,128]{1,0:T(8,128)} %bitcast.16, bf16[1536,1536]{1,0:T(8,128)(2,1)} %bitcast.8, f32[4,128]{1,0:T(4,128)} %bitcast.18), custom_call_target="tpu_custom_call" | custom-call | tf_op jit(solution)/shard_map/rotate_gram/pallas_call | solution.py:188
  92.2 2.3 all-to-all-done
  94.5 1.2 copy-done
  95.8 9.1 %rotate_gram.3 = (f32[64,80,128]{2,1,0:T(8,128)}, f32[64,80,128]{2,1,0:T(8,128)}) custom-call(s32[1]{0:T(128)} %bitcast.core, s32[12,128]{1,0:T(8,128)} %bitcast.17, bf16[1536,512]{1,0:T(8,128)(2,1)} %bitcast.10, f32[4,128]{1,0:T(4,128)} %bitcast.19, f32[64,80,128]{2,1,0:T(8,128)} %get-tuple-element.19.refs_3_, f32[64,80,128]{2,1,0:T(8,128)} %get-tuple-element.20.refs_4_), custom_call_target="tpu_custom_call" | custom-call | tf_op jit(solution)/shard_map/rotate_gram/pallas_call | solution.py:188
  104.9 0.9 collective-permute-start
  105.8 4.7 %collective-permute-done = f32[64,80,128]{2,1,0:T(8,128)S(1)} collective-permute-done((f32[64,80,128]{2,1,0:T(8,128)}, f32[64,80,128]{2,1,0:T(8,128)S(1)}, u32[]{:S(2)}, u32[]{:S(2)}) %collective-permute-start) | collective-permute-done | bytes 2621472 | tf_op jit(solution)/shard_map/ppermute | solution.py:503
  110.6 2.1 add.3
  112.7 43.6 %all_to_all.26 = f32[64,80,128]{2,1,0:T(8,128)S(1)} all-to-all(f32[64,80,128]{2,1,0:T(8,128)S(1)} %add.3), channel_id=1, replica_groups=mesh['z'=4,'x'=4,'y'=4,'core'=2] {'z','x','y'}, dimensions={0} | all-to-all | bytes 5242880 | tf_op jit(solution)/shard_map/all_to_all | solution.py:525
  156.3 0.2 reduce_sum.9
  156.4 0.9 broadcast_in_dim.5
  157.4 5.6 %all-to-all-start.3 = ((f32[64,24,128]{2,1,0:T(8,128)}), f32[64,24,128]{2,1,0:T(8,128)S(1)}, u32[]{:S(2)}, u32[]{:S(2)}) async-start(f32[64,24,128]{2,1,0:T(8,128)} %broadcast_in_dim.5), calls=%async_computation.3 | async-start | bytes 1572864 | tf_op jit(solution)/shard_map/all_to_all | solution.py:507
  163.0 13.9 %all-to-all-done.3 = f32[64,24,128]{2,1,0:T(8,128)S(1)} async-done(((f32[64,24,128]{2,1,0:T(8,128)}), f32[64,24,128]{2,1,0:T(8,128)S(1)}, u32[]{:S(2)}, u32[]{:S(2)}) %all-to-all-start.3) | async-done | bytes 786464 | tf_op jit(solution)/shard_map/all_to_all | solution.py:507
  176.9 0.0 copy-start.2
  176.9 1.4 broadcast_in_dim.4
  178.3 3.1 %collective-permute-start.1 = (f32[12,128,128]{2,1,0:T(8,128)S(1)}, f32[12,128,128]{2,1,0:T(8,128)S(1)}, u32[]{:S(2)}, u32[]{:S(2)}) collective-permute-start(f32[12,128,128]{2,1,0:T(8,128)S(1)} %bitcast.13), channel_id=1, source_target_pairs={{0,1},{1,0},{2,3},{3,2},{4,5},{5,4},{6,7},{7,6},{8,9},{9,8},{10,11... | collective-permute-start | bytes 2359304 | tf_op jit(solution)/shard_map/ppermute | solution.py:503
  181.4 0.0 copy-done.2
  181.4 4.7 %all-to-all-start.4 = ((f32[64,56,128]{2,1,0:T(8,128)}), f32[64,56,128]{2,1,0:T(8,128)S(1)}, u32[]{:S(2)}, u32[]{:S(2)}) async-start(f32[64,56,128]{2,1,0:T(8,128)} %broadcast_in_dim.4), calls=%async_computation.4 | async-start | bytes 3670016 | tf_op jit(solution)/shard_map/all_to_all | solution.py:507
  186.1 0.0 collective-permute-done.1.refs_1_
  186.1 0.0 copy-start.4
  186.1 0.9 copy-done.4
  187.0 24.2 %cholesky.2 = (f32[1536,1536]{1,0:T(8,128)}, f32[6,128,128]{2,1,0:T(8,128)}) custom-call(s32[1]{0:T(128)} %bitcast.core, f32[12,128,128]{2,1,0:T(8,128)} %bitcast.14, f32[12,128,128]{2,1,0:T(8,128)} %copy-done.4), custom_call_target="tpu_custom_call" | custom-call | flops 72477573120 | bytes 28311552 | tf_op jit(solution)/shard_map/cholesky/pallas_call | solution.py:473
  211.2 1.3 all-to-all-done.4
  212.5 0.0 copy-start.1
  212.5 1.3 collective-permute-start.2
  213.8 3.4 %collective-permute-done.2.refs_3_ = f32[28,128,128]{2,1,0:T(8,128)S(1)} collective-permute-done((f32[28,128,128]{2,1,0:T(8,128)S(1)}, f32[28,128,128]{2,1,0:T(8,128)S(1)}, u32[]{:S(2)}, u32[]{:S(2)}) %collective-permute-start.2) | collective-permute-done | bytes 1835040 | tf_op jit(solution)/shard_map/ppermute | solution.py:503
  217.2 0.0 copy-start.3
  217.2 0.0 copy-done.1
  217.2 1.2 copy-done.3
  218.5 35.3 %cholesky.3 = f32[1536,1536]{1,0:T(8,128)} custom-call(s32[1]{0:T(128)} %bitcast.core, f32[12,128,128]{2,1,0:T(8,128)} %bitcast.15, f32[12,128,128]{2,1,0:T(8,128)} %copy-done.4, f32[28,128,128]{2,1,0:T(8,128)} %bitcast.12, f32[28,128,128]{2,1,0:T(8,128)} %copy-done.3, f32[1536,1536]{1,0:T(8,128)} %get-tuple-element.27.refs_4_, ...), custom_call_target="tpu_custom_call", output_to_operand_aliasing={{}: (5, {})} | custom-call | flops 72477573120 | bytes 28311552 | tf_op jit(solution)/shard_map/cholesky/pallas_call | solution.py:473
  (3 shorter events, 0.0 us)
Async XLA Ops:
  69.3 25.3 %all-to-all-start = ((bf16[8,192,512]{2,1,0:T(8,128)(2,1)}), bf16[8,192,512]{2,1,0:T(8,128)(2,1)S(1)}, u32[]{:S(2)}, u32[]{:S(2)}) async-start(bf16[8,192,512]{2,1,0:T(8,128)(2,1)} %get-tuple-element.17), calls=%async_computation | async-start | bytes 3145728 | tf_op jit(solution)/shard_map/all_to_all | solution.py:521
  94.5 1.2 copy-start
  104.9 5.7 %collective-permute-start = (f32[64,80,128]{2,1,0:T(8,128)}, f32[64,80,128]{2,1,0:T(8,128)S(1)}, u32[]{:S(2)}, u32[]{:S(2)}) collective-permute-start(f32[64,80,128]{2,1,0:T(8,128)} %get-tuple-element.22), channel_id=1, source_target_pairs={{0,1},{1,0},{2,3},{3,2},{4,5},{5,4},{6,7},{7,6},{8,9},{9,8},{10,11... | collective-permute-start | bytes 7864328 | tf_op jit(solution)/shard_map/ppermute | solution.py:503
  157.4 19.5 %all-to-all-start.3 = ((f32[64,24,128]{2,1,0:T(8,128)}), f32[64,24,128]{2,1,0:T(8,128)S(1)}, u32[]{:S(2)}, u32[]{:S(2)}) async-start(f32[64,24,128]{2,1,0:T(8,128)} %broadcast_in_dim.5), calls=%async_computation.3 | async-start | bytes 1572864 | tf_op jit(solution)/shard_map/all_to_all | solution.py:507
  176.9 4.5 %copy-start.2 = (f32[64,24,128]{2,1,0:T(8,128)}, f32[64,24,128]{2,1,0:T(8,128)S(1)}, u32[]{:S(2)}) copy-start(f32[64,24,128]{2,1,0:T(8,128)S(1)} %all-to-all-done.3) | copy-start | bytes 2359300
  178.3 7.8 %collective-permute-start.1 = (f32[12,128,128]{2,1,0:T(8,128)S(1)}, f32[12,128,128]{2,1,0:T(8,128)S(1)}, u32[]{:S(2)}, u32[]{:S(2)}) collective-permute-start(f32[12,128,128]{2,1,0:T(8,128)S(1)} %bitcast.13), channel_id=1, source_target_pairs={{0,1},{1,0},{2,3},{3,2},{4,5},{5,4},{6,7},{7,6},{8,9},{9,8},{10,11... | collective-permute-start | bytes 2359304 | tf_op jit(solution)/shard_map/ppermute | solution.py:503
  181.4 31.1 %all-to-all-start.4 = ((f32[64,56,128]{2,1,0:T(8,128)}), f32[64,56,128]{2,1,0:T(8,128)S(1)}, u32[]{:S(2)}, u32[]{:S(2)}) async-start(f32[64,56,128]{2,1,0:T(8,128)} %broadcast_in_dim.4), calls=%async_computation.4 | async-start | bytes 3670016 | tf_op jit(solution)/shard_map/all_to_all | solution.py:507
  186.1 0.9 copy-start.4
  212.5 4.7 %copy-start.1 = (f32[64,56,128]{2,1,0:T(8,128)}, f32[64,56,128]{2,1,0:T(8,128)S(1)}, u32[]{:S(2)}) copy-start(f32[64,56,128]{2,1,0:T(8,128)S(1)} %all-to-all-done.4) | copy-start | bytes 5505028
  212.5 4.7 %collective-permute-start.2 = (f32[28,128,128]{2,1,0:T(8,128)S(1)}, f32[28,128,128]{2,1,0:T(8,128)S(1)}, u32[]{:S(2)}, u32[]{:S(2)}) collective-permute-start(f32[28,128,128]{2,1,0:T(8,128)S(1)} %bitcast.11), channel_id=1, source_target_pairs={{0,1},{1,0},{2,3},{3,2},{4,5},{5,4},{6,7},{7,6},{8,9},{9,8},{10,11... | collective-permute-start | bytes 5505032 | tf_op jit(solution)/shard_map/ppermute | solution.py:503
  217.2 1.2 copy-start.3

commit v7 on v6

--- a/solution.py
+++ b/solution.py
@@ -16,7 +16,8 @@
 GAUGE_AXES = ("y", "core")
 PLANE_AXES = ("z", "x", "y")
 HIGHEST = lax.Precision.HIGHEST
-VMEM_BYTES = 56 * 1024 * 1024
+VMEM_BYTES = 54 * 1024 * 1024
+GRAM_BYTES = 50 * 1024 * 1024
 
 
 class Layout:
@@ -183,8 +184,11 @@
 def gram_chunk(layout, core, arms, ft, angles, so_far):
     cols, samples = ft.shape
     run = (layout.plane, sum(layout.share), TILE)
-    shape = jax.ShapeDtypeStruct(run, jnp.float32)
     anywhere = pl.BlockSpec(memory_space=pl.ANY)
+    if so_far is None:
+        shape, place = jax.ShapeDtypeStruct(run, jnp.float32), anywhere
+    else:
+        shape, place = pltpu.VMEM(run, jnp.float32), pl.BlockSpec(memory_space=pltpu.VMEM)
     return pl.pallas_call(
         functools.partial(gram_kernel, layout, so_far is None),
         out_shape=(shape, shape),
@@ -193,20 +197,22 @@
             grid=(angles.shape[0],),
             in_specs=[
                 pl.BlockSpec(arms.shape, lambda g, core: (0, 0)),
-                pl.BlockSpec((cols, samples), lambda g, core: (0, 0)),
+                pl.BlockSpec((cols, samples), lambda g, core: (0, 0))
+                if so_far is None
+                else pl.BlockSpec(memory_space=pltpu.VMEM),
                 pl.BlockSpec(angles.shape, lambda g, core: (0, 0)),
             ]
             + ([] if so_far is None else [anywhere, anywhere]),
-            out_specs=(anywhere, anywhere),
+            out_specs=(place, place),
             scratch_shapes=[
                 pltpu.VMEM((cols, samples), jnp.bfloat16),
                 pltpu.VMEM((CORES, *run), jnp.float32),
                 pltpu.SemaphoreType.DMA((2,)),
             ],
         ),
-        compiler_params=pltpu.CompilerParams(vmem_limit_bytes=VMEM_BYTES),
+        compiler_params=pltpu.CompilerParams(vmem_limit_bytes=VMEM_BYTES if so_far is None else GRAM_BYTES),
         name="rotate_gram",
-    )(core, arms, ft, angles, *(() if so_far is None else so_far))
+    )(core, arms, ft if so_far is None else pltpu.with_memory_space_constraint(ft, pltpu.VMEM), angles, *(() if so_far is None else so_far))
 
 
 def split3(x):
@@ -466,7 +472,9 @@
     size = layout.nb * TILE
     leading = so_far is None
     anywhere = pl.BlockSpec(memory_space=pl.ANY)
-    sources = [x for pair in groups for x in pair] + ([] if leading else list(so_far))
+    sources = [pltpu.with_memory_space_constraint(x, pltpu.VMEM) for pair in groups for x in pair]
+    n_blocks = len(sources)
+    sources += [] if leading else list(so_far)
     factor = jax.ShapeDtypeStruct((size, size), jnp.float32)
     inverses = jax.ShapeDtypeStruct((layout.lead, TILE, TILE), jnp.float32)
     blocks = layout.lead if leading else layout.nb - layout.lead
@@ -476,7 +484,8 @@
         grid_spec=pltpu.PrefetchScalarGridSpec(
             num_scalar_prefetch=1,
             grid=(1,),
-            in_specs=[anywhere] * len(sources),
+            in_specs=[pl.BlockSpec(memory_space=pltpu.VMEM)] * n_blocks
+            + [anywhere] * (len(sources) - n_blocks),
             out_specs=(anywhere, anywhere) if leading else anywhere,
             scratch_shapes=[
                 pltpu.VMEM((size, size), jnp.float32),

time: 255 us -> 247 us (0.969)
  Pallas kernels: 95.2 us -> 90.8 us
  local copies, waits for them, and re-layouts: 5.78 us -> 2.32 us
    unnamed x10 -> x0, local copies, waits for them, and re-layouts: 3.4 us -> none
    pallas_call x2, Pallas kernels: 27.6 us -> 25 us  [gram_chunk(): pl.pallas_call(functools.partial(gram_kernel, layout, so_far is None), ou...]
where the time goes in v7:
time: 247 us; the launch traced here: 246 us
  blocking collectives  105 us (43%)
  Pallas kernels  90.8 us (37%)
  waiting for transfers between devices  27.6 us (11%)
  starting transfers between devices  20.1 us (8%)
    all_to_all x1, blocking collectives, shards(): lax.all_to_all(filtered, GAUGE_AXES, split_axis=0, concat_axis=0, tiled=T...  61.1 us
    pallas_call x2, Pallas kernels, cholesky_part(): pl.pallas_call(functools.partial(cholesky_kernel, layout, scale, leading)...  57.7 us
    all_to_all x1, blocking collectives, shards(): lax.all_to_all(mine, PLANE_AXES, split_axis=0, concat_axis=0, tiled=True)  43.6 us
    pallas_call x2, Pallas kernels, gram_chunk(): pl.pallas_call(functools.partial(gram_kernel, layout, so_far is None), ou...  25 us
    all_to_all x2, waiting for transfers between devices, gather_plane(): lax.all_to_all(copies, PLANE_AXES, split_axis=0, concat_axis=0, tiled=True)  17.3 us
    all_to_all x2, starting transfers between devices, gather_plane(): lax.all_to_all(copies, PLANE_AXES, split_axis=0, concat_axis=0, tiled=True)  10.3 us
    pallas_call x1, Pallas kernels, filter_records(): pl.pallas_call(filter_kernel, out_shape=tuple((jax.ShapeDtypeStruct((part...  8.2 us
    ppermute x3, waiting for transfers between devices, swap_cores(): return lax.ppermute(x, 'core', [(0, 1), (1, 0)])  7.95 us
  transfers between devices with their start and end apart: 6, of which 5 were waited for; matrix products, arithmetic and copies ran while one was open for 0% of the time, Pallas kernels for 17%

profile of v7, /device:TPU:1, one launch (start us, length us, event | category | flops | bytes accessed | tf_op | source)
XLA Modules:
  0.0 246.3 jit_solution(16561144254656207072)
XLA Ops:
  0.0 8.2 %drift_filter.1 = (bf16[8,192,1536]{2,1,0:T(8,128)(2,1)}, bf16[8,192,512]{2,1,0:T(8,128)(2,1)}) custom-call(s32[16]{0:T(128)} %offsets.1, bf16[192,16384]{1,0:T(8,128)(2,1)} %bitcast.15), custom_call_target="tpu_custom_call" | custom-call | tf_op jit(solution)/shard_map/drift_filter/pallas_call | solution.py:80
  8.2 61.1 %all_to_all.25 = bf16[8,192,1536]{2,1,0:T(8,128)(2,1)} all-to-all(bf16[8,192,1536]{2,1,0:T(8,128)(2,1)} %get-tuple-element.18), channel_id=1, replica_groups=mesh['z'=4,'x'=4,'y'=4,'core'=2] {'y','core'}, dimensions={0} | all-to-all | bytes 9437184 | tf_op jit(solution)/shard_map/all_to_all | solution.py:530
  69.3 4.5 %all-to-all-start = ((bf16[8,192,512]{2,1,0:T(8,128)(2,1)}), bf16[8,192,512]{2,1,0:T(8,128)(2,1)S(1)}, u32[]{:S(2)}, u32[]{:S(2)}) async-start(bf16[8,192,512]{2,1,0:T(8,128)(2,1)} %get-tuple-element.17), calls=%async_computation | async-start | bytes 3145728 | tf_op jit(solution)/shard_map/all_to_all | solution.py:530
  73.8 18.4 %rotate_gram.2 = (f32[64,80,128]{2,1,0:T(8,128)}, f32[64,80,128]{2,1,0:T(8,128)}) custom-call(s32[1]{0:T(128)} %bitcast.core, s32[12,128]{1,0:T(8,128)} %bitcast.16, bf16[1536,1536]{1,0:T(8,128)(2,1)} %bitcast.14, f32[4,128]{1,0:T(4,128)} %bitcast.18), custom_call_target="tpu_custom_call" | custom-call | tf_op jit(solution)/shard_map/rotate_gram/pallas_call | solution.py:192
  92.2 2.3 all-to-all-done
  94.5 6.5 %rotate_gram.3 = (f32[64,80,128]{2,1,0:T(8,128)S(1)}, f32[64,80,128]{2,1,0:T(8,128)S(1)}) custom-call(s32[1]{0:T(128)} %bitcast.core, s32[12,128]{1,0:T(8,128)} %bitcast.17, bf16[1536,512]{1,0:T(8,128)(2,1)S(1)} %bitcast.8, f32[4,128]{1,0:T(4,128)} %bitcast.19, f32[64,80,128]{2,1,0:T(8,128)} %get-tuple-element.19.refs_3_, ...), custom_call_target="tpu_custom_call" | custom-call | tf_op jit(solution)/shard_map/rotate_gram/pallas_call | solution.py:192
  101.1 1.0 collective-permute-start
  102.0 4.5 %collective-permute-done = f32[64,80,128]{2,1,0:T(8,128)S(1)} collective-permute-done((f32[64,80,128]{2,1,0:T(8,128)S(1)}, f32[64,80,128]{2,1,0:T(8,128)S(1)}, u32[]{:S(2)}, u32[]{:S(2)}) %collective-permute-start) | collective-permute-done | bytes 2621472 | tf_op jit(solution)/shard_map/ppermute | solution.py:512
  106.6 0.3 add.3
  106.9 43.6 %all_to_all.26 = f32[64,80,128]{2,1,0:T(8,128)S(1)} all-to-all(f32[64,80,128]{2,1,0:T(8,128)S(1)} %add.3), channel_id=1, replica_groups=mesh['z'=4,'x'=4,'y'=4,'core'=2] {'z','x','y'}, dimensions={0} | all-to-all | bytes 5242880 | tf_op jit(solution)/shard_map/all_to_all | solution.py:534
  150.5 0.2 reduce_sum.9
  150.7 0.9 broadcast_in_dim.5
  151.6 5.6 %all-to-all-start.3 = ((f32[64,24,128]{2,1,0:T(8,128)}), f32[64,24,128]{2,1,0:T(8,128)S(1)}, u32[]{:S(2)}, u32[]{:S(2)}) async-start(f32[64,24,128]{2,1,0:T(8,128)} %broadcast_in_dim.5), calls=%async_computation.3 | async-start | bytes 1572864 | tf_op jit(solution)/shard_map/all_to_all | solution.py:516
  157.3 13.9 %all-to-all-done.3 = f32[64,24,128]{2,1,0:T(8,128)S(1)} async-done(((f32[64,24,128]{2,1,0:T(8,128)}), f32[64,24,128]{2,1,0:T(8,128)S(1)}, u32[]{:S(2)}, u32[]{:S(2)}) %all-to-all-start.3) | async-done | bytes 786464 | tf_op jit(solution)/shard_map/all_to_all | solution.py:516
  171.1 1.4 broadcast_in_dim.4
  172.5 3.1 %collective-permute-start.1 = (f32[12,128,128]{2,1,0:T(8,128)S(1)}, f32[12,128,128]{2,1,0:T(8,128)S(1)}, u32[]{:S(2)}, u32[]{:S(2)}) collective-permute-start(f32[12,128,128]{2,1,0:T(8,128)S(1)} %bitcast.11), channel_id=1, source_target_pairs={{0,1},{1,0},{2,3},{3,2},{4,5},{5,4},{6,7},{7,6},{8,9},{9,8},{10,11... | collective-permute-start | bytes 2359304 | tf_op jit(solution)/shard_map/ppermute | solution.py:512
  175.6 4.7 %all-to-all-start.4 = ((f32[64,56,128]{2,1,0:T(8,128)}), f32[64,56,128]{2,1,0:T(8,128)S(1)}, u32[]{:S(2)}, u32[]{:S(2)}) async-start(f32[64,56,128]{2,1,0:T(8,128)} %broadcast_in_dim.4), calls=%async_computation.4 | async-start | bytes 3670016 | tf_op jit(solution)/shard_map/all_to_all | solution.py:516
  180.3 0.0 collective-permute-done.1.refs_1_
  180.3 22.9 %cholesky.2 = (f32[1536,1536]{1,0:T(8,128)}, f32[6,128,128]{2,1,0:T(8,128)}) custom-call(s32[1]{0:T(128)} %bitcast.core, f32[12,128,128]{2,1,0:T(8,128)S(1)} %bitcast.12, f32[12,128,128]{2,1,0:T(8,128)S(1)} %collective-permute-done.1.refs_1_), custom_call_target="tpu_custom_call" | custom-call | flops 72477573120 | bytes 28311552 | tf_op jit(solution)/shard_map/cholesky/pallas_call | solution.py:481
  203.2 3.4 %all-to-all-done.4 = f32[64,56,128]{2,1,0:T(8,128)S(1)} async-done(((f32[64,56,128]{2,1,0:T(8,128)}), f32[64,56,128]{2,1,0:T(8,128)S(1)}, u32[]{:S(2)}, u32[]{:S(2)}) %all-to-all-start.4) | async-done | bytes 1835040 | tf_op jit(solution)/shard_map/all_to_all | solution.py:516
  206.7 1.3 collective-permute-start.2
  207.9 3.4 %collective-permute-done.2.refs_3_ = f32[28,128,128]{2,1,0:T(8,128)S(1)} collective-permute-done((f32[28,128,128]{2,1,0:T(8,128)S(1)}, f32[28,128,128]{2,1,0:T(8,128)S(1)}, u32[]{:S(2)}, u32[]{:S(2)}) %collective-permute-start.2) | collective-permute-done | bytes 1835040 | tf_op jit(solution)/shard_map/ppermute | solution.py:512
  211.3 34.7 %cholesky.3 = f32[1536,1536]{1,0:T(8,128)} custom-call(s32[1]{0:T(128)} %bitcast.core, f32[12,128,128]{2,1,0:T(8,128)S(1)} %bitcast.13, f32[12,128,128]{2,1,0:T(8,128)S(1)} %collective-permute-done.1.refs_1_, f32[28,128,128]{2,1,0:T(8,128)S(1)} %bitcast.10, f32[28,128,128]{2,1,0:T(8,128)S(1)} %collective-permute-done.2.refs_3_, ...), custom_call_target="tpu_custom_call", output_to_operand_aliasing={{}: (5, {})} | custom-call | flops 72477573120 | bytes 28311552 | tf_op jit(solution)/shard_map/cholesky/pallas_call | solution.py:481
  (2 shorter events, 0.0 us)
Async XLA Ops:
  69.3 25.3 %all-to-all-start = ((bf16[8,192,512]{2,1,0:T(8,128)(2,1)}), bf16[8,192,512]{2,1,0:T(8,128)(2,1)S(1)}, u32[]{:S(2)}, u32[]{:S(2)}) async-start(bf16[8,192,512]{2,1,0:T(8,128)(2,1)} %get-tuple-element.17), calls=%async_computation | async-start | bytes 3145728 | tf_op jit(solution)/shard_map/all_to_all | solution.py:530
  101.1 5.5 %collective-permute-start = (f32[64,80,128]{2,1,0:T(8,128)S(1)}, f32[64,80,128]{2,1,0:T(8,128)S(1)}, u32[]{:S(2)}, u32[]{:S(2)}) collective-permute-start(f32[64,80,128]{2,1,0:T(8,128)S(1)} %get-tuple-element.22), channel_id=1, source_target_pairs={{0,1},{1,0},{2,3},{3,2},{4,5},{5,4},{6,7},{7,6},{8,9},{9,8},{10,11... | collective-permute-start | bytes 7864328 | tf_op jit(solution)/shard_map/ppermute | solution.py:512
  151.6 19.5 %all-to-all-start.3 = ((f32[64,24,128]{2,1,0:T(8,128)}), f32[64,24,128]{2,1,0:T(8,128)S(1)}, u32[]{:S(2)}, u32[]{:S(2)}) async-start(f32[64,24,128]{2,1,0:T(8,128)} %broadcast_in_dim.5), calls=%async_computation.3 | async-start | bytes 1572864 | tf_op jit(solution)/shard_map/all_to_all | solution.py:516
  172.5 7.8 %collective-permute-start.1 = (f32[12,128,128]{2,1,0:T(8,128)S(1)}, f32[12,128,128]{2,1,0:T(8,128)S(1)}, u32[]{:S(2)}, u32[]{:S(2)}) collective-permute-start(f32[12,128,128]{2,1,0:T(8,128)S(1)} %bitcast.11), channel_id=1, source_target_pairs={{0,1},{1,0},{2,3},{3,2},{4,5},{5,4},{6,7},{7,6},{8,9},{9,8},{10,11... | collective-permute-start | bytes 2359304 | tf_op jit(solution)/shard_map/ppermute | solution.py:512
  175.6 31.1 %all-to-all-start.4 = ((f32[64,56,128]{2,1,0:T(8,128)}), f32[64,56,128]{2,1,0:T(8,128)S(1)}, u32[]{:S(2)}, u32[]{:S(2)}) async-start(f32[64,56,128]{2,1,0:T(8,128)} %broadcast_in_dim.4), calls=%async_computation.4 | async-start | bytes 3670016 | tf_op jit(solution)/shard_map/all_to_all | solution.py:516
  206.7 4.7 %collective-permute-start.2 = (f32[28,128,128]{2,1,0:T(8,128)S(1)}, f32[28,128,128]{2,1,0:T(8,128)S(1)}, u32[]{:S(2)}, u32[]{:S(2)}) collective-permute-start(f32[28,128,128]{2,1,0:T(8,128)S(1)} %bitcast.9), channel_id=1, source_target_pairs={{0,1},{1,0},{2,3},{3,2},{4,5},{5,4},{6,7},{7,6},{8,9},{9,8},{10,11... | collective-permute-start | bytes 5505032 | tf_op jit(solution)/shard_map/ppermute | solution.py:512

commit v8 on v7

--- a/solution.py
+++ b/solution.py
@@ -18,6 +18,8 @@
 HIGHEST = lax.Precision.HIGHEST
 VMEM_BYTES = 54 * 1024 * 1024
 GRAM_BYTES = 50 * 1024 * 1024
+FILTER_BYTES = 54 * 1024 * 1024
+STEPS = 4
 
 
 class Layout:
@@ -53,10 +55,11 @@
 
 
 def filter_kernel(offsets, x_ref, head_ref, tail_ref):
-    parts, _, split = head_ref.shape
+    parts, split = tail_ref.shape[0], head_ref.shape[2]
+    step = pl.program_id(0)
     blocks = x_ref.shape[1] // BLOCK // parts
     for b in range(parts * blocks):
-        start = offsets[pl.program_id(0) * parts * blocks + b]
+        start = offsets[step * parts * blocks + b]
         x = x_ref[:, b * BLOCK : (b + 1) * BLOCK]
         sample = lax.broadcasted_iota(jnp.int32, (1, BLOCK), 1)
         inside = jnp.where((sample >= start) & (sample < start + BAND), 1.0, 0.0)
@@ -66,7 +69,7 @@
             value = (x[:, t : t + TILE].astype(jnp.float32) - baseline).astype(jnp.bfloat16)
             here = b % blocks * BLOCK + t
             if here < split:
-                head_ref[b // blocks, :, here : here + TILE] = value
+                head_ref[step * parts + b // blocks, :, here : here + TILE] = value
             else:
                 tail_ref[b // blocks, :, here - split : here - split + TILE] = value
 
@@ -75,20 +78,22 @@
     rows, samples = records_t.shape
     each = samples // parts
     tail = BLOCK // 2
-    widths = (each - tail, tail)
-    per = 2
     return pl.pallas_call(
         filter_kernel,
-        out_shape=tuple(jax.ShapeDtypeStruct((parts, rows, w), jnp.bfloat16) for w in widths),
+        out_shape=(
+            pltpu.VMEM((parts, rows, each - tail), jnp.bfloat16),
+            jax.ShapeDtypeStruct((parts, rows, tail), jnp.bfloat16),
+        ),
         grid_spec=pltpu.PrefetchScalarGridSpec(
             num_scalar_prefetch=1,
-            grid=(parts // per,),
-            in_specs=[pl.BlockSpec((rows, per * each), lambda d, off: (0, d))],
-            out_specs=tuple(
-                pl.BlockSpec((per, rows, w), lambda d, off: (d, 0, 0)) for w in widths
+            grid=(STEPS,),
+            in_specs=[pl.BlockSpec((rows, samples // STEPS), lambda d, off: (0, d))],
+            out_specs=(
+                pl.BlockSpec(memory_space=pltpu.VMEM),
+                pl.BlockSpec((parts // STEPS, rows, tail), lambda d, off: (d, 0, 0)),
             ),
         ),
-        compiler_params=pltpu.CompilerParams(vmem_limit_bytes=VMEM_BYTES),
+        compiler_params=pltpu.CompilerParams(vmem_limit_bytes=FILTER_BYTES),
         name="drift_filter",
     )(offsets, records_t)
 

time: 247 us -> 245 us (level)
  no operation moved by 1% of the time
where the time goes in v8:
time: 245 us
  blocking collectives  104 us (42%)
  Pallas kernels  89.7 us (37%)
  waiting for transfers between devices  27.5 us (11%)
  starting transfers between devices  20.1 us (8%)
    all_to_all x1, blocking collectives, shards(): lax.all_to_all(filtered, GAUGE_AXES, split_axis=0, concat_axis=0, tiled=T...  60.9 us
    pallas_call x2, Pallas kernels, cholesky_part(): pl.pallas_call(functools.partial(cholesky_kernel, layout, scale, leading)...  57.7 us
    all_to_all x1, blocking collectives, shards(): lax.all_to_all(mine, PLANE_AXES, split_axis=0, concat_axis=0, tiled=True)  43.6 us
    pallas_call x2, Pallas kernels, gram_chunk(): pl.pallas_call(functools.partial(gram_kernel, layout, so_far is None), ou...  25 us
    all_to_all x2, waiting for transfers between devices, gather_plane(): lax.all_to_all(copies, PLANE_AXES, split_axis=0, concat_axis=0, tiled=True)  17.3 us
    all_to_all x2, starting transfers between devices, gather_plane(): lax.all_to_all(copies, PLANE_AXES, split_axis=0, concat_axis=0, tiled=True)  10.3 us
    ppermute x3, waiting for transfers between devices, swap_cores(): return lax.ppermute(x, 'core', [(0, 1), (1, 0)])  7.95 us
    pallas_call x1, Pallas kernels, filter_records(): pl.pallas_call(filter_kernel, out_shape=(pltpu.VMEM((parts, rows, each -...  7.03 us
  transfers between devices with their start and end apart: 6, of which 5 were waited for; matrix products, arithmetic and copies ran while one was open for 0% of the time, Pallas kernels for 17%

profile of v8, /device:TPU:1, one launch (start us, length us, event | category | flops | bytes accessed | tf_op | source)
XLA Modules:
  0.0 244.9 jit_solution(10533062027065374463)
XLA Ops:
  0.0 7.0 %drift_filter.1 = (bf16[8,192,1536]{2,1,0:T(8,128)(2,1)S(1)}, bf16[8,192,512]{2,1,0:T(8,128)(2,1)}) custom-call(s32[16]{0:T(128)} %offsets.1, bf16[192,16384]{1,0:T(8,128)(2,1)} %bitcast.15), custom_call_target="tpu_custom_call" | custom-call | tf_op jit(solution)/shard_map/drift_filter/pallas_call | solution.py:81
  7.0 60.9 %all_to_all.25 = bf16[8,192,1536]{2,1,0:T(8,128)(2,1)} all-to-all(bf16[8,192,1536]{2,1,0:T(8,128)(2,1)S(1)} %get-tuple-element.18), channel_id=1, replica_groups=mesh['z'=4,'x'=4,'y'=4,'core'=2] {'y','core'}, dimensions={0} | all-to-all | bytes 9437184 | tf_op jit(solution)/shard_map/all_to_all | solution.py:535
  67.9 4.5 %all-to-all-start = ((bf16[8,192,512]{2,1,0:T(8,128)(2,1)}), bf16[8,192,512]{2,1,0:T(8,128)(2,1)S(1)}, u32[]{:S(2)}, u32[]{:S(2)}) async-start(bf16[8,192,512]{2,1,0:T(8,128)(2,1)} %get-tuple-element.17), calls=%async_computation | async-start | bytes 3145728 | tf_op jit(solution)/shard_map/all_to_all | solution.py:535
  72.4 18.4 %rotate_gram.2 = (f32[64,80,128]{2,1,0:T(8,128)}, f32[64,80,128]{2,1,0:T(8,128)}) custom-call(s32[1]{0:T(128)} %bitcast.core, s32[12,128]{1,0:T(8,128)} %bitcast.16, bf16[1536,1536]{1,0:T(8,128)(2,1)} %bitcast.14, f32[4,128]{1,0:T(4,128)} %bitcast.18), custom_call_target="tpu_custom_call" | custom-call | tf_op jit(solution)/shard_map/rotate_gram/pallas_call | solution.py:197
  90.9 2.3 all-to-all-done
  93.2 6.5 %rotate_gram.3 = (f32[64,80,128]{2,1,0:T(8,128)S(1)}, f32[64,80,128]{2,1,0:T(8,128)S(1)}) custom-call(s32[1]{0:T(128)} %bitcast.core, s32[12,128]{1,0:T(8,128)} %bitcast.17, bf16[1536,512]{1,0:T(8,128)(2,1)S(1)} %bitcast.8, f32[4,128]{1,0:T(4,128)} %bitcast.19, f32[64,80,128]{2,1,0:T(8,128)} %get-tuple-element.19.refs_3_, ...), custom_call_target="tpu_custom_call" | custom-call | tf_op jit(solution)/shard_map/rotate_gram/pallas_call | solution.py:197
  99.7 1.0 collective-permute-start
  100.7 4.5 %collective-permute-done = f32[64,80,128]{2,1,0:T(8,128)S(1)} collective-permute-done((f32[64,80,128]{2,1,0:T(8,128)S(1)}, f32[64,80,128]{2,1,0:T(8,128)S(1)}, u32[]{:S(2)}, u32[]{:S(2)}) %collective-permute-start) | collective-permute-done | bytes 2621472 | tf_op jit(solution)/shard_map/ppermute | solution.py:517
  105.2 0.3 add.3
  105.5 43.6 %all_to_all.26 = f32[64,80,128]{2,1,0:T(8,128)S(1)} all-to-all(f32[64,80,128]{2,1,0:T(8,128)S(1)} %add.3), channel_id=1, replica_groups=mesh['z'=4,'x'=4,'y'=4,'core'=2] {'z','x','y'}, dimensions={0} | all-to-all | bytes 5242880 | tf_op jit(solution)/shard_map/all_to_all | solution.py:539
  149.1 0.2 reduce_sum.9
  149.3 0.9 broadcast_in_dim.5
  150.2 5.6 %all-to-all-start.3 = ((f32[64,24,128]{2,1,0:T(8,128)}), f32[64,24,128]{2,1,0:T(8,128)S(1)}, u32[]{:S(2)}, u32[]{:S(2)}) async-start(f32[64,24,128]{2,1,0:T(8,128)} %broadcast_in_dim.5), calls=%async_computation.3 | async-start | bytes 1572864 | tf_op jit(solution)/shard_map/all_to_all | solution.py:521
  155.9 13.9 %all-to-all-done.3 = f32[64,24,128]{2,1,0:T(8,128)S(1)} async-done(((f32[64,24,128]{2,1,0:T(8,128)}), f32[64,24,128]{2,1,0:T(8,128)S(1)}, u32[]{:S(2)}, u32[]{:S(2)}) %all-to-all-start.3) | async-done | bytes 786464 | tf_op jit(solution)/shard_map/all_to_all | solution.py:521
  169.8 1.4 broadcast_in_dim.4
  171.1 3.1 %collective-permute-start.1 = (f32[12,128,128]{2,1,0:T(8,128)S(1)}, f32[12,128,128]{2,1,0:T(8,128)S(1)}, u32[]{:S(2)}, u32[]{:S(2)}) collective-permute-start(f32[12,128,128]{2,1,0:T(8,128)S(1)} %bitcast.11), channel_id=1, source_target_pairs={{0,1},{1,0},{2,3},{3,2},{4,5},{5,4},{6,7},{7,6},{8,9},{9,8},{10,11... | collective-permute-start | bytes 2359304 | tf_op jit(solution)/shard_map/ppermute | solution.py:517
  174.2 4.7 %all-to-all-start.4 = ((f32[64,56,128]{2,1,0:T(8,128)}), f32[64,56,128]{2,1,0:T(8,128)S(1)}, u32[]{:S(2)}, u32[]{:S(2)}) async-start(f32[64,56,128]{2,1,0:T(8,128)} %broadcast_in_dim.4), calls=%async_computation.4 | async-start | bytes 3670016 | tf_op jit(solution)/shard_map/all_to_all | solution.py:521
  178.9 0.0 collective-permute-done.1.refs_1_
  178.9 22.9 %cholesky.2 = (f32[1536,1536]{1,0:T(8,128)}, f32[6,128,128]{2,1,0:T(8,128)}) custom-call(s32[1]{0:T(128)} %bitcast.core, f32[12,128,128]{2,1,0:T(8,128)S(1)} %bitcast.12, f32[12,128,128]{2,1,0:T(8,128)S(1)} %collective-permute-done.1.refs_1_), custom_call_target="tpu_custom_call" | custom-call | flops 72477573120 | bytes 28311552 | tf_op jit(solution)/shard_map/cholesky/pallas_call | solution.py:486
  201.9 3.4 %all-to-all-done.4 = f32[64,56,128]{2,1,0:T(8,128)S(1)} async-done(((f32[64,56,128]{2,1,0:T(8,128)}), f32[64,56,128]{2,1,0:T(8,128)S(1)}, u32[]{:S(2)}, u32[]{:S(2)}) %all-to-all-start.4) | async-done | bytes 1835040 | tf_op jit(solution)/shard_map/all_to_all | solution.py:521
  205.3 1.3 collective-permute-start.2
  206.6 3.4 %collective-permute-done.2.refs_3_ = f32[28,128,128]{2,1,0:T(8,128)S(1)} collective-permute-done((f32[28,128,128]{2,1,0:T(8,128)S(1)}, f32[28,128,128]{2,1,0:T(8,128)S(1)}, u32[]{:S(2)}, u32[]{:S(2)}) %collective-permute-start.2) | collective-permute-done | bytes 1835040 | tf_op jit(solution)/shard_map/ppermute | solution.py:517
  210.0 34.7 %cholesky.3 = f32[1536,1536]{1,0:T(8,128)} custom-call(s32[1]{0:T(128)} %bitcast.core, f32[12,128,128]{2,1,0:T(8,128)S(1)} %bitcast.13, f32[12,128,128]{2,1,0:T(8,128)S(1)} %collective-permute-done.1.refs_1_, f32[28,128,128]{2,1,0:T(8,128)S(1)} %bitcast.10, f32[28,128,128]{2,1,0:T(8,128)S(1)} %collective-permute-done.2.refs_3_, ...), custom_call_target="tpu_custom_call", output_to_operand_aliasing={{}: (5, {})} | custom-call | flops 72477573120 | bytes 28311552 | tf_op jit(solution)/shard_map/cholesky/pallas_call | solution.py:486
  (2 shorter events, 0.0 us)
Async XLA Ops:
  67.9 25.3 %all-to-all-start = ((bf16[8,192,512]{2,1,0:T(8,128)(2,1)}), bf16[8,192,512]{2,1,0:T(8,128)(2,1)S(1)}, u32[]{:S(2)}, u32[]{:S(2)}) async-start(bf16[8,192,512]{2,1,0:T(8,128)(2,1)} %get-tuple-element.17), calls=%async_computation | async-start | bytes 3145728 | tf_op jit(solution)/shard_map/all_to_all | solution.py:535
  99.7 5.5 %collective-permute-start = (f32[64,80,128]{2,1,0:T(8,128)S(1)}, f32[64,80,128]{2,1,0:T(8,128)S(1)}, u32[]{:S(2)}, u32[]{:S(2)}) collective-permute-start(f32[64,80,128]{2,1,0:T(8,128)S(1)} %get-tuple-element.22), channel_id=1, source_target_pairs={{0,1},{1,0},{2,3},{3,2},{4,5},{5,4},{6,7},{7,6},{8,9},{9,8},{10,11... | collective-permute-start | bytes 7864328 | tf_op jit(solution)/shard_map/ppermute | solution.py:517
  150.2 19.5 %all-to-all-start.3 = ((f32[64,24,128]{2,1,0:T(8,128)}), f32[64,24,128]{2,1,0:T(8,128)S(1)}, u32[]{:S(2)}, u32[]{:S(2)}) async-start(f32[64,24,128]{2,1,0:T(8,128)} %broadcast_in_dim.5), calls=%async_computation.3 | async-start | bytes 1572864 | tf_op jit(solution)/shard_map/all_to_all | solution.py:521
  171.1 7.8 %collective-permute-start.1 = (f32[12,128,128]{2,1,0:T(8,128)S(1)}, f32[12,128,128]{2,1,0:T(8,128)S(1)}, u32[]{:S(2)}, u32[]{:S(2)}) collective-permute-start(f32[12,128,128]{2,1,0:T(8,128)S(1)} %bitcast.11), channel_id=1, source_target_pairs={{0,1},{1,0},{2,3},{3,2},{4,5},{5,4},{6,7},{7,6},{8,9},{9,8},{10,11... | collective-permute-start | bytes 2359304 | tf_op jit(solution)/shard_map/ppermute | solution.py:517
  174.2 31.1 %all-to-all-start.4 = ((f32[64,56,128]{2,1,0:T(8,128)}), f32[64,56,128]{2,1,0:T(8,128)S(1)}, u32[]{:S(2)}, u32[]{:S(2)}) async-start(f32[64,56,128]{2,1,0:T(8,128)} %broadcast_in_dim.4), calls=%async_computation.4 | async-start | bytes 3670016 | tf_op jit(solution)/shard_map/all_to_all | solution.py:521
  205.3 4.7 %collective-permute-start.2 = (f32[28,128,128]{2,1,0:T(8,128)S(1)}, f32[28,128,128]{2,1,0:T(8,128)S(1)}, u32[]{:S(2)}, u32[]{:S(2)}) collective-permute-start(f32[28,128,128]{2,1,0:T(8,128)S(1)} %bitcast.9), channel_id=1, source_target_pairs={{0,1},{1,0},{2,3},{3,2},{4,5},{5,4},{6,7},{7,6},{8,9},{9,8},{10,11... | collective-permute-start | bytes 5505032 | tf_op jit(solution)/shard_map/ppermute | solution.py:517

commit v9 on v8

--- a/solution.py
+++ b/solution.py
@@ -517,6 +517,35 @@
     return lax.ppermute(x, "core", [(0, 1), (1, 0)])
 
 
+def sum_kernel(x_ref, early_ref, late_ref):
+    total = x_ref[0]
+    for chip in range(1, x_ref.shape[0]):
+        total = total + x_ref[chip]
+    split = early_ref.shape[1]
+    for chip in range(x_ref.shape[0]):
+        early_ref[chip] = total[:split]
+        late_ref[chip] = total[split:]
+
+
+def sum_and_copy(layout, spread):
+    here = pl.BlockSpec(memory_space=pltpu.VMEM)
+    return pl.pallas_call(
+        sum_kernel,
+        out_shape=(
+            pltpu.VMEM((layout.plane, layout.share[0], TILE), jnp.float32),
+            jax.ShapeDtypeStruct((layout.plane, layout.share[1], TILE), jnp.float32),
+        ),
+        grid=(1,),
+        in_specs=[here],
+        out_specs=(
+            here,
+            pl.BlockSpec((layout.plane, layout.share[1], TILE), lambda g: (0, 0, 0)),
+        ),
+        compiler_params=pltpu.CompilerParams(vmem_limit_bytes=GRAM_BYTES),
+        name="sum_and_copy",
+    )(pltpu.with_memory_space_constraint(spread, pltpu.VMEM))
+
+
 def gather_plane(copies):
     return lax.all_to_all(copies, PLANE_AXES, split_axis=0, concat_axis=0, tiled=True)
 
@@ -536,12 +565,9 @@
         acc = gram_chunk(layout, core, arms, regrouped.reshape(cols, -1), angles, acc)
     mine, other = acc
     mine = mine + swap_cores(other)
-    spread = lax.all_to_all(mine, PLANE_AXES, split_axis=0, concat_axis=0, tiled=True).sum(0)
+    spread = lax.all_to_all(mine, PLANE_AXES, split_axis=0, concat_axis=0, tiled=True)
     scale = 1.0 / (rows * lax.axis_size(SAMPLE_AXES))
-    early, late = (
-        jnp.broadcast_to(x[None], (layout.plane, *x.shape))
-        for x in jnp.split(spread, [layout.share[0]])
-    )
+    early, late = sum_and_copy(layout, spread)
     early = gather_plane(early)
     late, early = lax.optimization_barrier((late, early))
     late = gather_plane(late)

time: 245 us -> 244 us (level)
  blocking collectives: 104 us -> 124 us
  waiting for transfers between devices: 27.5 us -> 13.7 us
  starting transfers between devices: 20.1 us -> 14.7 us
    all_to_all x0 -> x1, blocking collectives: none -> 19.3 us  [gather_plane(): lax.all_to_all(copies, PLANE_AXES, split_axis=0, concat_axis=0, tiled=True)]
    all_to_all x2 -> x1, waiting for transfers between devices: 17.3 us -> 3.42 us  [gather_plane(): lax.all_to_all(copies, PLANE_AXES, split_axis=0, concat_axis=0, tiled=True)]
    all_to_all x2 -> x1, starting transfers between devices: 10.3 us -> 4.86 us  [gather_plane(): lax.all_to_all(copies, PLANE_AXES, split_axis=0, concat_axis=0, tiled=True)]
  transfers between devices with their start and end apart: 6 -> 5, of which waited for: 5 -> 4; matrix products, arithmetic and copies ran while one was open for 0% -> 0% of each run, Pallas kernels for 17% -> 17%
where the time goes in v9:
time: 244 us
  blocking collectives  124 us (51%)
  Pallas kernels  91.2 us (37%)
  starting transfers between devices  14.7 us (6%)
  waiting for transfers between devices  13.7 us (6%)
    all_to_all x1, blocking collectives, shards(): lax.all_to_all(filtered, GAUGE_AXES, split_axis=0, concat_axis=0, tiled=T...  60.9 us
    pallas_call x2, Pallas kernels, cholesky_part(): pl.pallas_call(functools.partial(cholesky_kernel, layout, scale, leading)...  57.7 us
    all_to_all x1, blocking collectives, shards(): lax.all_to_all(mine, PLANE_AXES, split_axis=0, concat_axis=0, tiled=True)  43.6 us
    pallas_call x2, Pallas kernels, gram_chunk(): pl.pallas_call(functools.partial(gram_kernel, layout, so_far is None), ou...  25 us
    all_to_all x1, blocking collectives, gather_plane(): lax.all_to_all(copies, PLANE_AXES, split_axis=0, concat_axis=0, tiled=True)  19.3 us
    ppermute x3, waiting for transfers between devices, swap_cores(): return lax.ppermute(x, 'core', [(0, 1), (1, 0)])  7.95 us
    pallas_call x1, Pallas kernels, filter_records(): pl.pallas_call(filter_kernel, out_shape=(pltpu.VMEM((parts, rows, each -...  7.04 us
    ppermute x3, starting transfers between devices, swap_cores(): return lax.ppermute(x, 'core', [(0, 1), (1, 0)])  5.3 us
  transfers between devices with their start and end apart: 5, of which 4 were waited for; matrix products, arithmetic and copies ran while one was open for 0% of the time, Pallas kernels for 17%

profile of v9, /device:TPU:1, one launch (start us, length us, event | category | flops | bytes accessed | tf_op | source)
XLA Modules:
  0.0 243.8 jit_solution(17782646217809220618)
XLA Ops:
  0.0 7.0 %drift_filter.1 = (bf16[8,192,1536]{2,1,0:T(8,128)(2,1)S(1)}, bf16[8,192,512]{2,1,0:T(8,128)(2,1)}) custom-call(s32[16]{0:T(128)} %offsets.1, bf16[192,16384]{1,0:T(8,128)(2,1)} %bitcast.15), custom_call_target="tpu_custom_call" | custom-call | tf_op jit(solution)/shard_map/drift_filter/pallas_call | solution.py:81
  7.0 60.9 %all_to_all.25 = bf16[8,192,1536]{2,1,0:T(8,128)(2,1)} all-to-all(bf16[8,192,1536]{2,1,0:T(8,128)(2,1)S(1)} %get-tuple-element.20), channel_id=1, replica_groups=mesh['z'=4,'x'=4,'y'=4,'core'=2] {'y','core'}, dimensions={0} | all-to-all | bytes 9437184 | tf_op jit(solution)/shard_map/all_to_all | solution.py:564
  67.9 4.5 %all-to-all-start = ((bf16[8,192,512]{2,1,0:T(8,128)(2,1)}), bf16[8,192,512]{2,1,0:T(8,128)(2,1)S(1)}, u32[]{:S(2)}, u32[]{:S(2)}) async-start(bf16[8,192,512]{2,1,0:T(8,128)(2,1)} %get-tuple-element.19), calls=%async_computation | async-start | bytes 3145728 | tf_op jit(solution)/shard_map/all_to_all | solution.py:564
  72.4 18.4 %rotate_gram.2 = (f32[64,80,128]{2,1,0:T(8,128)}, f32[64,80,128]{2,1,0:T(8,128)}) custom-call(s32[1]{0:T(128)} %bitcast.core, s32[12,128]{1,0:T(8,128)} %bitcast.16, bf16[1536,1536]{1,0:T(8,128)(2,1)} %bitcast.14, f32[4,128]{1,0:T(4,128)} %bitcast.18), custom_call_target="tpu_custom_call" | custom-call | tf_op jit(solution)/shard_map/rotate_gram/pallas_call | solution.py:197
  90.9 2.3 all-to-all-done
  93.2 6.5 %rotate_gram.3 = (f32[64,80,128]{2,1,0:T(8,128)S(1)}, f32[64,80,128]{2,1,0:T(8,128)S(1)}) custom-call(s32[1]{0:T(128)} %bitcast.core, s32[12,128]{1,0:T(8,128)} %bitcast.17, bf16[1536,512]{1,0:T(8,128)(2,1)S(1)} %bitcast.8, f32[4,128]{1,0:T(4,128)} %bitcast.19, f32[64,80,128]{2,1,0:T(8,128)} %get-tuple-element.21.refs_3_, ...), custom_call_target="tpu_custom_call" | custom-call | tf_op jit(solution)/shard_map/rotate_gram/pallas_call | solution.py:197
  99.7 1.0 collective-permute-start
  100.7 4.5 %collective-permute-done = f32[64,80,128]{2,1,0:T(8,128)S(1)} collective-permute-done((f32[64,80,128]{2,1,0:T(8,128)S(1)}, f32[64,80,128]{2,1,0:T(8,128)S(1)}, u32[]{:S(2)}, u32[]{:S(2)}) %collective-permute-start) | collective-permute-done | bytes 2621472 | tf_op jit(solution)/shard_map/ppermute | solution.py:517
  105.2 0.3 add.3
  105.5 43.6 %all_to_all.26.x_ref = f32[64,80,128]{2,1,0:T(8,128)S(1)} all-to-all(f32[64,80,128]{2,1,0:T(8,128)S(1)} %add.3), channel_id=1, replica_groups=mesh['z'=4,'x'=4,'y'=4,'core'=2] {'z','x','y'}, dimensions={0} | all-to-all | bytes 5242880 | tf_op jit(solution)/shard_map/all_to_all | solution.py:568
  149.1 1.5 sum_and_copy.1
  150.6 19.3 %all_to_all.27 = f32[64,24,128]{2,1,0:T(8,128)S(1)} all-to-all(f32[64,24,128]{2,1,0:T(8,128)S(1)} %get-tuple-element.26), channel_id=1, replica_groups=mesh['z'=4,'x'=4,'y'=4,'core'=2] {'z','x','y'}, dimensions={0} | all-to-all | bytes 1572864 | tf_op jit(solution)/shard_map/all_to_all | solution.py:550
  169.9 3.1 %collective-permute-start.1 = (f32[12,128,128]{2,1,0:T(8,128)S(1)}, f32[12,128,128]{2,1,0:T(8,128)S(1)}, u32[]{:S(2)}, u32[]{:S(2)}) collective-permute-start(f32[12,128,128]{2,1,0:T(8,128)S(1)} %bitcast.11), channel_id=1, source_target_pairs={{0,1},{1,0},{2,3},{3,2},{4,5},{5,4},{6,7},{7,6},{8,9},{9,8},{10,11... | collective-permute-start | bytes 2359304 | tf_op jit(solution)/shard_map/ppermute | solution.py:517
  173.0 4.9 %all-to-all-start.4 = ((f32[64,56,128]{2,1,0:T(8,128)}), f32[64,56,128]{2,1,0:T(8,128)S(1)}, u32[]{:S(2)}, u32[]{:S(2)}) async-start(f32[64,56,128]{2,1,0:T(8,128)} %get-tuple-element.28), calls=%async_computation.4 | async-start | bytes 3670016 | tf_op jit(solution)/shard_map/all_to_all | solution.py:550
  177.8 0.0 collective-permute-done.1.refs_1_
  177.9 22.9 %cholesky.2 = (f32[1536,1536]{1,0:T(8,128)}, f32[6,128,128]{2,1,0:T(8,128)}) custom-call(s32[1]{0:T(128)} %bitcast.core, f32[12,128,128]{2,1,0:T(8,128)S(1)} %bitcast.12, f32[12,128,128]{2,1,0:T(8,128)S(1)} %collective-permute-done.1.refs_1_), custom_call_target="tpu_custom_call" | custom-call | flops 72477573120 | bytes 28311552 | tf_op jit(solution)/shard_map/cholesky/pallas_call | solution.py:486
  200.8 3.4 %all-to-all-done.4 = f32[64,56,128]{2,1,0:T(8,128)S(1)} async-done(((f32[64,56,128]{2,1,0:T(8,128)}), f32[64,56,128]{2,1,0:T(8,128)S(1)}, u32[]{:S(2)}, u32[]{:S(2)}) %all-to-all-start.4) | async-done | bytes 1835040 | tf_op jit(solution)/shard_map/all_to_all | solution.py:550
  204.2 1.3 collective-permute-start.2
  205.5 3.4 %collective-permute-done.2.refs_3_ = f32[28,128,128]{2,1,0:T(8,128)S(1)} collective-permute-done((f32[28,128,128]{2,1,0:T(8,128)S(1)}, f32[28,128,128]{2,1,0:T(8,128)S(1)}, u32[]{:S(2)}, u32[]{:S(2)}) %collective-permute-start.2) | collective-permute-done | bytes 1835040 | tf_op jit(solution)/shard_map/ppermute | solution.py:517
  208.9 34.7 %cholesky.3 = f32[1536,1536]{1,0:T(8,128)} custom-call(s32[1]{0:T(128)} %bitcast.core, f32[12,128,128]{2,1,0:T(8,128)S(1)} %bitcast.13, f32[12,128,128]{2,1,0:T(8,128)S(1)} %collective-permute-done.1.refs_1_, f32[28,128,128]{2,1,0:T(8,128)S(1)} %bitcast.10, f32[28,128,128]{2,1,0:T(8,128)S(1)} %collective-permute-done.2.refs_3_, ...), custom_call_target="tpu_custom_call", output_to_operand_aliasing={{}: (5, {})} | custom-call | flops 72477573120 | bytes 28311552 | tf_op jit(solution)/shard_map/cholesky/pallas_call | solution.py:486
Async XLA Ops:
  67.9 25.3 %all-to-all-start = ((bf16[8,192,512]{2,1,0:T(8,128)(2,1)}), bf16[8,192,512]{2,1,0:T(8,128)(2,1)S(1)}, u32[]{:S(2)}, u32[]{:S(2)}) async-start(bf16[8,192,512]{2,1,0:T(8,128)(2,1)} %get-tuple-element.19), calls=%async_computation | async-start | bytes 3145728 | tf_op jit(solution)/shard_map/all_to_all | solution.py:564
  99.7 5.5 %collective-permute-start = (f32[64,80,128]{2,1,0:T(8,128)S(1)}, f32[64,80,128]{2,1,0:T(8,128)S(1)}, u32[]{:S(2)}, u32[]{:S(2)}) collective-permute-start(f32[64,80,128]{2,1,0:T(8,128)S(1)} %get-tuple-element.24), channel_id=1, source_target_pairs={{0,1},{1,0},{2,3},{3,2},{4,5},{5,4},{6,7},{7,6},{8,9},{9,8},{10,11... | collective-permute-start | bytes 7864328 | tf_op jit(solution)/shard_map/ppermute | solution.py:517
  169.9 7.9 %collective-permute-start.1 = (f32[12,128,128]{2,1,0:T(8,128)S(1)}, f32[12,128,128]{2,1,0:T(8,128)S(1)}, u32[]{:S(2)}, u32[]{:S(2)}) collective-permute-start(f32[12,128,128]{2,1,0:T(8,128)S(1)} %bitcast.11), channel_id=1, source_target_pairs={{0,1},{1,0},{2,3},{3,2},{4,5},{5,4},{6,7},{7,6},{8,9},{9,8},{10,11... | collective-permute-start | bytes 2359304 | tf_op jit(solution)/shard_map/ppermute | solution.py:517
  173.0 31.3 %all-to-all-start.4 = ((f32[64,56,128]{2,1,0:T(8,128)}), f32[64,56,128]{2,1,0:T(8,128)S(1)}, u32[]{:S(2)}, u32[]{:S(2)}) async-start(f32[64,56,128]{2,1,0:T(8,128)} %get-tuple-element.28), calls=%async_computation.4 | async-start | bytes 3670016 | tf_op jit(solution)/shard_map/all_to_all | solution.py:550
  204.2 4.7 %collective-permute-start.2 = (f32[28,128,128]{2,1,0:T(8,128)S(1)}, f32[28,128,128]{2,1,0:T(8,128)S(1)}, u32[]{:S(2)}, u32[]{:S(2)}) collective-permute-start(f32[28,128,128]{2,1,0:T(8,128)S(1)} %bitcast.9), channel_id=1, source_target_pairs={{0,1},{1,0},{2,3},{3,2},{4,5},{5,4},{6,7},{7,6},{8,9},{9,8},{10,11... | collective-permute-start | bytes 5505032 | tf_op jit(solution)/shard_map/ppermute | solution.py:517
